TPU v7x, 32 devices: a whole 2x2x4 slice. The times are simulated.
32 devices in a mesh: dp: 4 (over z), head: 8 (over y, x, core).
Axes of the slice: x: 2, y: 2, z: 4, core: 2. Of those that a mesh axis runs over, the one named last changes fastest.
Arguments:
- hidden_in: bfloat16 [8192, 1024], P(('dp', 'head')), may hold values from -6 to 6
- frame_cond: bfloat16 [32, 1024], P(('dp', 'head')), may hold values from -6 to 6
- query_weight: bfloat16 [1024, 1024], replicated, may hold values from -0.1875 to 0.1875
- key_weight: bfloat16 [1024, 1024], replicated, may hold values from -0.1875 to 0.1875
- value_weight: bfloat16 [1024, 1024], replicated, may hold values from -0.1875 to 0.1875
- output_weight: bfloat16 [1024, 1024], replicated, may hold values from -1.5 to 1.5
- up_weight: bfloat16 [1024, 4096], replicated, may hold values from -0.1875 to 0.1875
- down_weight: bfloat16 [4096, 1024], replicated, may hold values from -0.09375 to 0.09375
- modulation_weight: bfloat16 [1024, 6144], replicated, may hold values from -0.1875 to 0.1875
- clip_lengths: int32 [4, 3], P('dp'), may hold values from 1 to 4, 8 in all within a row
- patch_valid: int32 [8192], P('dp'), may hold values 0 or 1
- cotangent: bfloat16 [8192, 1024], P(('dp', 'head')), may hold values from -6 to 6
Outputs:
- block_out: bfloat16 [8192, 1024], P(('dp', 'head'))
- grad_input: float32 [8192, 1024], P(('dp', 'head'))
- grad_cond: float32 [32, 1024], P(('dp', 'head'))
- grad_query_weight: float32 [1024, 1024], P(('dp', 'head'))
- grad_key_weight: float32 [1024, 1024], P(('dp', 'head'))
- grad_value_weight: float32 [1024, 1024], P(('dp', 'head'))
- grad_output_weight: float32 [1024, 1024], P(('dp', 'head'))
- grad_up_weight: float32 [1024, 4096], P(('dp', 'head'))
- grad_down_weight: float32 [4096, 1024], P(('dp', 'head'))
- grad_modulation_weight: float32 [1024, 6144], P(('dp', 'head'))
- frame_rms: float32 [32, 3], P(('dp', 'head'))
Inputs may be any that keep to these rules, and one draw needn't show every extreme that they name: `clip_lengths`: row g lists in order the frame counts of the 3 clips packed into the 8 frames of data group g; each row sums to 8 and its longest clip has exactly 4 frames.
All inputs are finite; a program needn't handle non-finite values. No bound on the sum of `patch_valid` on one device may be relied on, other than what follows from the above.
Results may differ from a plain program's by a relative error of at most 0.012.
The roundings to bfloat16 on the way count: a program that leaves them out, or rounds other values in their place, can miss the bound.
Values may be sent and summed in bfloat16 or wider, within the bound.
A program may use at most 192 MiB of HBM per device.

v0:
```python
import math

import jax
import jax.numpy as jnp
from jax import lax
from jax.sharding import PartitionSpec as P

HEADS = 16
HEAD_DIM = 64
PATCHES = 256


EPSILON = 1e-06
MASKED = -1e30


def rms_normed(values):
    return values * lax.rsqrt(jnp.mean(values * values, axis=-1, keepdims=True) + EPSILON)


def modulate(values, shift, scaling):
    return rms_normed(values) * (1.0 + scaling) + shift


def frequencies(half_dim):
    return jnp.exp(jnp.arange(half_dim, dtype=jnp.float32) * (-math.log(10000.0) / half_dim))


def rotate(values, angles):
    half_dim = values.shape[-1] // 2
    cosine = jnp.cos(angles)[:, None, :]
    sine_part = jnp.sin(angles)[:, None, :]
    first_half = values[..., :half_dim]
    second = values[..., half_dim:]
    return jnp.concatenate(
        [first_half * cosine - second * sine_part, first_half * sine_part + second * cosine],
        axis=-1,
    )


def group_layout(lengths, token_count, patches):
    frame_of = jnp.arange(token_count, dtype=jnp.int32) // patches
    clip_ends = jnp.cumsum(lengths)
    starts = clip_ends - lengths
    clip_of = jnp.sum((frame_of[:, None] >= clip_ends[None, :]).astype(jnp.int32), axis=1)
    picked = clip_of[:, None] == jnp.arange(lengths.shape[0], dtype=jnp.int32)[None, :]
    position = frame_of - jnp.sum(jnp.where(picked, starts[None, :], 0), axis=1)
    return (clip_of, frame_of, position)


def allowed_block(row_start, row_count, clip_of, frame_of, valid_mask):
    key_count = clip_of.shape[0]
    key_index = jnp.arange(key_count, dtype=jnp.int32)
    row_index = row_start + jnp.arange(row_count, dtype=jnp.int32)
    clip_rows = lax.dynamic_slice_in_dim(clip_of, row_start, row_count)
    frame_rows = lax.dynamic_slice_in_dim(frame_of, row_start, row_count)
    same_clip = clip_rows[:, None] == clip_of[None, :]
    causal = frame_of[None, :] <= frame_rows[:, None]
    usable = (valid_mask[None, :] == 1) | (row_index[:, None] == key_index[None, :])
    return same_clip & causal & usable


def inner_rows(left, right):
    return lax.dot_general(
        left, right, (((0,), (0,)), ((), ())), preferred_element_type=jnp.float32
    )


def times_transposed(left, right):
    return lax.dot_general(
        left, right, (((1,), (1,)), ((), ())), preferred_element_type=jnp.float32
    )


def frame_stats(values, valid_f):
    sums = jnp.sum(values * values, axis=2) * valid_f
    return jnp.sqrt(jnp.sum(sums, axis=1) / (values.shape[1] * values.shape[2]) + EPSILON)


def masked_scores(query_rows, all_keys, row_start, clip_of, frame_of, valid_mask, scaling):
    scores = (
        jnp.einsum("qhd,khd->hqk", query_rows, all_keys, preferred_element_type=jnp.float32)
        * scaling
    )
    permitted = allowed_block(row_start, query_rows.shape[0], clip_of, frame_of, valid_mask)
    return jnp.where(permitted[None], scores, MASKED)


def attend_forward(queries, all_keys, all_values, clip_of, frame_of, valid_mask, scaling):
    token_count = queries.shape[0]
    block_rows = min(512, token_count)

    def one_block(row_start):
        query_rows = lax.dynamic_slice_in_dim(queries, row_start, block_rows, 0)
        scores = masked_scores(
            query_rows, all_keys, row_start, clip_of, frame_of, valid_mask, scaling
        )
        row_max = jnp.max(scores, axis=-1, keepdims=True)
        exponent = jnp.exp(scores - row_max)
        totals = jnp.sum(exponent, axis=-1, keepdims=True)
        prob_low = (exponent / totals).astype(jnp.bfloat16)
        output = jnp.einsum(
            "hqk,khd->qhd", prob_low, all_values, preferred_element_type=jnp.float32
        )
        return (output, (row_max + jnp.log(totals))[..., 0])

    starts = jnp.arange(0, token_count, block_rows, dtype=jnp.int32)
    outputs, logsum = lax.map(one_block, starts)
    return (outputs.reshape(queries.shape), logsum)


def attend_backward(
    queries, all_keys, all_values, grad_out, logsum, clip_of, frame_of, valid_mask, scaling
):
    token_count = queries.shape[0]
    block_rows = logsum.shape[2]
    starts = jnp.arange(0, token_count, block_rows, dtype=jnp.int32)

    def one_block(running, inputs):
        key_grad, value_grad = running
        row_start, block_lse = inputs
        query_rows = lax.dynamic_slice_in_dim(queries, row_start, block_rows, 0)
        grad_rows = lax.dynamic_slice_in_dim(grad_out, row_start, block_rows, 0)
        scores = masked_scores(
            query_rows, all_keys, row_start, clip_of, frame_of, valid_mask, scaling
        )
        soft_probs = jnp.exp(scores - block_lse[..., None])
        prob_low = soft_probs.astype(jnp.bfloat16)
        prob_grad = jnp.einsum(
            "qhd,khd->hqk", grad_rows, all_values, preferred_element_type=jnp.float32
        )
        row_delta = jnp.sum(soft_probs * prob_grad, axis=-1, keepdims=True)
        score_grad = (soft_probs * (prob_grad - row_delta)).astype(jnp.bfloat16)
        query_grad = (
            jnp.einsum("hqk,khd->qhd", score_grad, all_keys, preferred_element_type=jnp.float32)
            * scaling
        )
        key_grad = (
            key_grad
            + jnp.einsum("hqk,qhd->khd", score_grad, query_rows, preferred_element_type=jnp.float32)
            * scaling
        )
        value_grad = value_grad + jnp.einsum(
            "hqk,qhd->khd", prob_low, grad_rows, preferred_element_type=jnp.float32
        )
        return ((key_grad, value_grad), query_grad)

    zero_grads = jnp.zeros(all_keys.shape, jnp.float32)
    (key_grad, value_grad), query_grad = lax.scan(
        one_block, (zero_grads, zero_grads), (starts, logsum)
    )
    return (query_grad.reshape(queries.shape), key_grad, value_grad)


def per_device(
    hidden_in,
    frame_cond,
    query_weight,
    key_weight,
    value_weight,
    output_weight,
    up_weight,
    down_weight,
    modulation_weight,
    clip_lengths,
    patch_valid,
    cotangent,
):
    tok_dev, model_width = hidden_in.shape
    frames_dev = frame_cond.shape[0]
    group_tokens = patch_valid.shape[0]
    head_index = lax.axis_index("head")
    clip_of, frame_of, position = group_layout(clip_lengths[0], group_tokens, PATCHES)
    local_start = head_index * tok_dev
    local_position = lax.dynamic_slice_in_dim(position, local_start, tok_dev)
    local_valid = (
        lax.dynamic_slice_in_dim(patch_valid, local_start, tok_dev)
        .astype(jnp.float32)
        .reshape(frames_dev, PATCHES)
    )
    angles = local_position.astype(jnp.float32)[:, None] * frequencies(HEAD_DIM // 2)[None, :]
    scaling = 1.0 / math.sqrt(HEAD_DIM)
    cond_value = frame_cond.astype(jnp.float32)
    cond_act = jax.nn.silu(cond_value).astype(jnp.bfloat16)
    modulation = jnp.dot(cond_act, modulation_weight, preferred_element_type=jnp.float32).reshape(
        frames_dev, 1, 6 * model_width
    )
    shift_one, scale_one, gate_one, shift_two, scale_two, gate_two = jnp.split(
        modulation, 6, axis=2
    )
    tokens = hidden_in.astype(jnp.float32).reshape(frames_dev, PATCHES, model_width)
    normed_one = (
        modulate(tokens, shift_one, scale_one).astype(jnp.bfloat16).reshape(tok_dev, model_width)
    )
    query_raw = jnp.dot(normed_one, query_weight, preferred_element_type=jnp.float32)
    key_raw = jnp.dot(normed_one, key_weight, preferred_element_type=jnp.float32)
    query_send = (
        rotate(query_raw.reshape(tok_dev, HEADS, HEAD_DIM), angles)
        .reshape(tok_dev, model_width)
        .astype(jnp.bfloat16)
    )
    key_send = (
        rotate(key_raw.reshape(tok_dev, HEADS, HEAD_DIM), angles)
        .reshape(tok_dev, model_width)
        .astype(jnp.bfloat16)
    )
    value_send = jnp.dot(normed_one, value_weight, preferred_element_type=jnp.float32).astype(
        jnp.bfloat16
    )
    head_query, head_key, head_value = (
        lax.all_to_all(query_send, "head", split_axis=1, concat_axis=0, tiled=True),
        lax.all_to_all(key_send, "head", split_axis=1, concat_axis=0, tiled=True),
        lax.all_to_all(value_send, "head", split_axis=1, concat_axis=0, tiled=True),
    )
    local_heads = head_query.shape[1] // HEAD_DIM
    head_shape = (group_tokens, local_heads, HEAD_DIM)
    head_query = head_query.reshape(head_shape)
    head_key = head_key.reshape(head_shape)
    head_value = head_value.reshape(head_shape)
    attended, logsum = attend_forward(
        head_query, head_key, head_value, clip_of, frame_of, patch_valid, scaling
    )
    attended_send = attended.reshape(group_tokens, local_heads * HEAD_DIM).astype(jnp.bfloat16)
    frame_attended = lax.all_to_all(attended_send, "head", split_axis=0, concat_axis=1, tiled=True)
    branch_attn = jnp.dot(
        frame_attended, output_weight, preferred_element_type=jnp.float32
    ).reshape(frames_dev, PATCHES, model_width)
    middle = tokens + gate_one * branch_attn
    normed_two = (
        modulate(middle, shift_two, scale_two).astype(jnp.bfloat16).reshape(tok_dev, model_width)
    )
    hidden = jnp.dot(normed_two, up_weight, preferred_element_type=jnp.float32)
    active = jax.nn.gelu(hidden).astype(jnp.bfloat16)
    branch_mlp = jnp.dot(active, down_weight, preferred_element_type=jnp.float32).reshape(
        frames_dev, PATCHES, model_width
    )
    result = middle + gate_two * branch_mlp
    statistics = jnp.stack(
        [
            frame_stats(gate_one * branch_attn, local_valid),
            frame_stats(gate_two * branch_mlp, local_valid),
            frame_stats(result, local_valid),
        ],
        axis=1,
    )
    out_grad = cotangent.astype(jnp.float32).reshape(frames_dev, PATCHES, model_width)
    gate_two_grad = jnp.sum(out_grad * branch_mlp, axis=1, keepdims=True)
    mlp_grad = (gate_two * out_grad).reshape(tok_dev, model_width).astype(jnp.bfloat16)
    down_term = inner_rows(active, mlp_grad)
    active_grad = times_transposed(mlp_grad, down_weight)
    hidden_grad = jax.vjp(jax.nn.gelu, hidden)[1](active_grad)[0].astype(jnp.bfloat16)
    up_term = inner_rows(normed_two, hidden_grad)
    normed_two_grad = times_transposed(hidden_grad, up_weight).reshape(
        frames_dev, PATCHES, model_width
    )
    middle_part, shift_two_grad, scale_two_grad = jax.vjp(modulate, middle, shift_two, scale_two)[
        1
    ](normed_two_grad)
    middle_grad = out_grad + middle_part
    gate_one_grad = jnp.sum(middle_grad * branch_attn, axis=1, keepdims=True)
    attn_grad = (gate_one * middle_grad).reshape(tok_dev, model_width).astype(jnp.bfloat16)
    output_term = inner_rows(frame_attended, attn_grad)
    attended_grad = times_transposed(attn_grad, output_weight).astype(jnp.bfloat16)
    head_grad = lax.all_to_all(
        attended_grad, "head", split_axis=1, concat_axis=0, tiled=True
    ).reshape(head_shape)
    query_grad, key_grad, value_grad = attend_backward(
        head_query, head_key, head_value, head_grad, logsum, clip_of, frame_of, patch_valid, scaling
    )
    flat_width = local_heads * HEAD_DIM
    back_query, back_key, back_value = (
        lax.all_to_all(
            query_grad.reshape(group_tokens, flat_width).astype(jnp.bfloat16),
            "head",
            split_axis=0,
            concat_axis=1,
            tiled=True,
        ),
        lax.all_to_all(
            key_grad.reshape(group_tokens, flat_width).astype(jnp.bfloat16),
            "head",
            split_axis=0,
            concat_axis=1,
            tiled=True,
        ),
        lax.all_to_all(
            value_grad.reshape(group_tokens, flat_width).astype(jnp.bfloat16),
            "head",
            split_axis=0,
            concat_axis=1,
            tiled=True,
        ),
    )
    query_raw_grad = (
        rotate(back_query.astype(jnp.float32).reshape(tok_dev, HEADS, HEAD_DIM), -angles)
        .reshape(tok_dev, model_width)
        .astype(jnp.bfloat16)
    )
    key_raw_grad = (
        rotate(back_key.astype(jnp.float32).reshape(tok_dev, HEADS, HEAD_DIM), -angles)
        .reshape(tok_dev, model_width)
        .astype(jnp.bfloat16)
    )
    query_term = inner_rows(normed_one, query_raw_grad)
    key_term = inner_rows(normed_one, key_raw_grad)
    value_term = inner_rows(normed_one, back_value)
    normed_one_grad = (
        times_transposed(query_raw_grad, query_weight)
        + times_transposed(key_raw_grad, key_weight)
        + times_transposed(back_value, value_weight)
    )
    token_part, shift_one_grad, scale_one_grad = jax.vjp(modulate, tokens, shift_one, scale_one)[1](
        normed_one_grad.reshape(frames_dev, PATCHES, model_width)
    )
    grad_input = (middle_grad + token_part).reshape(tok_dev, model_width)
    modulation_grad = (
        jnp.concatenate(
            [
                shift_one_grad,
                scale_one_grad,
                gate_one_grad,
                shift_two_grad,
                scale_two_grad,
                gate_two_grad,
            ],
            axis=2,
        )
        .reshape(frames_dev, 6 * model_width)
        .astype(jnp.bfloat16)
    )
    cond_act_grad = times_transposed(modulation_grad, modulation_weight)
    grad_cond = jax.vjp(jax.nn.silu, cond_value)[1](cond_act_grad)[0]
    grad_sums = (
        lax.psum_scatter(query_term, ("dp", "head"), scatter_dimension=0, tiled=True),
        lax.psum_scatter(key_term, ("dp", "head"), scatter_dimension=0, tiled=True),
        lax.psum_scatter(value_term, ("dp", "head"), scatter_dimension=0, tiled=True),
        lax.psum_scatter(output_term, ("dp", "head"), scatter_dimension=0, tiled=True),
        lax.psum_scatter(up_term, ("dp", "head"), scatter_dimension=0, tiled=True),
        lax.psum_scatter(down_term, ("dp", "head"), scatter_dimension=0, tiled=True),
    )
    grad_modulation = lax.psum_scatter(
        inner_rows(cond_act, modulation_grad), ("dp", "head"), scatter_dimension=0, tiled=True
    )
    return (
        result.reshape(tok_dev, model_width).astype(jnp.bfloat16),
        grad_input,
        grad_cond,
        grad_sums[0],
        grad_sums[1],
        grad_sums[2],
        grad_sums[3],
        grad_sums[4],
        grad_sums[5],
        grad_modulation,
        statistics,
    )


def solution(mesh):
    in_specs = (
        P(("dp", "head"), None),
        P(("dp", "head"), None),
        P(),
        P(),
        P(),
        P(),
        P(),
        P(),
        P(),
        P("dp", None),
        P("dp"),
        P(("dp", "head"), None),
    )
    out_specs = (
        P(("dp", "head"), None),
        P(("dp", "head"), None),
        P(("dp", "head"), None),
        P(("dp", "head"), None),
        P(("dp", "head"), None),
        P(("dp", "head"), None),
        P(("dp", "head"), None),
        P(("dp", "head"), None),
        P(("dp", "head"), None),
        P(("dp", "head"), None),
        P(("dp", "head"), None),
    )
    return jax.shard_map(
        per_device, mesh=mesh, in_specs=in_specs, out_specs=out_specs, check_vma=False
    )
```

profile of v0, /device:TPU:0, one launch (start us, length us, event | category | flops | bytes accessed | tf_op | source)
XLA Modules:
  0.0 1406.3 jit_solution(3524475825375531756)
XLA Ops:
  7.2 6.5 convolution_bitcast_fusion
  13.7 4.0 copy.84
  18.2 3.9 copy.82
  22.1 3.6 fusion.59
  28.7 2.6 subtract_convert_fusion.2
  32.1 5.2 all-to-all-start
  39.0 7.9 all-to-all-done
  47.0 4.1 all-to-all-start.1
  54.4 6.4 all-to-all-done.1
  60.8 4.4 all-to-all-start.2
  68.2 6.8 all-to-all-done.2
  79.3 58.7 %while.29 = (s32[]{:T(128)}, bf16[4,512,2,64]{1,3,2,0:T(8,128)(2,1)}, f32[4,2,512]{2,1,0:T(2,128)S(1)}, s32[4]{0:T(128)S(1)}, s32[2048]{0:T(1024)S(1)}, /*index=...) while((s32[]{:T(128)}, ...), condition=%wide.region_7.8_spmd.clone, body=%wide.region_4.7_spmd.clone.sunk | while | flops 568329728 | bytes 35074308 | solution.py:108
  84.9 3.0 fusion.157
  90.5 2.7 fusion.159
  99.6 3.0 fusion.157
  105.2 2.7 fusion.159
  114.3 3.0 fusion.157
  119.9 2.7 fusion.159
  129.0 3.0 fusion.157
  134.6 2.7 fusion.159
  143.4 12.1 all_to_all.110
  157.7 6.2 fusion.89
  163.9 9.5 fusion.46
  173.3 6.5 fusion.101
  179.9 8.2 multiply_reduce_fusion.2
  191.9 3.5 all-to-all-start.4
  195.4 4.0 fusion.70
  199.5 5.5 all-to-all-done.4
  207.3 113.4 %while.30 = (s32[]{:T(128)}, f32[2048,2,64]{0,2,1:T(8,128)S(1)}, f32[2048,2,64]{0,2,1:T(8,128)}, bf16[4,512,2,64]{1,3,2,0:T(8,128)(2,1)}, s32[4]{0:T(128)S(1)}, ...) while((s32[]{:T(128)}, f32[2048,2,64]{0,2,1:T(8,128)S(1)}, ...), condition=%wide.region_12.13_spmd.clone.clone, body=%wide.region_10.12_spmd.clone.clone.sunk | while | flops 1381303808 | bytes 161816976 | solution.py:149
  215.3 4.5 multiply_reduce_fusion.12
  219.7 3.9 multiply_convert_fusion.8
  223.6 3.5 fusion.171
  228.4 4.7 fusion.172
  243.3 4.5 multiply_reduce_fusion.12
  247.8 3.9 multiply_convert_fusion.8
  251.7 3.4 fusion.171
  256.4 5.1 fusion.172
  271.7 4.5 multiply_reduce_fusion.12
  276.2 3.9 multiply_convert_fusion.8
  280.1 3.4 fusion.171
  284.9 5.1 fusion.172
  300.2 4.5 multiply_reduce_fusion.12
  304.7 3.9 multiply_convert_fusion.8
  308.6 3.5 fusion.171
  313.3 5.1 fusion.172
  321.7 3.6 all-to-all-start.6
  326.8 9.6 all-to-all-done.6
  336.4 3.5 all-to-all-start.5
  340.3 9.2 all-to-all-done.5
  350.2 2.8 fusion.94
  353.1 2.8 fusion.92
  356.3 15.2 %all_to_all.111 = bf16[8,256,128]{1,2,0:T(8,128)(2,1)S(1)} all-to-all(bf16[8,256,128]{1,2,0:T(8,128)(2,1)S(1)} %copy.95), channel_id=1, replica_groups=mesh['dp'=4,'head'=8] {'head'}, dimensions={0} | all-to-all | bytes 1048576 | tf_op jit(solution)/shard_map/all_to_all | solution.py:286
  371.5 2.8 fusion.97
  374.4 9.8 fusion.88
  385.3 10.8 fusion.63
  402.6 11.6 broadcast_multiply_fusion
  418.2 3.0 fusion.56
  421.2 8.5 fusion.79
  429.7 65.9 %reduce-scatter.8.cloned.1.call-done = f32[32,1024]{1,0:T(8,128)} async-done(((f32[1024,1024]{1,0:T(8,128)}), f32[32,1024]{1,0:T(8,128)}) %reduce-scatter.8.cloned.1.call-update) | async-done | bytes 131088 | tf_op jit(solution)/shard_map/reduce_scatter | solution.py:334
  495.6 141.5 %reduce-scatter.10.cloned.1.call-done = f32[32,1024]{1,0:T(8,128)} async-done(((f32[1024,1024]{1,0:T(8,128)}), f32[32,1024]{1,0:T(8,128)}) %reduce-scatter.10.cloned.1.call-update) | async-done | bytes 131088 | tf_op jit(solution)/shard_map/reduce_scatter | solution.py:335
  637.1 141.2 %reduce-scatter.12.cloned.1.call-done = f32[32,1024]{1,0:T(8,128)} async-done(((f32[1024,1024]{1,0:T(8,128)}), f32[32,1024]{1,0:T(8,128)}) %reduce-scatter.12.cloned.1.call-update) | async-done | bytes 131088 | tf_op jit(solution)/shard_map/reduce_scatter | solution.py:336
  778.3 181.5 %reduce-scatter.16.cloned.1.call-done = f32[32,4096]{1,0:T(8,128)} async-done(((f32[1024,4096]{1,0:T(8,128)}), f32[32,4096]{1,0:T(8,128)}) %reduce-scatter.16.cloned.1.call-update) | async-done | bytes 524304 | tf_op jit(solution)/shard_map/reduce_scatter | solution.py:338
  959.8 187.4 %reduce-scatter.18.cloned.1.call-done = f32[128,1024]{1,0:T(8,128)} async-done(((f32[4096,1024]{1,0:T(8,128)}), f32[128,1024]{1,0:T(8,128)}) %reduce-scatter.18.cloned.1.call-update) | async-done | bytes 524304 | tf_op jit(solution)/shard_map/reduce_scatter | solution.py:339
  1147.2 251.8 %reduce-scatter.20.cloned.1.call-done = f32[32,6144]{1,0:T(8,128)} async-done(((f32[1024,6144]{1,0:T(8,128)}), f32[32,6144]{1,0:T(8,128)}) %reduce-scatter.20.cloned.1.call-update) | async-done | bytes 786448 | tf_op jit(solution)/shard_map/reduce_scatter | solution.py:341
  (298 shorter events, 109.5 us)
Async XLA Ops:
  7.2 148.3 %copy-start = (bf16[1024,1024]{1,0:T(8,128)(2,1)S(1)}, bf16[1024,1024]{1,0:T(8,128)(2,1)}, u32[]{:S(2)}) copy-start(bf16[1024,1024]{1,0:T(8,128)(2,1)} %param.21) | copy-start | bytes 6291460
  13.7 4.1 copy-start.5
  13.7 4.3 copy-start.49
  13.7 37.4 %copy-start.32 = (f32[1,1,1024]{2,1,0:T(1,128)}, f32[1,1,1024]{2,1,0:T(1,128)S(1)}, u32[]{:S(2)}) copy-start(f32[1,1,1024]{2,1,0:T(1,128)S(1)} %get-tuple-element.349) | copy-start | bytes 12292
  13.7 37.4 %copy-start.34 = (f32[1,1,1024]{2,1,0:T(1,128)}, f32[1,1,1024]{2,1,0:T(1,128)S(1)}, u32[]{:S(2)}) copy-start(f32[1,1,1024]{2,1,0:T(1,128)S(1)} %get-tuple-element.348) | copy-start | bytes 12292
  13.7 143.9 %copy-start.28 = (f32[1,1,1024]{2,1,0:T(1,128)}, f32[1,1,1024]{2,1,0:T(1,128)S(1)}, u32[]{:S(2)}) copy-start(f32[1,1,1024]{2,1,0:T(1,128)S(1)} %get-tuple-element.346) | copy-start | bytes 12292
  17.9 7.7 copy-start.40
  17.9 33.2 %copy-start.37 = (f32[256]{0:T(256)}, f32[256]{0:T(256)S(1)}, u32[]{:S(2)}) copy-start(f32[256]{0:T(256)S(1)} %fusion.85) | copy-start | bytes 3076
  22.1 3.6 copy-start.20
  32.1 14.9 %all-to-all-start = ((bf16[256,8,128]{0,2,1:T(8,128)(2,1)}), bf16[256,8,128]{0,2,1:T(8,128)(2,1)S(1)}, u32[]{:S(2)}, u32[]{:S(2)}) async-start(bf16[256,8,128]{0,2,1:T(8,128)(2,1)} %bitcast.197), calls=%async_computation | async-start | bytes 1048576 | tf_op jit(solution)/shard_map/all_to_all | solution.py:211
  47.0 13.9 all-to-all-start.1
  54.4 24.9 %copy-start.27 = (s32[2048]{0:T(1024)S(1)}, s32[2048]{0:T(1024)}, u32[]{:S(2)}) copy-start(s32[2048]{0:T(1024)} %param.26) | copy-start | bytes 24580
  60.8 14.1 %all-to-all-start.2 = ((bf16[256,8,128]{2,0,1:T(8,128)(2,1)}), bf16[256,8,128]{2,0,1:T(8,128)(2,1)}, u32[]{:S(2)}, u32[]{:S(2)}) async-start(bf16[256,8,128]{2,0,1:T(8,128)(2,1)} %bitcast.149), calls=%async_computation.2 | async-start | bytes 1048576 | tf_op jit(solution)/shard_map/all_to_all | solution.py:213
  157.6 30.5 %copy-start.8 = (f32[256,1024]{1,0:T(8,128)}, f32[256,1024]{1,0:T(8,128)S(1)}, u32[]{:S(2)}) copy-start(f32[256,1024]{1,0:T(8,128)S(1)} %get-tuple-element.327) | copy-start | bytes 3145732
  157.6 6.2 copy-start.16
  163.8 16.0 %copy-start.12 = (f32[256,4096]{1,0:T(8,128)}, f32[256,4096]{1,0:T(8,128)S(1)}, u32[]{:S(2)}) copy-start(f32[256,4096]{1,0:T(8,128)S(1)} %fusion.89) | copy-start | bytes 12582916
  173.3 6.5 copy-start.15
  191.9 13.2 all-to-all-start.4
  195.4 234.4 %reduce-scatter.14.cloned.1.call-start = ((), (), s32[]{:S(2)}) async-start(), calls=%async_computation.18 | async-start | bytes 4325376 | tf_op jit(solution)/shard_map/reduce_scatter | solution.py:337
  212.1 7.6 copy-start.2
  223.6 4.8 copy-start.3
  228.4 4.7 copy-start.4
  228.4 4.7 copy-start.21
  240.2 7.6 copy-start.2
  251.7 4.7 copy-start.3
  256.4 5.1 copy-start.4
  256.4 5.1 copy-start.21
  268.6 7.6 copy-start.2
  280.1 4.8 copy-start.3
  284.9 5.1 copy-start.4
  284.9 5.1 copy-start.21
  297.0 7.6 copy-start.2
  308.5 4.8 copy-start.3
  313.3 5.1 copy-start.4
  313.3 5.1 copy-start.21
  320.7 4.7 copy-start.23
  321.7 27.9 %copy-start.30 = (f32[256,32]{0,1:T(8,128)S(1)}, f32[256,32]{0,1:T(8,128)}, u32[]{:S(2)}) copy-start(f32[256,32]{0,1:T(8,128)} %get-tuple-element.351) | copy-start | bytes 98308
  321.7 28.0 %copy-start.31 = (f32[256,32]{0,1:T(8,128)S(1)}, f32[256,32]{0,1:T(8,128)}, u32[]{:S(2)}) copy-start(f32[256,32]{0,1:T(8,128)} %get-tuple-element.353) | copy-start | bytes 98308
  321.7 14.7 %all-to-all-start.6 = ((bf16[8,256,128]{1,2,0:T(8,128)(2,1)}), bf16[8,256,128]{1,2,0:T(8,128)(2,1)S(1)}, u32[]{:S(2)}, u32[]{:S(2)}) async-start(bf16[8,256,128]{1,2,0:T(8,128)(2,1)} %copy.94), calls=%async_computation.6 | async-start | bytes 1048576 | tf_op jit(solution)/shard_map/all_to_all | solution.py:279
  336.4 13.2 all-to-all-start.5
  339.9 10.2 copy-start.6
  339.9 10.2 copy-start.33
  340.0 10.2 copy-start.35
  340.0 10.2 copy-start.38
  340.0 155.6 %reduce-scatter.8.cloned.1.call-start = ((), (), s32[]{:S(2)}) async-start(), calls=%async_computation.15 | async-start | bytes 4325376 | tf_op jit(solution)/shard_map/reduce_scatter | solution.py:334
  350.1 2.9 copy-start.14
  353.0 284.1 %reduce-scatter.10.cloned.1.call-start = ((), (), s32[]{:S(2)}) async-start(), calls=%async_computation.16 | async-start | bytes 4325376 | tf_op jit(solution)/shard_map/reduce_scatter | solution.py:335
  353.1 2.9 copy-start.26
  355.9 422.4 %reduce-scatter.12.cloned.1.call-start = ((), (), s32[]{:S(2)}) async-start(), calls=%async_computation.17 | async-start | bytes 4325376 | tf_op jit(solution)/shard_map/reduce_scatter | solution.py:336
  371.5 2.8 copy-start.18
  371.5 2.9 copy-start.9
  371.5 2.9 copy-start.29
  374.4 585.5 %reduce-scatter.16.cloned.1.call-start = ((), (), s32[]{:S(2)}) async-start(), calls=%async_computation.19 | async-start | bytes 17301504 | tf_op jit(solution)/shard_map/reduce_scatter | solution.py:338
  384.3 763.0 %reduce-scatter.18.cloned.1.call-start = ((), (), s32[]{:S(2)}) async-start(), calls=%async_computation.20 | async-start | bytes 17301504 | tf_op jit(solution)/shard_map/reduce_scatter | solution.py:339
  396.1 1002.9 %reduce-scatter.20.cloned.1.call-start = ((), (), s32[]{:S(2)}) async-start(), calls=%async_computation.21 | async-start | bytes 25952256 | tf_op jit(solution)/shard_map/reduce_scatter | solution.py:341
  396.8 2.9 copy-start.11
  397.7 2.8 copy-start.19
  397.7 2.8 copy-start.48
  399.6 2.8 copy-start.39
  399.7 2.8 copy-start.44
  399.7 2.8 copy-start.43
  399.7 2.9 copy-start.42
  414.2 4.0 copy-start.41
  418.2 980.8 %copy-start.1 = (bf16[1024,1024]{1,0:T(8,128)(2,1)S(1)}, bf16[1024,1024]{1,0:T(8,128)(2,1)}, u32[]{:S(2)}) copy-start(bf16[1024,1024]{1,0:T(8,128)(2,1)} %param.21) | copy-start | bytes 6291460
  (20 other events, 25.0 us)
Sparse Core Ops, SparseCore 0:
  199.6 144.1 reduce-scatter.13
  353.1 142.4 reduce-scatter.7
  498.5 138.5 reduce-scatter.9
  639.8 138.4 reduce-scatter.11
  781.0 178.7 reduce-scatter.15
  962.6 184.6 reduce-scatter.17
  1154.2 244.7 reduce-scatter.19
where the time goes:
time: 1410 us
  waiting for transfers between devices  1010 us (72%)
  matrix products  183 us (13%)
  other arithmetic  73.8 us (5%)
  local copies, waits for them, and re-layouts  48.9 us (3%)
  blocking collectives  27.4 us (2%)
  starting transfers between devices  25.1 us (2%)
  between operations  17.3 us (1%)
  loops' own time  15.9 us (1%)
    reduce_scatter x1, waiting for transfers between devices, per_device(): lax.psum_scatter(inner_rows(cond_act, modulation_grad), ('dp', 'head'), s...  252 us
    reduce_scatter x1, waiting for transfers between devices, per_device(): lax.psum_scatter(down_term, ('dp', 'head'), scatter_dimension=0, tiled=True)  187 us
    reduce_scatter x1, waiting for transfers between devices, per_device(): lax.psum_scatter(up_term, ('dp', 'head'), scatter_dimension=0, tiled=True)  182 us
    reduce_scatter x1, waiting for transfers between devices, per_device(): lax.psum_scatter(key_term, ('dp', 'head'), scatter_dimension=0, tiled=True)  141 us
    reduce_scatter x1, waiting for transfers between devices, per_device(): lax.psum_scatter(value_term, ('dp', 'head'), scatter_dimension=0, tiled=T...  141 us
    reduce_scatter x1, waiting for transfers between devices, per_device(): lax.psum_scatter(query_term, ('dp', 'head'), scatter_dimension=0, tiled=T...  65.9 us
    dot_general x6, matrix products, inner_rows(): lax.dot_general(left, right, (((0,), (0,)), ((), ())), preferred_element_...  33.1 us
    dot_general x7, matrix products, times_transposed(): lax.dot_general(left, right, (((1,), (1,)), ((), ())), preferred_element_...  29.9 us
  transfers between devices with their start and end apart: 13, of which 12 were waited for; matrix products, arithmetic and copies ran while one was open for 12% of the time, Pallas kernels for 0%

commit v1 on v0

--- a/solution.py
+++ b/solution.py
@@ -3,6 +3,8 @@
 import jax
 import jax.numpy as jnp
 from jax import lax
+from jax.experimental import pallas as pl
+from jax.experimental.pallas import tpu as pltpu
 from jax.sharding import PartitionSpec as P
 
 HEADS = 16
@@ -48,18 +50,6 @@
     return (clip_of, frame_of, position)
 
 
-def allowed_block(row_start, row_count, clip_of, frame_of, valid_mask):
-    key_count = clip_of.shape[0]
-    key_index = jnp.arange(key_count, dtype=jnp.int32)
-    row_index = row_start + jnp.arange(row_count, dtype=jnp.int32)
-    clip_rows = lax.dynamic_slice_in_dim(clip_of, row_start, row_count)
-    frame_rows = lax.dynamic_slice_in_dim(frame_of, row_start, row_count)
-    same_clip = clip_rows[:, None] == clip_of[None, :]
-    causal = frame_of[None, :] <= frame_rows[:, None]
-    usable = (valid_mask[None, :] == 1) | (row_index[:, None] == key_index[None, :])
-    return same_clip & causal & usable
-
-
 def inner_rows(left, right):
     return lax.dot_general(
         left, right, (((0,), (0,)), ((), ())), preferred_element_type=jnp.float32
@@ -77,79 +67,445 @@
     return jnp.sqrt(jnp.sum(sums, axis=1) / (values.shape[1] * values.shape[2]) + EPSILON)
 
 
-def masked_scores(query_rows, all_keys, row_start, clip_of, frame_of, valid_mask, scaling):
-    scores = (
-        jnp.einsum("qhd,khd->hqk", query_rows, all_keys, preferred_element_type=jnp.float32)
-        * scaling
-    )
-    permitted = allowed_block(row_start, query_rows.shape[0], clip_of, frame_of, valid_mask)
-    return jnp.where(permitted[None], scores, MASKED)
-
-
-def attend_forward(queries, all_keys, all_values, clip_of, frame_of, valid_mask, scaling):
-    token_count = queries.shape[0]
-    block_rows = min(512, token_count)
-
-    def one_block(row_start):
-        query_rows = lax.dynamic_slice_in_dim(queries, row_start, block_rows, 0)
-        scores = masked_scores(
-            query_rows, all_keys, row_start, clip_of, frame_of, valid_mask, scaling
+def dot_nt(left, right):
+    return lax.dot_general(
+        left, right, (((1,), (1,)), ((), ())), preferred_element_type=jnp.float32
+    )
+
+
+def dot_nn(left, right):
+    return lax.dot_general(
+        left, right, (((1,), (0,)), ((), ())), preferred_element_type=jnp.float32
+    )
+
+
+def head_parts(block):
+    lane = lax.broadcasted_iota(jnp.int32, block.shape, 1)
+    zero = jnp.zeros_like(block)
+    return jnp.where(lane < HEAD_DIM, block, zero), jnp.where(lane < HEAD_DIM, zero, block)
+
+
+def key_bias(bias_ref, key_frame, frame):
+    half = bias_ref[pl.ds(key_frame * PATCHES, PATCHES), :]
+    bias = jnp.concatenate([half, half], axis=1)
+    row = lax.broadcasted_iota(jnp.int32, bias.shape, 0)
+    column = lax.broadcasted_iota(jnp.int32, bias.shape, 1)
+    own = (row == column) & (key_frame == frame)
+    return jnp.where(own, 0.0, bias)
+
+
+def attend_forward_kernel(first_ref, q_ref, k_ref, v_ref, bias_ref, o_ref, lse_ref, scores):
+    frames = q_ref.shape[0] // PATCHES
+
+    def one_frame(frame, _):
+        rows = pl.ds(frame * PATCHES, PATCHES)
+        parts = head_parts(q_ref[rows, :] * jnp.bfloat16(0.125))
+        first = first_ref[frame]
+
+        def score(key_frame, tops):
+            keys = k_ref[pl.ds(key_frame * PATCHES, PATCHES), :]
+            bias = key_bias(bias_ref, key_frame, frame)
+            new = []
+            for head in range(2):
+                value = dot_nt(keys, parts[head]) + bias
+                scores[head, key_frame - first] = value
+                new.append(jnp.maximum(tops[head], jnp.max(value, axis=0, keepdims=True)))
+            return tuple(new)
+
+        low = jnp.full((1, PATCHES), MASKED, jnp.float32)
+        tops = lax.fori_loop(first, frame + 1, score, (low, low))
+
+        def exponent(key_frame, totals):
+            new = []
+            for head in range(2):
+                value = jnp.exp(scores[head, key_frame - first] - tops[head])
+                scores[head, key_frame - first] = value
+                new.append(totals[head] + jnp.sum(value, axis=0, keepdims=True))
+            return tuple(new)
+
+        zero = jnp.zeros((1, PATCHES), jnp.float32)
+        totals = lax.fori_loop(first, frame + 1, exponent, (zero, zero))
+        inverse = [1.0 / total for total in totals]
+
+        def weigh(key_frame, sums):
+            turned = v_ref[pl.ds(key_frame * PATCHES, PATCHES), :].T
+            new = []
+            for head in range(2):
+                probs = (scores[head, key_frame - first] * inverse[head]).astype(jnp.bfloat16)
+                new.append(
+                    sums[head]
+                    + dot_nn(turned[head * HEAD_DIM : (head + 1) * HEAD_DIM, :], probs)
+                )
+            return tuple(new)
+
+        empty = jnp.zeros((HEAD_DIM, PATCHES), jnp.float32)
+        sums = lax.fori_loop(first, frame + 1, weigh, (empty, empty))
+        o_ref[rows, :] = jnp.concatenate(sums, axis=0).T.astype(jnp.bfloat16)
+        for head in range(2):
+            lse_ref[frame, head : head + 1, :] = tops[head] + jnp.log(totals[head])
+        return 0
+
+    lax.fori_loop(0, frames, one_frame, 0)
+
+
+def attend_backward_kernel(
+    first_ref,
+    q_ref,
+    k_ref,
+    v_ref,
+    o_ref,
+    do_ref,
+    bias_ref,
+    lse_ref,
+    dq_ref,
+    dk_ref,
+    dv_ref,
+    dk_sum,
+    dv_sum,
+):
+    frames = q_ref.shape[0] // PATCHES
+    dk_sum[...] = jnp.zeros_like(dk_sum)
+    dv_sum[...] = jnp.zeros_like(dv_sum)
+
+    def one_frame(frame, _):
+        rows = pl.ds(frame * PATCHES, PATCHES)
+        q_parts = head_parts(q_ref[rows, :] * jnp.bfloat16(0.125))
+        grads = do_ref[rows, :]
+        do_parts = head_parts(grads)
+        product = (grads.astype(jnp.float32) * o_ref[rows, :].astype(jnp.float32)).T
+        deltas = [
+            jnp.sum(product[h * HEAD_DIM : (h + 1) * HEAD_DIM, :], axis=0, keepdims=True)
+            for h in range(2)
+        ]
+        lses = [lse_ref[frame, h : h + 1, :] for h in range(2)]
+        first = first_ref[frame]
+
+        def one_block(key_frame, sums):
+            where = pl.ds(key_frame * PATCHES, PATCHES)
+            keys = k_ref[where, :]
+            values = v_ref[where, :]
+            turned = keys.T
+            bias = key_bias(bias_ref, key_frame, frame)
+            dv = dv_sum[where, :]
+            dk = dk_sum[where, :]
+            new = []
+            for head in range(2):
+                probs = jnp.exp(dot_nt(keys, q_parts[head]) + bias - lses[head])
+                prob_grad = dot_nt(values, do_parts[head])
+                score_grad = (probs * (prob_grad - deltas[head])).astype(jnp.bfloat16)
+                dv = dv + dot_nn(probs.astype(jnp.bfloat16), do_parts[head])
+                dk = dk + dot_nn(score_grad, q_parts[head])
+                new.append(
+                    sums[head]
+                    + dot_nn(turned[head * HEAD_DIM : (head + 1) * HEAD_DIM, :], score_grad)
+                )
+            dv_sum[where, :] = dv
+            dk_sum[where, :] = dk
+            return tuple(new)
+
+        empty = jnp.zeros((HEAD_DIM, PATCHES), jnp.float32)
+        sums = lax.fori_loop(first, frame + 1, one_block, (empty, empty))
+        dq_ref[rows, :] = (jnp.concatenate(sums, axis=0).T * 0.125).astype(jnp.bfloat16)
+        return 0
+
+    lax.fori_loop(0, frames, one_frame, 0)
+    dk_ref[...] = dk_sum[...].astype(jnp.bfloat16)
+    dv_ref[...] = dv_sum[...].astype(jnp.bfloat16)
+
+
+IN_SMEM = pl.BlockSpec(memory_space=pltpu.SMEM)
+IN_VMEM = pl.BlockSpec(memory_space=pltpu.VMEM)
+IN_PLACE = pl.BlockSpec(memory_space=pl.ANY)
+MESH_ID = pl.DeviceIdType.MESH
+
+
+def attend_forward(first, queries, keys, values, bias):
+    tokens, width = queries.shape
+    frames = tokens // PATCHES
+    return pl.pallas_call(
+        attend_forward_kernel,
+        out_shape=(
+            jax.ShapeDtypeStruct((tokens, width), jnp.bfloat16),
+            jax.ShapeDtypeStruct((frames, 2, PATCHES), jnp.float32),
+        ),
+        in_specs=[IN_SMEM] + [IN_VMEM] * 4,
+        out_specs=(IN_VMEM, IN_VMEM),
+        scratch_shapes=[pltpu.VMEM((2, 4, PATCHES, PATCHES), jnp.float32)],
+        name="attend_forward",
+    )(first, queries, keys, values, bias)
+
+
+def attend_backward(first, queries, keys, values, attended, grads, bias, lse):
+    tokens, width = queries.shape
+    shape = jax.ShapeDtypeStruct((tokens, width), jnp.bfloat16)
+    return pl.pallas_call(
+        attend_backward_kernel,
+        out_shape=(shape, shape, shape),
+        in_specs=[IN_SMEM] + [IN_VMEM] * 7,
+        out_specs=(IN_VMEM, IN_VMEM, IN_VMEM),
+        scratch_shapes=[pltpu.VMEM((tokens, width), jnp.float32)] * 2,
+        name="attend_backward",
+    )(first, queries, keys, values, attended, grads, bias, lse)
+
+
+def position_bits():
+    head = lax.axis_index("head")
+    core = lax.rem(head, 2)
+    second = lax.rem(lax.div(head, 2), 2)
+    third = lax.div(head, 4)
+    return head, core, second, third
+
+
+def scatter_kernel(n_dp, units, *refs):
+    n_in = 6
+    terms = refs[:n_in]
+    row_ref = refs[n_in]
+    outs = refs[n_in + 1 : 2 * n_in + 1]
+    rows_ref = refs[2 * n_in + 1]
+    (
+        own,
+        from_core,
+        from_first,
+        from_second,
+        from_dp,
+        load_sem,
+        core_send,
+        core_recv,
+        first_send,
+        first_recv,
+        second_send,
+        second_recv,
+        dp_send,
+        dp_recv,
+        row_load,
+        row_send,
+        row_recv,
+        row_dp_send,
+        row_dp_recv,
+    ) = refs[2 * n_in + 2 :]
+    group = lax.axis_index("dp")
+    head, core, xbit, ybit = position_bits()
+    core_peer = head + 1 - 2 * core
+    x_peer = head + 2 - 4 * xbit
+    y_peer = head + 4 - 8 * ybit
+    dp_peers = [lax.rem(group + hop, n_dp) for hop in range(1, n_dp)]
+
+    barrier = pltpu.get_barrier_semaphore()
+    for peer in (core_peer, x_peer, y_peer):
+        pl.semaphore_signal(barrier, inc=1, device_id=(group, peer), device_id_type=MESH_ID)
+    for peer in dp_peers:
+        pl.semaphore_signal(barrier, inc=1, device_id=(peer, head), device_id_type=MESH_ID)
+    pl.semaphore_wait(barrier, 3 + len(dp_peers))
+
+    def term_part(unit, side):
+        which, row, column = units[unit][:3]
+        rows, columns = own.shape[4], own.shape[5]
+        return terms[which].at[:, :, :, side, pl.ds(row, rows), pl.ds(column, columns)]
+
+    def remote(source, target, send, receive, where):
+        return pltpu.make_async_remote_copy(
+            src_ref=source,
+            dst_ref=target,
+            send_sem=send,
+            recv_sem=receive,
+            device_id=where,
+            device_id_type=MESH_ID,
         )
-        row_max = jnp.max(scores, axis=-1, keepdims=True)
-        exponent = jnp.exp(scores - row_max)
-        totals = jnp.sum(exponent, axis=-1, keepdims=True)
-        prob_low = (exponent / totals).astype(jnp.bfloat16)
-        output = jnp.einsum(
-            "hqk,khd->qhd", prob_low, all_values, preferred_element_type=jnp.float32
+
+    def load(unit):
+        return pltpu.make_async_copy(term_part(unit, core), own.at[unit], load_sem.at[unit])
+
+    def core_copy(unit):
+        return remote(
+            term_part(unit, 1 - core),
+            from_core.at[unit],
+            core_send.at[unit],
+            core_recv.at[unit],
+            (group, core_peer),
         )
-        return (output, (row_max + jnp.log(totals))[..., 0])
-
-    starts = jnp.arange(0, token_count, block_rows, dtype=jnp.int32)
-    outputs, logsum = lax.map(one_block, starts)
-    return (outputs.reshape(queries.shape), logsum)
-
-
-def attend_backward(
-    queries, all_keys, all_values, grad_out, logsum, clip_of, frame_of, valid_mask, scaling
-):
-    token_count = queries.shape[0]
-    block_rows = logsum.shape[2]
-    starts = jnp.arange(0, token_count, block_rows, dtype=jnp.int32)
-
-    def one_block(running, inputs):
-        key_grad, value_grad = running
-        row_start, block_lse = inputs
-        query_rows = lax.dynamic_slice_in_dim(queries, row_start, block_rows, 0)
-        grad_rows = lax.dynamic_slice_in_dim(grad_out, row_start, block_rows, 0)
-        scores = masked_scores(
-            query_rows, all_keys, row_start, clip_of, frame_of, valid_mask, scaling
+
+    def x_leads(unit):
+        return units[unit][3] == 0
+
+    def first_copy(unit):
+        if x_leads(unit):
+            source, peer = own.at[unit, :, :, 1 - xbit], x_peer
+        else:
+            source, peer = own.at[unit, :, 1 - ybit], y_peer
+        return remote(
+            source, from_first.at[unit], first_send.at[unit], first_recv.at[unit], (group, peer)
         )
-        soft_probs = jnp.exp(scores - block_lse[..., None])
-        prob_low = soft_probs.astype(jnp.bfloat16)
-        prob_grad = jnp.einsum(
-            "qhd,khd->hqk", grad_rows, all_values, preferred_element_type=jnp.float32
+
+    def second_copy(unit):
+        if x_leads(unit):
+            source, peer = own.at[unit, :, 1 - ybit, xbit], y_peer
+        else:
+            source, peer = own.at[unit, :, ybit, 1 - xbit], x_peer
+        return remote(
+            source, from_second.at[unit], second_send.at[unit], second_recv.at[unit], (group, peer)
         )
-        row_delta = jnp.sum(soft_probs * prob_grad, axis=-1, keepdims=True)
-        score_grad = (soft_probs * (prob_grad - row_delta)).astype(jnp.bfloat16)
-        query_grad = (
-            jnp.einsum("hqk,khd->qhd", score_grad, all_keys, preferred_element_type=jnp.float32)
-            * scaling
+
+    def dp_copy(unit, hop):
+        peer = dp_peers[hop]
+        return remote(
+            own.at[unit, peer, ybit, xbit],
+            from_dp.at[unit, hop],
+            dp_send.at[unit, hop],
+            dp_recv.at[unit, hop],
+            (peer, head),
         )
-        key_grad = (
-            key_grad
-            + jnp.einsum("hqk,qhd->khd", score_grad, query_rows, preferred_element_type=jnp.float32)
-            * scaling
-        )
-        value_grad = value_grad + jnp.einsum(
-            "hqk,qhd->khd", prob_low, grad_rows, preferred_element_type=jnp.float32
-        )
-        return ((key_grad, value_grad), query_grad)
-
-    zero_grads = jnp.zeros(all_keys.shape, jnp.float32)
-    (key_grad, value_grad), query_grad = lax.scan(
-        one_block, (zero_grads, zero_grads), (starts, logsum)
-    )
-    return (query_grad.reshape(queries.shape), key_grad, value_grad)
+
+    def added(left, right):
+        return (left.astype(jnp.float32) + right.astype(jnp.float32)).astype(jnp.bfloat16)
+
+    def take_core(unit):
+        load(unit).wait()
+        core_copy(unit).wait()
+
+        def body(index, _):
+            at_dp = lax.div(index, 4)
+            at_y = lax.rem(lax.div(index, 2), 2)
+            at_x = lax.rem(index, 2)
+            own[unit, at_dp, at_y, at_x] = added(
+                own[unit, at_dp, at_y, at_x], from_core[unit, at_dp, at_y, at_x]
+            )
+            return 0
+
+        lax.fori_loop(0, n_dp * 4, body, 0)
+        first_copy(unit).start()
+
+    def take_first(unit):
+        first_copy(unit).wait()
+
+        def body(index, _):
+            at_dp = lax.div(index, 2)
+            other = lax.rem(index, 2)
+            at_y, at_x = (other, xbit) if x_leads(unit) else (ybit, other)
+            own[unit, at_dp, at_y, at_x] = added(
+                own[unit, at_dp, at_y, at_x], from_first[unit, at_dp, other]
+            )
+            return 0
+
+        lax.fori_loop(0, n_dp * 2, body, 0)
+        second_copy(unit).start()
+
+    def take_second(unit):
+        second_copy(unit).wait()
+
+        def body(at_dp, _):
+            own[unit, at_dp, ybit, xbit] = added(
+                own[unit, at_dp, ybit, xbit], from_second[unit, at_dp]
+            )
+            return 0
+
+        lax.fori_loop(0, n_dp, body, 0)
+        for hop in range(n_dp - 1):
+            dp_copy(unit, hop).start()
+
+    def take_dp(unit):
+        which, row, column = units[unit][:3]
+        rows, columns = own.shape[4], own.shape[5]
+        for hop in range(n_dp - 1):
+            dp_copy(unit, hop).wait()
+        total = own[unit, group, ybit, xbit].astype(jnp.float32)
+        for hop in range(n_dp - 1):
+            total = total + from_dp[unit, hop].astype(jnp.float32)
+        outs[which][row : row + rows, column : column + columns] = total
+
+    mine = rows_ref.at[group, ybit, xbit, core]
+    row_copy = pltpu.make_async_copy(row_ref, mine, row_load)
+    row_copy.start()
+    row_copy.wait()
+    row_dp = [
+        remote(mine, mine, row_dp_send.at[hop], row_dp_recv.at[hop], (dp_peers[hop], head))
+        for hop in range(n_dp - 1)
+    ]
+    for copy in row_dp:
+        copy.start()
+    y_part = rows_ref.at[:, ybit, xbit, core]
+    x_part = rows_ref.at[:, :, xbit, core]
+    core_part = rows_ref.at[:, :, :, core]
+    row_y = remote(y_part, y_part, row_send.at[0], row_recv.at[0], (group, y_peer))
+    row_x = remote(x_part, x_part, row_send.at[1], row_recv.at[1], (group, x_peer))
+    row_core = remote(core_part, core_part, row_send.at[2], row_recv.at[2], (group, core_peer))
+
+    count = len(units)
+    for unit in range(count):
+        core_copy(unit).start()
+        load(unit).start()
+    for step in range(count + 3):
+        if step < count:
+            take_core(step)
+        if 0 <= step - 1 < count:
+            take_first(step - 1)
+        if 0 <= step - 2 < count:
+            take_second(step - 2)
+        if 0 <= step - 3:
+            take_dp(step - 3)
+        if step == 1:
+            for copy in row_dp:
+                copy.wait()
+            row_y.start()
+        if step == 3:
+            row_y.wait()
+            row_x.start()
+        if step == 5:
+            row_x.wait()
+            row_core.start()
+        if step == 7:
+            row_core.wait()
+
+
+def scatter_sums(n_dp, terms, factors):
+    devices = n_dp * 8
+    rows = min(term.shape[0] for term in terms) // devices
+    columns = min(term.shape[1] for term in terms)
+    units = []
+    for which, term in enumerate(terms):
+        for row in range(0, term.shape[0] // devices, rows):
+            for column in range(0, term.shape[1], columns):
+                units.append((which, row, column, len(units) % 2))
+    count = len(units)
+    views = [
+        term.reshape(n_dp, 2, 2, 2, term.shape[0] // devices, term.shape[1]) for term in terms
+    ]
+    out_shapes = [
+        jax.ShapeDtypeStruct((term.shape[0] // devices, term.shape[1]), jnp.float32)
+        for term in terms
+    ]
+    dma = pltpu.SemaphoreType.DMA
+    results = pl.pallas_call(
+        lambda *refs: scatter_kernel(n_dp, units, *refs),
+        out_shape=(*out_shapes, jax.ShapeDtypeStruct((n_dp, 2, 2, 2, *factors.shape), factors.dtype)),
+        in_specs=[IN_PLACE] * (len(terms) + 1),
+        out_specs=tuple([IN_VMEM] * (len(terms) + 1)),
+        scratch_shapes=[
+            pltpu.VMEM((count, n_dp, 2, 2, rows, columns), jnp.bfloat16),
+            pltpu.VMEM((count, n_dp, 2, 2, rows, columns), jnp.bfloat16),
+            pltpu.VMEM((count, n_dp, 2, rows, columns), jnp.bfloat16),
+            pltpu.VMEM((count, n_dp, rows, columns), jnp.bfloat16),
+            pltpu.VMEM((count, n_dp - 1, rows, columns), jnp.bfloat16),
+            dma((count,)),
+            dma((count,)),
+            dma((count,)),
+            dma((count,)),
+            dma((count,)),
+            dma((count,)),
+            dma((count,)),
+            dma((count, n_dp - 1)),
+            dma((count, n_dp - 1)),
+            dma,
+            dma((3,)),
+            dma((3,)),
+            dma((n_dp - 1,)),
+            dma((n_dp - 1,)),
+        ],
+        compiler_params=pltpu.CompilerParams(
+            collective_id=0, has_side_effects=True, vmem_limit_bytes=60 * 1024 * 1024
+        ),
+        name="scatter_sums",
+    )(*views, factors)
+    return results[:-1], results[-1]
 
 
 def per_device(
@@ -179,7 +535,6 @@
         .reshape(frames_dev, PATCHES)
     )
     angles = local_position.astype(jnp.float32)[:, None] * frequencies(HEAD_DIM // 2)[None, :]
-    scaling = 1.0 / math.sqrt(HEAD_DIM)
     cond_value = frame_cond.astype(jnp.float32)
     cond_act = jax.nn.silu(cond_value).astype(jnp.bfloat16)
     modulation = jnp.dot(cond_act, modulation_weight, preferred_element_type=jnp.float32).reshape(
@@ -212,15 +567,12 @@
         lax.all_to_all(key_send, "head", split_axis=1, concat_axis=0, tiled=True),
         lax.all_to_all(value_send, "head", split_axis=1, concat_axis=0, tiled=True),
     )
-    local_heads = head_query.shape[1] // HEAD_DIM
-    head_shape = (group_tokens, local_heads, HEAD_DIM)
-    head_query = head_query.reshape(head_shape)
-    head_key = head_key.reshape(head_shape)
-    head_value = head_value.reshape(head_shape)
-    attended, logsum = attend_forward(
-        head_query, head_key, head_value, clip_of, frame_of, patch_valid, scaling
-    )
-    attended_send = attended.reshape(group_tokens, local_heads * HEAD_DIM).astype(jnp.bfloat16)
+    first_frames = (frame_of - position)[::PATCHES]
+    bias = jnp.broadcast_to(
+        jnp.where(patch_valid == 1, 0.0, MASKED).astype(jnp.float32)[:, None],
+        (group_tokens, 128),
+    )
+    attended_send, logsum = attend_forward(first_frames, head_query, head_key, head_value, bias)
     frame_attended = lax.all_to_all(attended_send, "head", split_axis=0, concat_axis=1, tiled=True)
     branch_attn = jnp.dot(
         frame_attended, output_weight, preferred_element_type=jnp.float32
@@ -261,30 +613,27 @@
     attn_grad = (gate_one * middle_grad).reshape(tok_dev, model_width).astype(jnp.bfloat16)
     output_term = inner_rows(frame_attended, attn_grad)
     attended_grad = times_transposed(attn_grad, output_weight).astype(jnp.bfloat16)
-    head_grad = lax.all_to_all(
-        attended_grad, "head", split_axis=1, concat_axis=0, tiled=True
-    ).reshape(head_shape)
+    head_grad = lax.all_to_all(attended_grad, "head", split_axis=1, concat_axis=0, tiled=True)
     query_grad, key_grad, value_grad = attend_backward(
-        head_query, head_key, head_value, head_grad, logsum, clip_of, frame_of, patch_valid, scaling
-    )
-    flat_width = local_heads * HEAD_DIM
+        first_frames, head_query, head_key, head_value, attended_send, head_grad, bias, logsum
+    )
     back_query, back_key, back_value = (
         lax.all_to_all(
-            query_grad.reshape(group_tokens, flat_width).astype(jnp.bfloat16),
+            query_grad,
             "head",
             split_axis=0,
             concat_axis=1,
             tiled=True,
         ),
         lax.all_to_all(
-            key_grad.reshape(group_tokens, flat_width).astype(jnp.bfloat16),
+            key_grad,
             "head",
             split_axis=0,
             concat_axis=1,
             tiled=True,
         ),
         lax.all_to_all(
-            value_grad.reshape(group_tokens, flat_width).astype(jnp.bfloat16),
+            value_grad,
             "head",
             split_axis=0,
             concat_axis=1,
@@ -330,16 +679,17 @@
     )
     cond_act_grad = times_transposed(modulation_grad, modulation_weight)
     grad_cond = jax.vjp(jax.nn.silu, cond_value)[1](cond_act_grad)[0]
-    grad_sums = (
-        lax.psum_scatter(query_term, ("dp", "head"), scatter_dimension=0, tiled=True),
-        lax.psum_scatter(key_term, ("dp", "head"), scatter_dimension=0, tiled=True),
-        lax.psum_scatter(value_term, ("dp", "head"), scatter_dimension=0, tiled=True),
-        lax.psum_scatter(output_term, ("dp", "head"), scatter_dimension=0, tiled=True),
-        lax.psum_scatter(up_term, ("dp", "head"), scatter_dimension=0, tiled=True),
-        lax.psum_scatter(down_term, ("dp", "head"), scatter_dimension=0, tiled=True),
-    )
-    grad_modulation = lax.psum_scatter(
-        inner_rows(cond_act, modulation_grad), ("dp", "head"), scatter_dimension=0, tiled=True
+    n_dp = lax.axis_size("dp")
+    factors = jnp.concatenate([cond_act, modulation_grad], axis=1).reshape(-1, 128)
+    terms = [query_term, key_term, value_term, output_term, up_term, down_term]
+    grad_sums, gathered = scatter_sums(
+        n_dp, [term.astype(jnp.bfloat16) for term in terms], factors
+    )
+    device = lax.axis_index("dp") * lax.axis_size("head") + head_index
+    gathered = gathered.reshape(n_dp * 8 * frames_dev, 7 * model_width)
+    share = model_width // (n_dp * 8)
+    grad_modulation = inner_rows(
+        lax.dynamic_slice_in_dim(gathered, device * share, share, 1), gathered[:, model_width:]
     )
     return (
         result.reshape(tok_dev, model_width).astype(jnp.bfloat16),

time: 1410 us -> 364 us (0.26)
  waiting for transfers between devices: 1010 us -> 30.9 us
  Pallas kernels: 0 us -> 157 us
  matrix products: 183 us -> 86.8 us
  other arithmetic: 73.8 us -> 14.1 us
  blocking collectives: 27.4 us -> 0 us
  local copies, waits for them, and re-layouts: 48.9 us -> 30.9 us
  loops' own time: 15.9 us -> 0 us
    reduce_scatter x7 -> x0, waiting for transfers between devices: 969 us -> none  [the longest x1 252 us: per_device(): lax.psum_scatter(inner_rows(cond_act, modulation_grad), ('dp', 'head'), s...]
    pallas_call x0 -> x3, Pallas kernels: none -> 157 us  [the longest x1 129 us: scatter_sums(): pl.pallas_call(lambda *refs: scatter_kernel(n_dp, units, *refs), out_shap...]
    dot_general x28 -> x0, matrix products: 89.4 us -> none  [the longest x8 21.4 us: masked_scores(): jnp.einsum('qhd,khd->hqk', query_rows, all_keys, preferred_element_type=j...]
    all_to_all x2 -> x0, blocking collectives: 27.4 us -> none  [the longest x1 15.2 us: per_device(): lax.all_to_all(value_grad.reshape(group_tokens, flat_width).astype(jnp.bf...]
    and x8 -> x0, other arithmetic: 18.3 us -> none  [allowed_block(): return same_clip & causal & usable]
    another operation x2 -> x0, loops' own time: 15.9 us -> none  [the longest x1 7.97 us: attend_forward(): outputs, logsum = lax.map(one_block, starts)]
    convert_element_type x6 -> x0, other arithmetic: 15.7 us -> none  [the longest x4 15.6 us: one_block(): score_grad = (soft_probs * (prob_grad - row_delta)).astype(jnp.bfloat16)]
    dot_general x6 -> x7, matrix products: 33.1 us -> 26.8 us  [inner_rows(): lax.dot_general(left, right, (((0,), (0,)), ((), ())), preferred_element_...]
  transfers between devices with their start and end apart: 13 -> 8, of which waited for: 12 -> 6; matrix products, arithmetic and copies ran while one was open for 12% -> 16% of each run, Pallas kernels for 0% -> 0%
where the time goes in v1:
time: 364 us; the launch traced here: 356 us
  Pallas kernels  157 us (43%)
  matrix products  86.8 us (24%)
  starting transfers between devices  33 us (9%)
  local copies, waits for them, and re-layouts  30.9 us (8%)
  waiting for transfers between devices  30.9 us (8%)
  other arithmetic  14.1 us (4%)
  between operations  3.64 us (1%)
    pallas_call x1, Pallas kernels, scatter_sums(): pl.pallas_call(lambda *refs: scatter_kernel(n_dp, units, *refs), out_shap...  129 us
    dot_general x7, matrix products, times_transposed(): lax.dot_general(left, right, (((1,), (1,)), ((), ())), preferred_element_...  29.4 us
    dot_general x7, matrix products, inner_rows(): lax.dot_general(left, right, (((0,), (0,)), ((), ())), preferred_element_...  26.8 us
    unnamed x70, local copies, waits for them, and re-layouts  15.9 us
    pallas_call x1, Pallas kernels, attend_backward(): pl.pallas_call(attend_backward_kernel, out_shape=(shape, shape, shape), i...  15.9 us
    pallas_call x1, Pallas kernels, attend_forward(): pl.pallas_call(attend_forward_kernel, out_shape=(jax.ShapeDtypeStruct((to...  12.6 us
    all_to_all x1, waiting for transfers between devices, per_device(): lax.all_to_all(attended_send, 'head', split_axis=0, concat_axis=1, tiled=...  9.6 us
    all_to_all x1, waiting for transfers between devices, per_device(): lax.all_to_all(query_send, 'head', split_axis=1, concat_axis=0, tiled=True)  9.12 us
  transfers between devices with their start and end apart: 8, of which 6 were waited for; matrix products, arithmetic and copies ran while one was open for 16% of the time, Pallas kernels for 0%

profile of v1, /device:TPU:0, one launch (start us, length us, event | category | flops | bytes accessed | tf_op | source)
XLA Modules:
  0.0 356.4 jit_solution(15496733671978786737)
XLA Ops:
  0.7 1.4 fusion.17
  2.1 6.5 %convolution_bitcast_fusion = f32[1,1,6144]{2,1,0:T(1,128)S(1)} fusion(bf16[1024,6144]{1,0:T(8,128)(2,1)} %param.20, bf16[1,1024]{1,0:T(2,128)(2,1)} %param.13), kind=kOutput, calls=%fused_computation.2 | convolution fusion | flops 12589056 | bytes 12609536 | tf_op jit(solution)/shard_map/dot_general | solution.py:540
  8.6 0.8 fusion.9
  9.4 0.9 copy.58
  10.2 5.2 %all-to-all-start.2 = ((bf16[256,8,128]{2,0,1:T(8,128)(2,1)}), bf16[256,8,128]{2,0,1:T(8,128)(2,1)S(1)}, u32[]{:S(2)}, u32[]{:S(2)}) async-start(bf16[256,8,128]{2,0,1:T(8,128)(2,1)} %bitcast.146), calls=%async_computation.2 | async-start | bytes 1048576 | tf_op jit(solution)/shard_map/all_to_all | solution.py:568
  15.7 4.0 %copy.41 = bf16[1024,1024]{0,1:T(8,128)(2,1)} copy(bf16[1024,1024]{1,0:T(8,128)(2,1)} %param.14) | data formatting | bytes 4194304 | tf_op args[2]
  19.6 3.4 fusion.21
  23.0 4.0 %copy.43 = bf16[1024,1024]{0,1:T(8,128)(2,1)} copy(bf16[1024,1024]{1,0:T(8,128)(2,1)} %param.15) | data formatting | bytes 4194304 | tf_op args[3]
  27.0 3.4 fusion.19
  31.0 1.9 subtract_convert_fusion.2
  32.9 1.1 pad_maximum_fusion
  33.9 2.0 copy.44
  36.0 4.2 %all-to-all-start.1 = ((bf16[256,8,128]{2,0,1:T(8,128)(2,1)}), bf16[256,8,128]{2,0,1:T(8,128)(2,1)}, u32[]{:S(2)}, u32[]{:S(2)}) async-start(bf16[256,8,128]{2,0,1:T(8,128)(2,1)} %copy.44), calls=%async_computation.1 | async-start | bytes 1048576 | tf_op jit(solution)/shard_map/all_to_all | solution.py:567
  40.2 2.0 copy.42
  42.2 7.8 %all-to-all-done.1 = bf16[256,8,128]{2,0,1:T(8,128)(2,1)} async-done(((bf16[256,8,128]{2,0,1:T(8,128)(2,1)}), bf16[256,8,128]{2,0,1:T(8,128)(2,1)}, u32[]{:S(2)}, u32[]{:S(2)}) %all-to-all-start.1) | async-done | bytes 524320 | tf_op jit(solution)/shard_map/all_to_all | solution.py:567
  50.0 4.2 %all-to-all-start = ((bf16[256,8,128]{2,0,1:T(8,128)(2,1)}), bf16[256,8,128]{2,0,1:T(8,128)(2,1)}, u32[]{:S(2)}, u32[]{:S(2)}) async-start(bf16[256,8,128]{2,0,1:T(8,128)(2,1)} %copy.42), calls=%async_computation | async-start | bytes 1048576 | tf_op jit(solution)/shard_map/all_to_all | solution.py:566
  54.8 9.1 %all-to-all-done = bf16[256,8,128]{2,0,1:T(8,128)(2,1)} async-done(((bf16[256,8,128]{2,0,1:T(8,128)(2,1)}), bf16[256,8,128]{2,0,1:T(8,128)(2,1)}, u32[]{:S(2)}, u32[]{:S(2)}) %all-to-all-start) | async-done | bytes 524320 | tf_op jit(solution)/shard_map/all_to_all | solution.py:566
  63.9 1.3 broadcast_in_dim.37.bias_ref
  65.2 12.6 %attend_forward.1 = (bf16[2048,128]{1,0:T(8,128)(2,1)}, f32[8,2,256]{2,1,0:T(2,128)}) custom-call(s32[8]{0:T(128)} %slice.30.first_ref, bf16[2048,128]{1,0:T(8,128)(2,1)} %bitcast.15.q_ref, bf16[2048,128]{1,0:T(8,128)(2,1)} %bitcast.20.k_ref, bf16[2048,128]{1,0:T(8,128)(2,1)} %bitcast.140, f32[2048,128]{1,0:T(8,128)} %broadcast_in_dim.37.bias_ref), custom_call_target="tpu_custom_call" | custom-call | tf_op jit(solution)/shard_map/attend_forward/pallas_call | solution.py:225
  77.7 2.0 copy.46
  79.8 3.7 %all-to-all-start.3 = ((bf16[8,256,128]{1,2,0:T(8,128)(2,1)}), bf16[8,256,128]{1,2,0:T(8,128)(2,1)S(1)}, u32[]{:S(2)}, u32[]{:S(2)}) async-start(bf16[8,256,128]{1,2,0:T(8,128)(2,1)} %copy.46), calls=%async_computation.3 | async-start | bytes 1048576 | tf_op jit(solution)/shard_map/all_to_all | solution.py:576
  83.5 9.6 %all-to-all-done.3 = bf16[8,256,128]{1,2,0:T(8,128)(2,1)S(1)} async-done(((bf16[8,256,128]{1,2,0:T(8,128)(2,1)}), bf16[8,256,128]{1,2,0:T(8,128)(2,1)S(1)}, u32[]{:S(2)}, u32[]{:S(2)}) %all-to-all-start.3) | async-done | bytes 524320 | tf_op jit(solution)/shard_map/all_to_all | solution.py:576
  93.1 0.9 multiply_reduce_fusion.6
  94.0 8.2 %fusion.50 = f32[256,4096]{1,0:T(8,128)} fusion(bf16[1024,4096]{1,0:T(8,128)(2,1)} %param.18, f32[256,1024]{1,0:T(8,128)S(1)} %get-tuple-element.53, f32[1024]{0:T(1024)S(1)} %bitcast.165, f32[1024]{0:T(1024)S(1)} %bitcast.156, f32[256]{0:T(256)S(1)} %fusion.47), kind=kOutput, calls=%fused_computation.128 | convolution fusion | flops 2148532224 | bytes 13640704 | tf_op jit(solution)/shard_map/dot_general | solution.py:584
  102.2 11.3 %fusion.6 = bf16[256,4096]{1,0:T(8,128)(2,1)S(1)} fusion(f32[256,4096]{1,0:T(8,128)} %fusion.50, bf16[4096,1024]{1,0:T(8,128)(2,1)} %param.19, bf16[256,1024]{1,0:T(8,128)(2,1)S(1)} %copy-done.16, f32[1024]{0:T(1024)S(1)} %bitcast.183), kind=kOutput, calls=%fused_computation.11 | convolution fusion | flops 2169241600 | bytes 15208448 | tf_op jit(solution)/shard_map/dot_general | solution.py:60
  113.6 2.4 fusion.59
  116.5 7.5 %multiply_reduce_fusion.1 = (f32[256]{0:T(256)S(1)}, f32[256]{0:T(256)S(1)}, f32[256]{0:T(256)S(1)}, f32[1024]{0:T(1024)S(1)}, f32[1024]{0:T(1024)S(1)}, /*index=5*/f32[1024]{0:T(1024)S(1)}, bf16[256,1024]{1,0:T(8,128)(2,1)}) fusion(f32[1024]{0:T(1024)S(1)} %bitcast.184, f32[256,1024]{1,0:T(8,128)S(1)} %get-tuple-element.53, f32[256,1024]{1,0:T(8,128)S(1)} %fusion.59, ...), kind=kOutput, calls=%fused_computation.44 | convolution fusion | flops 2161373440 | bytes 15753216 | tf_op jit(solution)/shard_map/dot_general | solution.py:586
  124.6 1.1 copy-done.3
  125.6 0.8 fusion.10
  126.4 0.9 copy.57
  127.3 3.7 %all-to-all-start.4 = ((bf16[256,8,128]{2,0,1:T(8,128)(2,1)}), bf16[256,8,128]{2,0,1:T(8,128)(2,1)S(1)}, u32[]{:S(2)}, u32[]{:S(2)}) async-start(bf16[256,8,128]{2,0,1:T(8,128)(2,1)} %bitcast.125), calls=%async_computation.4 | async-start | bytes 1048576 | tf_op jit(solution)/shard_map/all_to_all | solution.py:616
  131.0 8.6 %convolution_convert_fusion = bf16[4096,1024]{1,0:T(8,128)(2,1)} fusion(bf16[256,1024]{1,0:T(8,128)(2,1)} %param.23, f32[1024]{0:T(1024)S(1)} %bitcast.185, f32[256,4096]{1,0:T(8,128)} %fusion.50), kind=kOutput, calls=%fused_computation | convolution fusion | flops 2161901568 | bytes 13111296 | tf_op jit(solution)/shard_map/dot_general | solution.py:54
  139.6 1.0 all-to-all-done.4
  140.7 0.8 copy-done.11
  141.4 15.9 %attend_backward.1 = (bf16[2048,128]{1,0:T(8,128)(2,1)}, bf16[2048,128]{1,0:T(8,128)(2,1)}, bf16[2048,128]{1,0:T(8,128)(2,1)}) custom-call(s32[8]{0:T(128)} %slice.30.first_ref, bf16[2048,128]{1,0:T(8,128)(2,1)} %bitcast.15.q_ref, bf16[2048,128]{1,0:T(8,128)(2,1)} %bitcast.20.k_ref, bf16[2048,128]{1,0:T(8,128)(2,1)} %bitcast.141, ...), custom_call_target="tpu_custom_call" | custom-call | tf_op jit(solution)/shard_map/attend_backward/pallas_call | solution.py:241
  157.3 2.1 copy.48
  159.5 4.2 %all-to-all-start.5 = ((bf16[8,256,128]{1,2,0:T(8,128)(2,1)}), bf16[8,256,128]{1,2,0:T(8,128)(2,1)}, u32[]{:S(2)}, u32[]{:S(2)}) async-start(bf16[8,256,128]{1,2,0:T(8,128)(2,1)} %copy.48), calls=%async_computation.5 | async-start | bytes 1048576 | tf_op jit(solution)/shard_map/all_to_all | solution.py:621
  163.6 0.7 multiply_reduce_fusion.9
  167.0 2.1 convolution_convert_fusion.2
  169.1 2.0 copy.49
  171.1 2.3 all-to-all-done.5
  173.4 3.5 all-to-all-start.6
  176.9 7.3 %convolution_convert_fusion.1 = bf16[1024,4096]{1,0:T(8,128)(2,1)} fusion(bf16[256,4096]{1,0:T(8,128)(2,1)} %copy-done.12, f32[256,1024]{1,0:T(8,128)S(1)} %copy-done.7, f32[1024]{0:T(1024)S(1)} %bitcast.166, f32[1024]{0:T(1024)S(1)} %bitcast.159, f32[256]{0:T(256)S(1)} %fusion.47), kind=kOutput, calls=%fused_computation.1 | convolution fusion | flops 2152726528 | bytes 11543552 | tf_op jit(solution)/shard_map/dot_general | solution.py:54
  184.2 1.0 copy.50
  185.2 2.3 convert_element_type.167
  187.5 4.4 %all-to-all-start.7 = ((bf16[8,256,128]{1,2,0:T(8,128)(2,1)}), bf16[8,256,128]{1,2,0:T(8,128)(2,1)}, u32[]{:S(2)}, u32[]{:S(2)}) async-start(bf16[8,256,128]{1,2,0:T(8,128)(2,1)} %copy.50), calls=%async_computation.7 | async-start | bytes 1048576 | tf_op jit(solution)/shard_map/all_to_all | solution.py:635
  192.0 1.5 subtract_convert_fusion
  193.6 0.8 fusion.60
  194.4 2.2 convolution_convert_fusion.5
  196.6 2.2 convolution_convert_fusion.4
  198.8 1.8 convolution_add_fusion.1
  200.5 1.2 all-to-all-done.7
  201.7 3.2 convolution_convert_fusion.3
  204.9 3.9 %fusion.13 = (f32[1024]{0:T(1024)S(1)}, f32[256]{0:T(256)S(1)}, f32[1024]{0:T(1024)S(1)}, f32[256,1024]{1,0:T(8,128)}) fusion(bf16[256,1024]{1,0:T(8,128)(2,1)S(1)} %copy-done.2, f32[256]{0:T(256)S(1)} %fusion.46, f32[1024]{0:T(1024)S(1)} %bitcast.173, f32[256,1024]{1,0:T(8,128)} %convolution_add_fusion.1, bf16[256,1024]{0,1:T(8,128)(2,1)} %bitcast.46, ...), kind=kOutput, calls=%fused_computation.37 | convolution fusion | flops 539227904 | bytes 5257216 | tf_op jit(solution)/shard_map/dot_general | solution.py:60
  208.9 8.5 %fusion.41 = f32[1,1024]{1,0:T(1,128)} fusion(bf16[1024,6144]{1,0:T(8,128)(2,1)} %param.20, bf16[1,1,6144]{2,1,0:T(2,128)(2,1)S(1)} %constant_dynamic-update-slice_fusion, bf16[1,1024]{1,0:T(2,128)(2,1)S(1)} %copy-done.21), kind=kOutput, calls=%fused_computation.106 | convolution fusion | flops 12593152 | bytes 12601344 | tf_op jit(solution)/shard_map/dot_general | solution.py:60
  217.4 0.7 maximum_reduce_fusion
  218.1 128.6 %scatter_sums.1 = (f32[32,1024]{1,0:T(8,128)}, f32[32,1024]{1,0:T(8,128)}, f32[32,1024]{1,0:T(8,128)}, f32[32,1024]{1,0:T(8,128)}, f32[32,4096]{1,0:T(8,128)}, /...) custom-call(bf16[4,2,2,2,32,1024]{5,4,3,2,1,0:T(8,128)(2,1)} %bitcast.130, ...), custom_call_target="tpu_custom_call" | custom-call | tf_op jit(solution)/shard_map/scatter_sums/pallas_call | solution.py:477
  346.8 1.2 copy.59
  348.0 2.5 fusion.16
  350.5 1.2 fusion.29
  351.8 0.7 copy.71
  352.4 0.7 copy.72
  354.4 0.8 copy.75
  355.2 0.8 copy.76
  (86 shorter events, 4.8 us)
Async XLA Ops:
  0.6 92.5 %copy-start = (bf16[1024,1024]{1,0:T(8,128)(2,1)S(1)}, bf16[1024,1024]{1,0:T(8,128)(2,1)}, u32[]{:S(2)}) copy-start(bf16[1024,1024]{1,0:T(8,128)(2,1)} %param.17) | copy-start | bytes 6291460
  2.0 6.5 %copy-start.2 = (bf16[256,1024]{1,0:T(8,128)(2,1)S(1)}, bf16[256,1024]{1,0:T(8,128)(2,1)}, u32[]{:S(2)}) copy-start(bf16[256,1024]{1,0:T(8,128)(2,1)} %param.12) | copy-start | bytes 1572868
  2.1 6.5 %copy-start.23 = (bf16[1024,1024]{1,0:T(8,128)(2,1)S(1)}, bf16[1024,1024]{1,0:T(8,128)(2,1)}, u32[]{:S(2)}) copy-start(bf16[1024,1024]{1,0:T(8,128)(2,1)} %param.16) | copy-start | bytes 6291460
  8.5 6.9 %copy-start.24 = (s32[1,3]{1,0:T(1,128)S(1)}, s32[1,3]{1,0:T(1,128)}, u32[]{:S(2)}) copy-start(s32[1,3]{1,0:T(1,128)} %param.21) | copy-start | bytes 40
  10.2 25.7 %all-to-all-start.2 = ((bf16[256,8,128]{2,0,1:T(8,128)(2,1)}), bf16[256,8,128]{2,0,1:T(8,128)(2,1)S(1)}, u32[]{:S(2)}, u32[]{:S(2)}) async-start(bf16[256,8,128]{2,0,1:T(8,128)(2,1)} %bitcast.146), calls=%async_computation.2 | async-start | bytes 1048576 | tf_op jit(solution)/shard_map/all_to_all | solution.py:568
  31.0 23.8 %copy-start.22 = (s32[2048]{0:T(1024)S(1)}, s32[2048]{0:T(1024)}, u32[]{:S(2)}) copy-start(s32[2048]{0:T(1024)} %param.22) | copy-start | bytes 24580
  36.0 29.2 %copy-start.10 = (bf16[256,8,128]{2,0,1:T(8,128)(2,1)}, bf16[256,8,128]{2,0,1:T(8,128)(2,1)S(1)}, u32[]{:S(2)}) copy-start(bf16[256,8,128]{2,0,1:T(8,128)(2,1)S(1)} %all-to-all-done.2) | copy-start | bytes 1572868
  36.0 14.0 %all-to-all-start.1 = ((bf16[256,8,128]{2,0,1:T(8,128)(2,1)}), bf16[256,8,128]{2,0,1:T(8,128)(2,1)}, u32[]{:S(2)}, u32[]{:S(2)}) async-start(bf16[256,8,128]{2,0,1:T(8,128)(2,1)} %copy.44), calls=%async_computation.1 | async-start | bytes 1048576 | tf_op jit(solution)/shard_map/all_to_all | solution.py:567
  40.2 43.3 %copy-start.21 = (bf16[1,1024]{1,0:T(2,128)(2,1)S(1)}, bf16[1,1024]{1,0:T(2,128)(2,1)}, u32[]{:S(2)}) copy-start(bf16[1,1024]{1,0:T(2,128)(2,1)} %param.13) | copy-start | bytes 6148
  50.0 13.9 %all-to-all-start = ((bf16[256,8,128]{2,0,1:T(8,128)(2,1)}), bf16[256,8,128]{2,0,1:T(8,128)(2,1)}, u32[]{:S(2)}, u32[]{:S(2)}) async-start(bf16[256,8,128]{2,0,1:T(8,128)(2,1)} %copy.42), calls=%async_computation | async-start | bytes 1048576 | tf_op jit(solution)/shard_map/all_to_all | solution.py:566
  79.8 13.3 %all-to-all-start.3 = ((bf16[8,256,128]{1,2,0:T(8,128)(2,1)}), bf16[8,256,128]{1,2,0:T(8,128)(2,1)S(1)}, u32[]{:S(2)}, u32[]{:S(2)}) async-start(bf16[8,256,128]{1,2,0:T(8,128)(2,1)} %copy.46), calls=%async_computation.3 | async-start | bytes 1048576 | tf_op jit(solution)/shard_map/all_to_all | solution.py:576
  94.0 30.0 %copy-start.6 = (f32[256,1024]{1,0:T(8,128)}, f32[256,1024]{1,0:T(8,128)S(1)}, u32[]{:S(2)}) copy-start(f32[256,1024]{1,0:T(8,128)S(1)} %get-tuple-element.53) | copy-start | bytes 3145732
  94.0 8.2 %copy-start.16 = (bf16[256,1024]{1,0:T(8,128)(2,1)S(1)}, bf16[256,1024]{1,0:T(8,128)(2,1)}, u32[]{:S(2)}) copy-start(bf16[256,1024]{1,0:T(8,128)(2,1)} %param.23) | copy-start | bytes 1572868
  94.0 19.5 %slice-start = ((s8[8388608]{0:T(1024)(128)(4,1)}), s8[4194304]{0:T(1024)(128)(4,1)S(1)}, s32[]{:S(2)}) async-start(s8[8388608]{0:T(1024)(128)(4,1)} %bitcast.192), calls=%async_computation.8 | async-start | bytes 8388608
  102.2 11.3 %slice-start.1 = ((s8[8388608]{0:T(1024)(128)(4,1)}), s8[4194304]{0:T(1024)(128)(4,1)S(1)}, s32[]{:S(2)}) async-start(s8[8388608]{0:T(1024)(128)(4,1)} %bitcast.192), calls=%async_computation.9 | async-start | bytes 8388608
  113.6 2.4 copy-start.12
  113.6 2.9 copy-start.25
  124.6 1.1 copy-start.3
  127.3 13.4 %all-to-all-start.4 = ((bf16[256,8,128]{2,0,1:T(8,128)(2,1)}), bf16[256,8,128]{2,0,1:T(8,128)(2,1)S(1)}, u32[]{:S(2)}, u32[]{:S(2)}) async-start(bf16[256,8,128]{2,0,1:T(8,128)(2,1)} %bitcast.125), calls=%async_computation.4 | async-start | bytes 1048576 | tf_op jit(solution)/shard_map/all_to_all | solution.py:616
  139.6 27.3 %copy-start.4 = (f32[256,1024]{1,0:T(8,128)S(1)}, f32[256,1024]{1,0:T(8,128)}, u32[]{:S(2)}) copy-start(f32[256,1024]{1,0:T(8,128)} %copy-done.3) | copy-start | bytes 3145732
  140.7 0.8 copy-start.11
  157.3 19.5 %copy-start.7 = (f32[256,1024]{1,0:T(8,128)S(1)}, f32[256,1024]{1,0:T(8,128)}, u32[]{:S(2)}) copy-start(f32[256,1024]{1,0:T(8,128)} %copy-done.6) | copy-start | bytes 3145732
  159.5 13.9 %all-to-all-start.5 = ((bf16[8,256,128]{1,2,0:T(8,128)(2,1)}), bf16[8,256,128]{1,2,0:T(8,128)(2,1)}, u32[]{:S(2)}, u32[]{:S(2)}) async-start(bf16[8,256,128]{1,2,0:T(8,128)(2,1)} %copy.48), calls=%async_computation.5 | async-start | bytes 1048576 | tf_op jit(solution)/shard_map/all_to_all | solution.py:621
  173.4 14.1 %all-to-all-start.6 = ((bf16[8,256,128]{1,2,0:T(8,128)(2,1)}), bf16[8,256,128]{1,2,0:T(8,128)(2,1)S(1)}, u32[]{:S(2)}, u32[]{:S(2)}) async-start(bf16[8,256,128]{1,2,0:T(8,128)(2,1)} %copy.49), calls=%async_computation.6 | async-start | bytes 1048576 | tf_op jit(solution)/shard_map/all_to_all | solution.py:628
  176.9 7.3 %copy-start.13 = (bf16[2048,128]{1,0:T(8,128)(2,1)S(1)}, bf16[2048,128]{1,0:T(8,128)(2,1)}, u32[]{:S(2)}) copy-start(bf16[2048,128]{1,0:T(8,128)(2,1)} %get-tuple-element.27) | copy-start | bytes 1572868
  185.2 8.4 %copy-start.8 = (bf16[1024,1024]{1,0:T(8,128)(2,1)S(1)}, bf16[1024,1024]{1,0:T(8,128)(2,1)}, u32[]{:S(2)}) copy-start(bf16[1024,1024]{1,0:T(8,128)(2,1)} %param.14) | copy-start | bytes 6291460
  187.5 14.2 %all-to-all-start.7 = ((bf16[8,256,128]{1,2,0:T(8,128)(2,1)}), bf16[8,256,128]{1,2,0:T(8,128)(2,1)}, u32[]{:S(2)}, u32[]{:S(2)}) async-start(bf16[8,256,128]{1,2,0:T(8,128)(2,1)} %copy.50), calls=%async_computation.7 | async-start | bytes 1048576 | tf_op jit(solution)/shard_map/all_to_all | solution.py:635
  194.4 4.4 %copy-start.9 = (bf16[1024,1024]{1,0:T(8,128)(2,1)S(1)}, bf16[1024,1024]{1,0:T(8,128)(2,1)}, u32[]{:S(2)}) copy-start(bf16[1024,1024]{1,0:T(8,128)(2,1)} %param.15) | copy-start | bytes 6291460
  218.1 129.9 %copy-start.5 = (f32[256,1024]{1,0:T(8,128)S(1)}, f32[256,1024]{1,0:T(8,128)}, u32[]{:S(2)}) copy-start(f32[256,1024]{1,0:T(8,128)} %copy-done.3) | copy-start | bytes 3145732
  346.7 5.1 %copy-start.20 = (f32[32,1024]{1,0:T(8,128)S(1)}, f32[32,1024]{1,0:T(8,128)}, u32[]{:S(2)}) copy-start(f32[32,1024]{1,0:T(8,128)} %get-tuple-element.95) | copy-start | bytes 393220
  346.7 5.7 %copy-start.19 = (f32[32,1024]{1,0:T(8,128)S(1)}, f32[32,1024]{1,0:T(8,128)}, u32[]{:S(2)}) copy-start(f32[32,1024]{1,0:T(8,128)} %get-tuple-element.96) | copy-start | bytes 393220
  346.7 6.4 %copy-start.18 = (f32[32,1024]{1,0:T(8,128)S(1)}, f32[32,1024]{1,0:T(8,128)}, u32[]{:S(2)}) copy-start(f32[32,1024]{1,0:T(8,128)} %get-tuple-element.97) | copy-start | bytes 393220
  346.7 7.0 %copy-start.17 = (f32[32,1024]{1,0:T(8,128)S(1)}, f32[32,1024]{1,0:T(8,128)}, u32[]{:S(2)}) copy-start(f32[32,1024]{1,0:T(8,128)} %get-tuple-element.98) | copy-start | bytes 393220
  346.7 7.7 %copy-start.15 = (f32[32,4096]{1,0:T(8,128)S(1)}, f32[32,4096]{1,0:T(8,128)}, u32[]{:S(2)}) copy-start(f32[32,4096]{1,0:T(8,128)} %get-tuple-element.99) | copy-start | bytes 1572868
  346.7 8.4 %copy-start.14 = (f32[128,1024]{1,0:T(8,128)S(1)}, f32[128,1024]{1,0:T(8,128)}, u32[]{:S(2)}) copy-start(f32[128,1024]{1,0:T(8,128)} %get-tuple-element.100) | copy-start | bytes 1572868
  346.8 9.2 %copy-start.1 = (bf16[1024,1024]{1,0:T(8,128)(2,1)S(1)}, bf16[1024,1024]{1,0:T(8,128)(2,1)}, u32[]{:S(2)}) copy-start(bf16[1024,1024]{1,0:T(8,128)(2,1)} %param.17) | copy-start | bytes 6291460

commit v2 on v1

v2 whole, which is shorter than its diff:
```python
import math

import jax
import jax.numpy as jnp
from jax import lax
from jax.experimental import pallas as pl
from jax.experimental.pallas import tpu as pltpu
from jax.sharding import PartitionSpec as P

HEADS = 16
HEAD_DIM = 64
PATCHES = 256


EPSILON = 1e-06
MASKED = -1e30


def rms_normed(values):
    return values * lax.rsqrt(jnp.mean(values * values, axis=-1, keepdims=True) + EPSILON)


def modulate(values, shift, scaling):
    return rms_normed(values) * (1.0 + scaling) + shift


def frequencies(half_dim):
    return jnp.exp(jnp.arange(half_dim, dtype=jnp.float32) * (-math.log(10000.0) / half_dim))


def rotate(values, angles):
    half_dim = values.shape[-1] // 2
    cosine = jnp.cos(angles)[:, None, :]
    sine_part = jnp.sin(angles)[:, None, :]
    first_half = values[..., :half_dim]
    second = values[..., half_dim:]
    return jnp.concatenate(
        [first_half * cosine - second * sine_part, first_half * sine_part + second * cosine],
        axis=-1,
    )


def group_layout(lengths, token_count, patches):
    frame_of = jnp.arange(token_count, dtype=jnp.int32) // patches
    clip_ends = jnp.cumsum(lengths)
    starts = clip_ends - lengths
    clip_of = jnp.sum((frame_of[:, None] >= clip_ends[None, :]).astype(jnp.int32), axis=1)
    picked = clip_of[:, None] == jnp.arange(lengths.shape[0], dtype=jnp.int32)[None, :]
    position = frame_of - jnp.sum(jnp.where(picked, starts[None, :], 0), axis=1)
    return (clip_of, frame_of, position)


def inner_rows(left, right):
    return lax.dot_general(
        left, right, (((0,), (0,)), ((), ())), preferred_element_type=jnp.float32
    )


def times_transposed(left, right):
    return lax.dot_general(
        left, right, (((1,), (1,)), ((), ())), preferred_element_type=jnp.float32
    )


def frame_stats(values, valid_f):
    sums = jnp.sum(values * values, axis=2) * valid_f
    return jnp.sqrt(jnp.sum(sums, axis=1) / (values.shape[1] * values.shape[2]) + EPSILON)


def dot_nt(left, right):
    return lax.dot_general(
        left, right, (((1,), (1,)), ((), ())), preferred_element_type=jnp.float32
    )


def dot_nn(left, right):
    return lax.dot_general(
        left, right, (((1,), (0,)), ((), ())), preferred_element_type=jnp.float32
    )


def head_parts(block):
    lane = lax.broadcasted_iota(jnp.int32, block.shape, 1)
    zero = jnp.zeros_like(block)
    return jnp.where(lane < HEAD_DIM, block, zero), jnp.where(lane < HEAD_DIM, zero, block)


def key_bias(bias_ref, key_frame, frame):
    half = bias_ref[pl.ds(key_frame * PATCHES, PATCHES), :]
    bias = jnp.concatenate([half, half], axis=1)
    row = lax.broadcasted_iota(jnp.int32, bias.shape, 0)
    column = lax.broadcasted_iota(jnp.int32, bias.shape, 1)
    own = (row == column) & (key_frame == frame)
    return jnp.where(own, 0.0, bias)


def attend_forward_kernel(first_ref, q_ref, k_ref, v_ref, bias_ref, o_ref, lse_ref, scores):
    frames = q_ref.shape[0] // PATCHES

    def one_frame(frame, _):
        rows = pl.ds(frame * PATCHES, PATCHES)
        parts = head_parts(q_ref[rows, :] * jnp.bfloat16(0.125))
        first = first_ref[frame]

        def score(key_frame, tops):
            keys = k_ref[pl.ds(key_frame * PATCHES, PATCHES), :]
            bias = key_bias(bias_ref, key_frame, frame)
            new = []
            for head in range(2):
                value = dot_nt(keys, parts[head]) + bias
                scores[head, key_frame - first] = value
                new.append(jnp.maximum(tops[head], jnp.max(value, axis=0, keepdims=True)))
            return tuple(new)

        low = jnp.full((1, PATCHES), MASKED, jnp.float32)
        tops = lax.fori_loop(first, frame + 1, score, (low, low))

        def exponent(key_frame, totals):
            new = []
            for head in range(2):
                value = jnp.exp(scores[head, key_frame - first] - tops[head])
                scores[head, key_frame - first] = value
                new.append(totals[head] + jnp.sum(value, axis=0, keepdims=True))
            return tuple(new)

        zero = jnp.zeros((1, PATCHES), jnp.float32)
        totals = lax.fori_loop(first, frame + 1, exponent, (zero, zero))
        inverse = [1.0 / total for total in totals]

        def weigh(key_frame, sums):
            turned = v_ref[pl.ds(key_frame * PATCHES, PATCHES), :].T
            new = []
            for head in range(2):
                probs = (scores[head, key_frame - first] * inverse[head]).astype(jnp.bfloat16)
                new.append(
                    sums[head]
                    + dot_nn(turned[head * HEAD_DIM : (head + 1) * HEAD_DIM, :], probs)
                )
            return tuple(new)

        empty = jnp.zeros((HEAD_DIM, PATCHES), jnp.float32)
        sums = lax.fori_loop(first, frame + 1, weigh, (empty, empty))
        o_ref[rows, :] = jnp.concatenate(sums, axis=0).T.astype(jnp.bfloat16)
        for head in range(2):
            lse_ref[frame, head : head + 1, :] = tops[head] + jnp.log(totals[head])
        return 0

    lax.fori_loop(0, frames, one_frame, 0)


IN_SMEM = pl.BlockSpec(memory_space=pltpu.SMEM)
IN_VMEM = pl.BlockSpec(memory_space=pltpu.VMEM)
IN_PLACE = pl.BlockSpec(memory_space=pl.ANY)
MESH_ID = pl.DeviceIdType.MESH


def attend_forward(first, queries, keys, values, bias):
    tokens, width = queries.shape
    frames = tokens // PATCHES
    return pl.pallas_call(
        attend_forward_kernel,
        out_shape=(
            jax.ShapeDtypeStruct((tokens, width), jnp.bfloat16),
            jax.ShapeDtypeStruct((frames, 2, PATCHES), jnp.float32),
        ),
        in_specs=[IN_SMEM] + [IN_VMEM] * 4,
        out_specs=(IN_VMEM, IN_VMEM),
        scratch_shapes=[pltpu.VMEM((2, 4, PATCHES, PATCHES), jnp.float32)],
        name="attend_forward",
    )(first, queries, keys, values, bias)


SLOTS = 17
BLOCK = 256


def peer_head(head, flips):
    core = lax.rem(head, 2)
    second = lax.rem(lax.div(head, 2), 2)
    third = lax.div(head, 4)
    if flips % 2:
        core = 1 - core
    if flips // 2 % 2:
        second = 1 - second
    if flips // 4:
        third = 1 - third
    return 4 * third + 2 * second + core


def remote(source, target, send, receive, where):
    return pltpu.make_async_remote_copy(
        src_ref=source,
        dst_ref=target,
        send_sem=send,
        recv_sem=receive,
        device_id=where,
        device_id_type=MESH_ID,
    )


def gelu_and_slope(value):
    square = value * value
    inner = 0.7978845608028654 * value * (1.0 + 0.044715 * square)
    bend = jnp.tanh(inner)
    half = 0.5 * (1.0 + bend)
    slope = half + 0.5 * value * (1.0 - bend * bend) * (
        0.7978845608028654 * (1.0 + 0.134145 * square)
    )
    return value * half, slope


def turn_pairs(values, column):
    lane = lax.rem(lax.broadcasted_iota(jnp.int32, values.shape, 1), HEAD_DIM)
    up = pltpu.roll(values, 128 - HEAD_DIM // 2, 1)
    down = pltpu.roll(values, HEAD_DIM // 2, 1)
    return jnp.where(lane < HEAD_DIM // 2, up, down)


def back_kernel(n_dp, *refs):
    (
        table,
        att_own,
        q_ref,
        k_ref,
        v_ref,
        lse_ref,
        bias_ref,
        x_ref,
        cot_ref,
        n1_ref,
        mod_ref,
        cond_ref,
        valid_ref,
        wo_hbm,
        up_hbm,
        down_hbm,
        wq_hbm,
        wk_hbm,
        wv_hbm,
        block_ref,
        gin_ref,
        stat_ref,
        gq_ref,
        gk_ref,
        gv_ref,
        go_ref,
        gup_ref,
        gdown_ref,
        rows_ref,
        att_fr,
        do_own,
        back,
        from_core,
        from_first,
        from_second,
        from_dp,
        core_out,
        da_send,
        lhs,
        n2,
        dmlp,
        dhid,
        dattn,
        ba,
        mid,
        wo,
        load_sem,
        a2a_send,
        a2a_recv,
        core_send,
        core_recv,
        first_send,
        first_recv,
        second_send,
        second_recv,
        dp_send,
        dp_recv,
        row_send,
        row_recv,
        row_dp_send,
        row_dp_recv,
    ) = refs
    tokens, width = x_ref.shape
    frames = q_ref.shape[0]
    hidden_width = up_hbm.shape[1]
    tiles = hidden_width // width
    chunks = width // BLOCK
    small = width // (n_dp * 8)
    large = hidden_width // (n_dp * 8)
    half_rows = n_dp * 4 * small
    group = lax.axis_index("dp")
    head = lax.axis_index("head")
    core = lax.rem(head, 2)
    xbit = lax.rem(lax.div(head, 2), 2)
    ybit = lax.div(head, 4)
    core_peer, x_peer, y_peer = peer_head(head, 1), peer_head(head, 2), peer_head(head, 4)
    dp_peers = [lax.rem(group + hop, n_dp) for hop in range(1, n_dp)]
    others = range(1, 8)

    barrier = pltpu.get_barrier_semaphore()
    for flips in others:
        pl.semaphore_signal(
            barrier, inc=1, device_id=(group, peer_head(head, flips)), device_id_type=MESH_ID
        )
    for peer in dp_peers:
        pl.semaphore_signal(barrier, inc=1, device_id=(peer, head), device_id_type=MESH_ID)

    wo_load = pltpu.make_async_copy(wo_hbm, wo, load_sem.at[0])
    wo_load.start()
    pl.semaphore_wait(barrier, 7 + len(dp_peers))

    own_rows = pl.ds(head * tokens, tokens)
    own_lanes = pl.ds(head * 128, 128)

    def att_copy(flips):
        peer = peer_head(head, flips)
        return remote(
            att_own.at[pl.ds(peer * tokens, tokens), :],
            att_fr.at[:, own_lanes],
            a2a_send.at[0, flips],
            a2a_recv.at[0, flips],
            (group, peer),
        )

    def grad_copy(flips):
        peer = peer_head(head, flips)
        return remote(
            da_send.at[:, pl.ds(peer * 128, 128)],
            do_own.at[head],
            a2a_send.at[1, flips],
            a2a_recv.at[1, flips],
            (group, peer),
        )

    first_up = large // small
    first_out = first_up + tiles
    count = first_out + 4

    def slot_of(unit):
        return unit if unit < first_out + 1 else unit - first_out - 1

    def lhs_of(unit):
        if unit < first_up:
            return unit
        if unit < first_out:
            return first_up
        return first_up + 1 if unit == first_out else first_up + 2

    def core_copy(unit):
        return remote(
            core_out.at[unit % 2],
            from_core.at[slot_of(unit)],
            core_send.at[unit],
            core_recv.at[unit],
            (group, core_peer),
        )

    def x_leads(unit):
        return unit % 2 == 0

    def first_copy(unit):
        slot = slot_of(unit)
        if x_leads(unit):
            source, peer = from_core.at[slot, :, :, 1 - xbit], x_peer
        else:
            source, peer = from_core.at[slot, :, 1 - ybit], y_peer
        return remote(
            source, from_first.at[slot], first_send.at[unit], first_recv.at[unit], (group, peer)
        )

    def second_copy(unit):
        slot = slot_of(unit)
        if x_leads(unit):
            source, peer = from_core.at[slot, :, 1 - ybit, xbit], y_peer
        else:
            source, peer = from_core.at[slot, :, ybit, 1 - xbit], x_peer
        return remote(
            source, from_second.at[slot], second_send.at[unit], second_recv.at[unit], (group, peer)
        )

    def dp_copy(unit, hop):
        peer = dp_peers[hop]
        return remote(
            from_core.at[slot_of(unit), peer, ybit, xbit],
            from_dp.at[unit, hop],
            dp_send.at[unit, hop],
            dp_recv.at[unit, hop],
            (peer, head),
        )

    def added(left, right):
        return (left.astype(jnp.float32) + right.astype(jnp.float32)).astype(jnp.bfloat16)

    def produce(unit, right):
        if unit >= 2:
            core_copy(unit - 2).wait_send()
        left = lhs_of(unit)

        def body(chunk, _):
            lanes = pl.ds(pl.multiple_of(chunk * BLOCK, BLOCK), BLOCK)
            value = dot_nn(lhs[left, 1 - core], right(chunk)).astype(jnp.bfloat16)
            core_out[unit % 2, :, :, :, :, lanes] = value.reshape(n_dp, 2, 2, small, BLOCK)
            return 0

        lax.fori_loop(0, chunks, body, 0)
        core_copy(unit).start()

    def take_core(unit, right):
        core_copy(unit).wait_recv()
        left, slot = lhs_of(unit), slot_of(unit)

        def body(chunk, _):
            lanes = pl.ds(pl.multiple_of(chunk * BLOCK, BLOCK), BLOCK)
            value = dot_nn(lhs[left, core], right(chunk))
            came = from_core[slot, :, :, :, :, lanes].reshape(half_rows, BLOCK)
            value = (value + came.astype(jnp.float32)).astype(jnp.bfloat16)
            from_core[slot, :, :, :, :, lanes] = value.reshape(n_dp, 2, 2, small, BLOCK)
            return 0

        lax.fori_loop(0, chunks, body, 0)
        first_copy(unit).start()

    def take_first(unit):
        first_copy(unit).wait()
        slot = slot_of(unit)

        def body(index, _):
            at_dp = lax.div(index, 2)
            other = lax.rem(index, 2)
            at_y, at_x = (other, xbit) if x_leads(unit) else (ybit, other)
            from_core[slot, at_dp, at_y, at_x] = added(
                from_core[slot, at_dp, at_y, at_x], from_first[slot, at_dp, other]
            )
            return 0

        lax.fori_loop(0, n_dp * 2, body, 0)
        second_copy(unit).start()

    def take_second(unit):
        second_copy(unit).wait()
        slot = slot_of(unit)

        def body(at_dp, _):
            from_core[slot, at_dp, ybit, xbit] = added(
                from_core[slot, at_dp, ybit, xbit], from_second[slot, at_dp]
            )
            return 0

        lax.fori_loop(0, n_dp, body, 0)
        for hop in range(n_dp - 1):
            dp_copy(unit, hop).start()

    def take_dp(unit):
        for hop in range(n_dp - 1):
            dp_copy(unit, hop).wait()
        total = from_core[slot_of(unit), group, ybit, xbit].astype(jnp.float32)
        for hop in range(n_dp - 1):
            total = total + from_dp[unit, hop].astype(jnp.float32)
        if unit < first_up:
            gdown_ref[unit * small : (unit + 1) * small, :] = total
        elif unit < first_out:
            place = (unit - first_up) * width
            gup_ref[:, place : place + width] = total
        else:
            (go_ref, gv_ref, gq_ref, gk_ref)[unit - first_out][...] = total

    def turned_rows(index, source):
        for chunk in range(chunks):
            value = source[:, chunk * BLOCK : (chunk + 1) * BLOCK].T
            value = value.reshape(BLOCK // (2 * small), 2, small, tokens)
            for side in range(2):
                lhs[index, side, chunk * BLOCK // 2 : (chunk + 1) * BLOCK // 2, :] = value[
                    :, side
                ].reshape(BLOCK // 2, tokens)

    shift_one, scale_one, gate_one = (mod_ref[row : row + 1, :] for row in range(3))
    shift_two, scale_two, gate_two = (mod_ref[row : row + 1, :] for row in range(3, 6))
    step_rows = 32
    steps = tokens // step_rows

    def row_block(index):
        return pl.ds(pl.multiple_of(index * step_rows, step_rows), step_rows)

    def lane_block(chunk):
        return pl.ds(pl.multiple_of(chunk * BLOCK, BLOCK), BLOCK)

    def masked_square(values, rows):
        sums = jnp.sum(values * values, axis=1, keepdims=True) * valid_ref[rows, :1]
        return jnp.sum(sums, axis=0, keepdims=True)

    one = jnp.zeros((1, 1), jnp.float32)
    row_zero = jnp.zeros((1, width), jnp.float32)

    for flips in others:
        att_copy(flips).start()
    att_fr[:, own_lanes] = att_own[own_rows, :]

    def down_right(chunk):
        return dmlp[:, lane_block(chunk)]

    def up_right(unit):
        def value(chunk):
            start = (unit - first_up) * width + chunk * BLOCK
            return dhid[:, pl.ds(pl.multiple_of(start, BLOCK), BLOCK)]

        return value

    def mlp_right(unit):
        return down_right if unit < first_up else up_right(unit)

    def out_right(chunk):
        return dattn[:, lane_block(chunk)]

    def mlp_part(up, down, act, dn2):
        up_loads = [
            pltpu.make_async_copy(
                up_hbm.at[:, pl.ds(tile * width, width)],
                up.at[:, pl.ds(tile * width, width)],
                load_sem.at[1 + tile],
            )
            for tile in range(tiles)
        ]
        down_loads = [
            pltpu.make_async_copy(
                down_hbm.at[pl.ds(tile * width, width), :],
                down.at[pl.ds(tile * width, width), :],
                load_sem.at[1 + tiles + tile],
            )
            for tile in range(tiles)
        ]
        for tile in range(tiles):
            up_loads[tile].start()
            down_loads[tile].start()

        turned_rows(first_up + 2, n1_ref)
        wo_load.wait()
        for flips in others:
            att_copy(flips).wait()
        turned_rows(first_up + 1, att_fr)

        def project(chunk, _):
            lanes = lane_block(chunk)
            ba[:, lanes] = dot_nn(att_fr[...], wo[:, lanes])
            return 0

        lax.fori_loop(0, chunks, project, 0)

        def second_norm(index, total):
            rows = row_block(index)
            branch = gate_one * ba[rows, :]
            value = x_ref[rows, :].astype(jnp.float32) + branch
            mid[rows, :] = value
            scale = lax.rsqrt(jnp.mean(value * value, axis=1, keepdims=True) + EPSILON)
            n2[rows, :] = (value * scale * (1.0 + scale_two) + shift_two).astype(jnp.bfloat16)
            dmlp[rows, :] = (gate_two * cot_ref[rows, :].astype(jnp.float32)).astype(jnp.bfloat16)
            return total + masked_square(branch, rows)

        stat_attn = lax.fori_loop(0, steps, second_norm, one)
        turned_rows(first_up, n2)

        pairs = BLOCK // (2 * large)

        def feed(index, _):
            @pl.when(lax.rem(index, chunks) == 0)
            def _():
                tile = lax.div(index, chunks)
                pltpu.make_async_copy(
                    up_hbm.at[:, pl.ds(0, width)],
                    up.at[:, pl.ds(0, width)],
                    load_sem.at[1 + tile],
                ).wait()
                pltpu.make_async_copy(
                    down_hbm.at[pl.ds(0, width), :],
                    down.at[pl.ds(0, width), :],
                    load_sem.at[1 + tiles + tile],
                ).wait()

            lanes = lane_block(index)
            active, slope = gelu_and_slope(dot_nn(n2[...], up[:, lanes]))
            active = active.astype(jnp.bfloat16)
            act[:, lanes] = active
            grad = dot_nt(dmlp[...], down[lanes, :])
            dhid[:, lanes] = (grad * slope).astype(jnp.bfloat16)
            turned = active.T.reshape(pairs, 2, first_up, small, tokens)
            where = pl.ds(pl.multiple_of(index * pairs * small, pairs * small), pairs * small)
            for unit in range(first_up):
                for side in range(2):
                    lhs[unit, side, where, :] = turned[:, side, unit].reshape(
                        pairs * small, tokens
                    )
            return 0

        lax.fori_loop(0, hidden_width // BLOCK, feed, 0)

        produce(0, mlp_right(0))
        produce(1, mlp_right(1))

        def to_normed(chunk, _):
            lanes = lane_block(chunk)
            dn2[:, lanes] = dot_nt(dhid[...], up[lanes, :])
            return 0

        lax.fori_loop(0, chunks, to_normed, 0)
        take_core(0, mlp_right(0))
        take_core(1, mlp_right(1))

        def second_norm_back(index, sums):
            shift_sum, scale_sum, gate_sum = sums
            rows = row_block(index)
            value = mid[rows, :]
            scale = lax.rsqrt(jnp.mean(value * value, axis=1, keepdims=True) + EPSILON)
            normed = value * scale
            grad = dn2[rows, :]
            shift_sum = shift_sum + jnp.sum(grad, axis=0, keepdims=True)
            scale_sum = scale_sum + jnp.sum(grad * normed, axis=0, keepdims=True)
            inner = grad * (1.0 + scale_two)
            mean = jnp.mean(inner * normed, axis=1, keepdims=True)
            total = cot_ref[rows, :].astype(jnp.float32) + scale * (inner - normed * mean)
            dn2[rows, :] = total
            gate_sum = gate_sum + jnp.sum(total * ba[rows, :], axis=0, keepdims=True)
            dattn[rows, :] = (gate_one * total).astype(jnp.bfloat16)
            return shift_sum, scale_sum, gate_sum

        shift_two_grad, scale_two_grad, gate_one_grad = lax.fori_loop(
            0, steps, second_norm_back, (row_zero, row_zero, row_zero)
        )

        def to_attended(chunk, _):
            lanes = lane_block(chunk)
            da_send[:, lanes] = dot_nt(dattn[...], wo[lanes, :]).astype(jnp.bfloat16)
            return 0

        lax.fori_loop(0, chunks, to_attended, 0)
        for flips in others:
            grad_copy(flips).start()
        do_own[head] = da_send[:, own_lanes]

        produce(2, mlp_right(2))
        produce(3, mlp_right(3))

        def branch_out(chunk, _):
            lanes = lane_block(chunk)
            ba[:, lanes] = dot_nn(act[...], down[:, lanes])
            return 0

        lax.fori_loop(0, chunks, branch_out, 0)
        take_core(2, mlp_right(2))
        take_core(3, mlp_right(3))

        def outputs(index, sums):
            gate_sum, stat_mlp, stat_out = sums
            rows = row_block(index)
            raw = ba[rows, :]
            branch = gate_two * raw
            value = mid[rows, :] + branch
            block_ref[rows, :] = value.astype(jnp.bfloat16)
            gate_sum = gate_sum + jnp.sum(
                cot_ref[rows, :].astype(jnp.float32) * raw, axis=0, keepdims=True
            )
            stat_mlp = stat_mlp + masked_square(branch, rows)
            stat_out = stat_out + masked_square(value, rows)
            mid[rows, :] = dn2[rows, :]
            return gate_sum, stat_mlp, stat_out

        gate_two_grad, stat_mlp, stat_out = lax.fori_loop(0, steps, outputs, (row_zero, one, one))
        lane = lax.broadcasted_iota(jnp.int32, stat_ref.shape, 1)
        stats = jnp.where(lane == 0, stat_attn, jnp.where(lane == 1, stat_mlp, stat_out))
        stat_ref[...] = jnp.sqrt(stats / (tokens * width) + EPSILON)
        for row, vector in (
            (3, gate_one_grad),
            (4, shift_two_grad),
            (5, scale_two_grad),
            (6, gate_two_grad),
        ):
            gin_ref[row : row + 1, :] = vector
        produce(4, mlp_right(4))
        produce(5, mlp_right(5))

    pl.run_scoped(
        mlp_part,
        pltpu.VMEM((width, hidden_width), jnp.bfloat16),
        pltpu.VMEM((hidden_width, width), jnp.bfloat16),
        pltpu.VMEM((tokens, hidden_width), jnp.bfloat16),
        pltpu.VMEM((tokens, width), jnp.float32),
    )
    saved_rows = [gin_ref[row : row + 1, :] for row in range(3, 7)]

    def attention_part(wqkv, dq_slots, dk_slots, dv_slots, qkv_send, dq_raw, dk_raw, deltas):
        qkv_loads = [
            pltpu.make_async_copy(source, wqkv.at[place], load_sem.at[1 + 2 * tiles + place])
            for place, source in enumerate((wq_hbm, wk_hbm, wv_hbm))
        ]
        for copy in qkv_loads:
            copy.start()
        take_first(0)
        take_first(1)
        for flips in others:
            grad_copy(flips).wait()
        for slots in (dq_slots, dk_slots, dv_slots):
            slots[SLOTS] = jnp.zeros(slots.shape[1:], jnp.float32)

        def frame_delta(frame, _):
            rows = pl.ds(pl.multiple_of(frame * tokens, tokens), tokens)
            product = (
                do_own[frame].astype(jnp.float32) * att_own[rows, :].astype(jnp.float32)
            ).T
            for part in range(2):
                deltas[frame, part : part + 1, :] = jnp.sum(
                    product[part * HEAD_DIM : (part + 1) * HEAD_DIM, :], axis=0, keepdims=True
                )
            return 0

        lax.fori_loop(0, frames, frame_delta, 0)

        side_work = {
            1: lambda: take_core(4, mlp_right(4)),
            2: lambda: take_core(5, mlp_right(5)),
            3: lambda: produce(6, mlp_right(6)),
            4: lambda: take_second(0),
            5: lambda: take_second(1),
            6: lambda: take_first(2),
            7: lambda: take_first(3),
            8: lambda: take_core(6, mlp_right(6)),
            9: lambda: produce(7, mlp_right(7)),
            10: lambda: take_dp(0),
            11: lambda: take_dp(1),
            12: lambda: take_second(2),
            13: lambda: take_second(3),
            14: lambda: take_first(4),
            15: lambda: take_core(7, mlp_right(7)),
            16: lambda: take_dp(2),
        }

        def one_slot(index, _):
            frame = table[index]
            key_frame = table[SLOTS + index]
            q_parts = head_parts(q_ref[frame] * jnp.bfloat16(0.125))
            do_parts = head_parts(do_own[frame])
            keys = k_ref[key_frame]
            values = v_ref[key_frame]
            turned = keys.T
            half = bias_ref[key_frame]
            row = lax.broadcasted_iota(jnp.int32, (tokens, tokens), 0)
            column = lax.broadcasted_iota(jnp.int32, (tokens, tokens), 1)
            same = table[2 * SLOTS + 8 * frames + index].astype(jnp.float32)
            keep = 1.0 - jnp.where(row == column, 1.0, 0.0) * same
            bias = jnp.concatenate([half, half], axis=1) * keep
            dv = dk = None
            dq = []
            for part in range(2):
                lse = lse_ref[frame, part : part + 1, :]
                delta = deltas[frame, part : part + 1, :]
                probs = jnp.exp(dot_nt(keys, q_parts[part]) + bias - lse)
                prob_grad = dot_nt(values, do_parts[part])
                score_grad = (probs * (prob_grad - delta)).astype(jnp.bfloat16)
                dv_part = dot_nn(probs.astype(jnp.bfloat16), do_parts[part])
                dk_part = dot_nn(score_grad, q_parts[part])
                dv = dv_part if dv is None else dv + dv_part
                dk = dk_part if dk is None else dk + dk_part
                dq.append(
                    dot_nn(turned[part * HEAD_DIM : (part + 1) * HEAD_DIM, :], score_grad)
                )
            dv_slots[index] = dv
            dk_slots[index] = dk
            dq_slots[index] = jnp.concatenate(dq, axis=0)
            for place, work in side_work.items():
                pl.when(index == place)(work)
            return 0

        lax.fori_loop(0, SLOTS, one_slot, 0)

        def summed(slots, start, frame):
            total = slots[table[start + 4 * frame]]
            for way in range(1, 4):
                total = total + slots[table[start + 4 * frame + way]]
            return total

        def combine(frame):
            dq = summed(dq_slots, 2 * SLOTS, frame).T * 0.125
            qkv_send[frame, 0] = dq.astype(jnp.bfloat16)
            dk = summed(dk_slots, 2 * SLOTS + 4 * frames, frame)
            qkv_send[frame, 1] = dk.astype(jnp.bfloat16)
            dv = summed(dv_slots, 2 * SLOTS + 4 * frames, frame)
            qkv_send[frame, 2] = dv.astype(jnp.bfloat16)

        def qkv_copy(flips):
            peer = peer_head(head, flips)
            return remote(
                qkv_send.at[peer],
                back.at[:, :, own_lanes],
                a2a_send.at[2, flips],
                a2a_recv.at[2, flips],
                (group, peer),
            )

        def combine_loop(frame, _):
            combine(frame)
            return 0

        lax.fori_loop(0, frames, combine_loop, 0)
        for flips in others:
            qkv_copy(flips).start()
        back[:, :, own_lanes] = qkv_send[head]

        produce(8, out_right)
        take_second(4)
        take_first(5)
        take_core(8, out_right)
        take_dp(3)
        for copy in qkv_loads:
            copy.wait()
        for flips in others:
            qkv_copy(flips).wait()

        def rope_back(chunk, _):
            lanes = pl.ds(pl.multiple_of(chunk * 128, 128), 128)
            cosine = mod_ref[6:7, lanes]
            sine = mod_ref[7:8, lanes]
            for place, target in ((0, dq_raw), (1, dk_raw)):
                value = back[place, :, lanes].astype(jnp.float32)
                target[:, lanes] = (value * cosine + turn_pairs(value, lanes) * sine).astype(
                    jnp.bfloat16
                )
            return 0

        lax.fori_loop(0, width // 128, rope_back, 0)

        def value_right(chunk):
            return back[2, :, lane_block(chunk)]

        def query_right(chunk):
            return dq_raw[:, lane_block(chunk)]

        def key_right(chunk):
            return dk_raw[:, lane_block(chunk)]

        rights = {9: value_right, 10: query_right, 11: key_right}
        produce(9, value_right)
        produce(10, query_right)
        take_core(9, value_right)
        take_core(10, query_right)
        produce(11, key_right)
        take_core(11, key_right)

        def to_first(chunk, _):
            lanes = lane_block(chunk)
            ba[:, lanes] = (
                dot_nt(dq_raw[...], wqkv[0, lanes, :])
                + dot_nt(dk_raw[...], wqkv[1, lanes, :])
                + dot_nt(back[2], wqkv[2, lanes, :])
            )
            return 0

        lax.fori_loop(0, chunks, to_first, 0)

        def first_norm_back(index, sums):
            shift_sum, scale_sum = sums
            rows = row_block(index)
            value = x_ref[rows, :].astype(jnp.float32)
            scale = lax.rsqrt(jnp.mean(value * value, axis=1, keepdims=True) + EPSILON)
            normed = value * scale
            grad = ba[rows, :]
            shift_sum = shift_sum + jnp.sum(grad, axis=0, keepdims=True)
            scale_sum = scale_sum + jnp.sum(grad * normed, axis=0, keepdims=True)
            inner = grad * (1.0 + scale_one)
            mean = jnp.mean(inner * normed, axis=1, keepdims=True)
            gin_ref[rows, :] = mid[rows, :] + scale * (inner - normed * mean)
            return shift_sum, scale_sum

        shift_one_grad, scale_one_grad = lax.fori_loop(
            0, steps, first_norm_back, (row_zero, row_zero)
        )
        vectors = jnp.concatenate(
            [
                cond_ref[...].astype(jnp.float32),
                shift_one_grad,
                scale_one_grad,
                *saved_rows,
                row_zero,
            ],
            axis=0,
        )
        rows_ref[group, ybit, xbit, core] = vectors.astype(jnp.bfloat16)

    pl.run_scoped(
        attention_part,
        pltpu.VMEM((3, width, width), jnp.bfloat16),
        pltpu.VMEM((SLOTS + 1, 128, tokens), jnp.float32),
        pltpu.VMEM((SLOTS + 1, tokens, 128), jnp.float32),
        pltpu.VMEM((SLOTS + 1, tokens, 128), jnp.float32),
        pltpu.VMEM((frames, 3, tokens, 128), jnp.bfloat16),
        pltpu.VMEM((tokens, width), jnp.bfloat16),
        pltpu.VMEM((tokens, width), jnp.bfloat16),
        pltpu.VMEM((frames, 2, tokens), jnp.float32),
    )

    mine = rows_ref.at[group, ybit, xbit, core]
    row_dp = [
        remote(mine, mine, row_dp_send.at[hop], row_dp_recv.at[hop], (dp_peers[hop], head))
        for hop in range(n_dp - 1)
    ]
    y_part = rows_ref.at[:, ybit, xbit, core]
    x_part = rows_ref.at[:, :, xbit, core]
    core_part = rows_ref.at[:, :, :, core]
    row_y = remote(y_part, y_part, row_send.at[0], row_recv.at[0], (group, y_peer))
    row_x = remote(x_part, x_part, row_send.at[1], row_recv.at[1], (group, x_peer))
    row_core = remote(core_part, core_part, row_send.at[2], row_recv.at[2], (group, core_peer))
    for copy in row_dp:
        copy.start()

    take_first(6)
    take_second(5)
    take_dp(4)
    for copy in row_dp:
        copy.wait()
    row_y.start()
    take_first(7)
    take_second(6)
    take_dp(5)
    row_y.wait()
    row_x.start()
    take_first(8)
    take_second(7)
    take_dp(6)
    row_x.wait()
    row_core.start()
    take_first(9)
    take_second(8)
    take_dp(7)
    row_core.wait()
    take_first(10)
    take_second(9)
    take_dp(8)
    take_first(11)
    take_second(10)
    take_dp(9)
    take_second(11)
    take_dp(10)
    take_dp(11)
    core_copy(count - 2).wait_send()
    core_copy(count - 1).wait_send()


def back_part(n_dp, table, attended, queries, keys, values, lse, bias, hidden, cotangent, normed,
              modulation, cond_act, valid, weights):
    tokens, width = hidden.shape
    frames = attended.shape[0] // tokens
    hidden_width = weights[1].shape[1]
    devices = n_dp * 8
    small, large = width // devices, hidden_width // devices
    first_up = large // small
    tiles = hidden_width // width
    units = first_up + tiles + 4
    slots = units - 3
    dma = pltpu.SemaphoreType.DMA
    f32, bf16 = jnp.float32, jnp.bfloat16
    shape = jax.ShapeDtypeStruct
    return pl.pallas_call(
        lambda *refs: back_kernel(n_dp, *refs),
        out_shape=(
            shape((tokens, width), bf16),
            shape((tokens, width), f32),
            shape((8, 128), f32),
            *[shape((small, width), f32)] * 4,
            shape((small, hidden_width), f32),
            shape((large, width), f32),
            shape((n_dp, 2, 2, 2, 8, width), bf16),
        ),
        in_specs=[IN_SMEM] + [IN_VMEM] * 12 + [IN_PLACE] * 6,
        out_specs=tuple([IN_VMEM] * 10),
        scratch_shapes=[
            pltpu.VMEM((tokens, width), bf16),
            pltpu.VMEM((frames, tokens, 128), bf16),
            pltpu.VMEM((3, tokens, width), bf16),
            pltpu.VMEM((slots, n_dp, 2, 2, small, width), bf16),
            pltpu.VMEM((slots, n_dp, 2, small, width), bf16),
            pltpu.VMEM((slots, n_dp, small, width), bf16),
            pltpu.VMEM((units, n_dp - 1, small, width), bf16),
            pltpu.VMEM((2, n_dp, 2, 2, small, width), bf16),
            pltpu.VMEM((tokens, width), bf16),
            pltpu.VMEM((first_up + 3, 2, width // 2, tokens), bf16),
            pltpu.VMEM((tokens, width), bf16),
            pltpu.VMEM((tokens, width), bf16),
            pltpu.VMEM((tokens, hidden_width), bf16),
            pltpu.VMEM((tokens, width), bf16),
            pltpu.VMEM((tokens, width), f32),
            pltpu.VMEM((tokens, width), f32),
            pltpu.VMEM((width, width), bf16),
            dma((1 + 2 * tiles + 3,)),
            dma((3, 8)),
            dma((3, 8)),
            *[dma((units,))] * 6,
            dma((units, n_dp - 1)),
            dma((units, n_dp - 1)),
            dma((3,)),
            dma((3,)),
            dma((n_dp - 1,)),
            dma((n_dp - 1,)),
        ],
        compiler_params=pltpu.CompilerParams(
            collective_id=0, has_side_effects=True, vmem_limit_bytes=67043328
        ),
        name="back_part",
    )(
        table,
        attended,
        *[array.reshape(frames, tokens, 128) for array in (queries, keys, values)],
        lse,
        bias.reshape(frames, tokens, 128),
        hidden,
        cotangent,
        normed,
        modulation,
        cond_act,
        valid,
        *weights,
    )


def slot_table(first, frames):
    pair = jnp.arange(4 * frames, dtype=jnp.int32)
    frame, back = pair // 4, pair % 4
    held = (frame - back) >= jnp.repeat(first, 4)
    rank = jnp.sum((held[None, :] & (pair[None, :] < pair[:, None])).astype(jnp.int32), axis=1)
    slot = jnp.where(held, rank, SLOTS)
    hit = slot[None, :] == jnp.arange(SLOTS, dtype=jnp.int32)[:, None]
    query = jnp.sum(jnp.where(hit, frame[None, :], 0), axis=1)
    key = jnp.sum(jnp.where(hit, (frame - back)[None, :], 0), axis=1)
    grid = slot.reshape(frames, 4)
    columns = [
        jnp.concatenate([grid[way:, way], jnp.full((way,), SLOTS, jnp.int32)]) for way in range(4)
    ]
    same = (query == key).astype(jnp.int32)
    return jnp.concatenate([query, key, slot, jnp.stack(columns, axis=1).reshape(-1), same])


def per_device(
    hidden_in,
    frame_cond,
    query_weight,
    key_weight,
    value_weight,
    output_weight,
    up_weight,
    down_weight,
    modulation_weight,
    clip_lengths,
    patch_valid,
    cotangent,
):
    tok_dev, model_width = hidden_in.shape
    frames_dev = frame_cond.shape[0]
    group_tokens = patch_valid.shape[0]
    head_index = lax.axis_index("head")
    clip_of, frame_of, position = group_layout(clip_lengths[0], group_tokens, PATCHES)
    local_start = head_index * tok_dev
    local_position = lax.dynamic_slice_in_dim(position, local_start, tok_dev)
    local_valid = (
        lax.dynamic_slice_in_dim(patch_valid, local_start, tok_dev)
        .astype(jnp.float32)
        .reshape(frames_dev, PATCHES)
    )
    angles = local_position.astype(jnp.float32)[:, None] * frequencies(HEAD_DIM // 2)[None, :]
    cond_value = frame_cond.astype(jnp.float32)
    cond_act = jax.nn.silu(cond_value).astype(jnp.bfloat16)
    modulation = jnp.dot(cond_act, modulation_weight, preferred_element_type=jnp.float32).reshape(
        frames_dev, 1, 6 * model_width
    )
    shift_one, scale_one, gate_one, shift_two, scale_two, gate_two = jnp.split(
        modulation, 6, axis=2
    )
    tokens = hidden_in.astype(jnp.float32).reshape(frames_dev, PATCHES, model_width)
    normed_one = (
        modulate(tokens, shift_one, scale_one).astype(jnp.bfloat16).reshape(tok_dev, model_width)
    )
    query_raw = jnp.dot(normed_one, query_weight, preferred_element_type=jnp.float32)
    key_raw = jnp.dot(normed_one, key_weight, preferred_element_type=jnp.float32)
    query_send = (
        rotate(query_raw.reshape(tok_dev, HEADS, HEAD_DIM), angles)
        .reshape(tok_dev, model_width)
        .astype(jnp.bfloat16)
    )
    key_send = (
        rotate(key_raw.reshape(tok_dev, HEADS, HEAD_DIM), angles)
        .reshape(tok_dev, model_width)
        .astype(jnp.bfloat16)
    )
    value_send = jnp.dot(normed_one, value_weight, preferred_element_type=jnp.float32).astype(
        jnp.bfloat16
    )
    head_query, head_key, head_value = (
        lax.all_to_all(query_send, "head", split_axis=1, concat_axis=0, tiled=True),
        lax.all_to_all(key_send, "head", split_axis=1, concat_axis=0, tiled=True),
        lax.all_to_all(value_send, "head", split_axis=1, concat_axis=0, tiled=True),
    )
    first_frames = (frame_of - position)[::PATCHES]
    bias = jnp.broadcast_to(
        jnp.where(patch_valid == 1, 0.0, MASKED).astype(jnp.float32)[:, None],
        (group_tokens, 128),
    )
    attended_send, logsum = attend_forward(first_frames, head_query, head_key, head_value, bias)
    n_dp = lax.axis_size("dp")
    row_angles = angles[0]
    cosine, sine = jnp.cos(row_angles), jnp.sin(row_angles)
    table_rows = jnp.concatenate(
        [
            modulation.reshape(6, model_width),
            jnp.tile(jnp.concatenate([cosine, cosine]), HEADS)[None],
            jnp.tile(jnp.concatenate([sine, -sine]), HEADS)[None],
        ],
        axis=0,
    )
    (
        block_out,
        grad_input,
        statistics,
        grad_query,
        grad_key,
        grad_value,
        grad_output,
        grad_up,
        grad_down,
        gathered,
    ) = back_part(
        n_dp,
        slot_table(first_frames, group_tokens // PATCHES),
        attended_send,
        head_query,
        head_key,
        head_value,
        logsum,
        bias,
        hidden_in,
        cotangent,
        normed_one,
        table_rows,
        cond_act,
        jnp.broadcast_to(local_valid.reshape(tok_dev, 1), (tok_dev, 128)),
        (output_weight, up_weight, down_weight, query_weight, key_weight, value_weight),
    )
    device = lax.axis_index("dp") * lax.axis_size("head") + head_index
    gathered = gathered.reshape(n_dp * 8, 8, model_width)
    share = model_width // (n_dp * 8)
    dmod_all = gathered[:, 1:7].reshape(n_dp * 8, 6 * model_width)
    grad_modulation = inner_rows(
        lax.dynamic_slice_in_dim(gathered[:, 0], device * share, share, 1), dmod_all
    )
    modulation_grad = lax.dynamic_slice_in_dim(dmod_all, device, 1, 0)
    cond_act_grad = times_transposed(modulation_grad, modulation_weight)
    grad_cond = jax.vjp(jax.nn.silu, cond_value)[1](cond_act_grad)[0]
    return (
        block_out,
        grad_input,
        grad_cond,
        grad_query,
        grad_key,
        grad_value,
        grad_output,
        grad_up,
        grad_down,
        grad_modulation,
        statistics[:1, :3],
    )


def solution(mesh):
    in_specs = (
        P(("dp", "head"), None),
        P(("dp", "head"), None),
        P(),
        P(),
        P(),
        P(),
        P(),
        P(),
        P(),
        P("dp", None),
        P("dp"),
        P(("dp", "head"), None),
    )
    out_specs = (
        P(("dp", "head"), None),
        P(("dp", "head"), None),
        P(("dp", "head"), None),
        P(("dp", "head"), None),
        P(("dp", "head"), None),
        P(("dp", "head"), None),
        P(("dp", "head"), None),
        P(("dp", "head"), None),
        P(("dp", "head"), None),
        P(("dp", "head"), None),
        P(("dp", "head"), None),
    )
    return jax.shard_map(
        per_device, mesh=mesh, in_specs=in_specs, out_specs=out_specs, check_vma=False
    )
```

time: 364 us -> 297 us (0.82); the launches traced: 356 us -> 296 us
  matrix products: 86.8 us -> 23.8 us
  Pallas kernels: 157 us -> 208 us
  starting transfers between devices: 33 us -> 12.4 us
  waiting for transfers between devices: 30.9 us -> 20.2 us
  other arithmetic: 14.1 us -> 6.21 us
  local copies, waits for them, and re-layouts: 30.9 us -> 24.1 us
    pallas_call x2 -> x1, Pallas kernels: 144 us -> 196 us  [back_part(): pl.pallas_call(lambda *refs: back_kernel(n_dp, *refs), out_shape=(shape((...]
    dot_general x7 -> x1, matrix products: 26.8 us -> 1.18 us  [inner_rows(): lax.dot_general(left, right, (((0,), (0,)), ((), ())), preferred_element_...]
    dot_general x7 -> x1, matrix products: 29.4 us -> 8.64 us  [times_transposed(): lax.dot_general(left, right, (((1,), (1,)), ((), ())), preferred_element_...]
    all_to_all x5 -> x0, starting transfers between devices: 19.5 us -> none  [the longest x1 4.43 us: per_device(): lax.all_to_all(value_grad, 'head', split_axis=0, concat_axis=1, tiled=True)]
    dot_general x3 -> x0, matrix products: 16.5 us -> none  [the longest x1 8.18 us: per_device(): hidden = jnp.dot(normed_two, up_weight, preferred_element_type=jnp.float32)]
    all_to_all x5 -> x0, waiting for transfers between devices: 14 us -> none  [the longest x1 9.6 us: per_device(): lax.all_to_all(attended_send, 'head', split_axis=0, concat_axis=1, tiled=...]
    all_to_all x5 -> x0, local copies, waits for them, and re-layouts: 8.11 us -> none  [the longest x1 2.13 us: per_device(): lax.all_to_all(query_grad, 'head', split_axis=0, concat_axis=1, tiled=True)]
    all_to_all x1, waiting for transfers between devices: 0.01 us -> 7.21 us  [per_device(): lax.all_to_all(value_send, 'head', split_axis=1, concat_axis=0, tiled=True)]
  transfers between devices with their start and end apart: 8 -> 3, of which waited for: 6 -> 3; matrix products, arithmetic and copies ran while one was open for 16% -> 3% of each run, Pallas kernels for 0% -> 0%
where the time goes in v2:
time: 297 us; the launch traced here: 296 us
  Pallas kernels  208 us (70%)
  local copies, waits for them, and re-layouts  24.1 us (8%)
  matrix products  23.8 us (8%)
  waiting for transfers between devices  20.2 us (7%)
  starting transfers between devices  12.4 us (4%)
  other arithmetic  6.21 us (2%)
    pallas_call x1, Pallas kernels, back_part(): pl.pallas_call(lambda *refs: back_kernel(n_dp, *refs), out_shape=(shape((...  196 us
    pallas_call x1, Pallas kernels, attend_forward(): pl.pallas_call(attend_forward_kernel, out_shape=(jax.ShapeDtypeStruct((to...  12.6 us
    unnamed x47, local copies, waits for them, and re-layouts  11.7 us
    dot_general x1, matrix products, times_transposed(): lax.dot_general(left, right, (((1,), (1,)), ((), ())), preferred_element_...  8.64 us
    all_to_all x1, waiting for transfers between devices, per_device(): lax.all_to_all(key_send, 'head', split_axis=1, concat_axis=0, tiled=True)  8.34 us
    all_to_all x1, waiting for transfers between devices, per_device(): lax.all_to_all(value_send, 'head', split_axis=1, concat_axis=0, tiled=True)  7.21 us
    dot_general x1, matrix products, per_device(): jnp.dot(cond_act, modulation_weight, preferred_element_type=jnp.float32)  6.47 us
  transfers between devices with their start and end apart: 3, of which 3 were waited for; matrix products, arithmetic and copies ran while one was open for 3% of the time, Pallas kernels for 0%

profile of v2, /device:TPU:0, one launch (start us, length us, event | category | flops | bytes accessed | tf_op | source)
XLA Modules:
  0.0 295.9 jit_solution(15567742102631053597)
XLA Ops:
  0.7 0.8 reduce-window.4
  1.5 0.7 fusion.32
  2.2 6.5 %fusion.20 = f32[1,6144]{1,0:T(1,128)S(1)} fusion(bf16[1024,6144]{1,0:T(8,128)(2,1)} %param.20, bf16[1,1024]{1,0:T(2,128)(2,1)} %param.13), kind=kOutput, calls=%fused_computation.57 | convolution fusion | flops 12589056 | bytes 12609536 | tf_op jit(solution)/shard_map/dot_general | solution.py:1066
  8.7 0.2 fusion
  8.9 2.6 copy.69
  11.4 2.9 copy.67
  14.3 0.2 fusion.3.refs_9_
  14.5 3.5 %fusion.4 = f32[256,16,64]{0,2,1:T(8,128)} fusion(bf16[16,64,1024]{2,1,0:T(8,128)(2,1)} %bitcast.66, bf16[256,1024]{1,0:T(8,128)(2,1)S(1)} %fusion.3.refs_9_), kind=kOutput, calls=%fused_computation.9 | convolution fusion | flops 536870912 | bytes 3670016 | tf_op jit(solution)/shard_map/dot_general | solution.py:1077
  18.0 1.7 fusion.6
  19.8 0.1 convert_reduce_fusion
  19.9 0.1 select_reduce_fusion
  20.0 0.1 fusion.30
  20.0 0.2 broadcast_multiply_fusion
  20.2 1.9 subtract_convert_fusion
  22.1 0.1 pad_maximum_fusion
  22.2 1.0 copy.68
  23.2 5.2 %all-to-all-start = ((bf16[256,8,128]{2,0,1:T(8,128)(2,1)}), bf16[256,8,128]{2,0,1:T(8,128)(2,1)S(1)}, u32[]{:S(2)}, u32[]{:S(2)}) async-start(bf16[256,8,128]{2,0,1:T(8,128)(2,1)} %copy.68), calls=%async_computation | async-start | bytes 1048576 | tf_op jit(solution)/shard_map/all_to_all | solution.py:1092
  28.4 0.1 slice.39.first_ref
  28.6 0.1 reshape.233
  28.7 0.1 convert_reduce_fusion.1
  28.9 0.1 fusion.27
  28.9 0.2 slice_reduce_fusion.2
  29.1 0.2 slice_reduce_fusion.1
  29.3 0.2 slice_reduce_fusion
  29.5 0.1 select_reduce_fusion.1
  29.7 1.0 copy.70
  30.7 0.1 copy.64
  30.8 0.1 copy.65
  30.9 0.1 copy.66
  31.0 0.2 cosine_reduce_fusion
  31.2 2.3 convolution_convert_fusion
  33.5 4.6 %all-to-all-done = bf16[256,8,128]{2,0,1:T(8,128)(2,1)S(1)} async-done(((bf16[256,8,128]{2,0,1:T(8,128)(2,1)}), bf16[256,8,128]{2,0,1:T(8,128)(2,1)S(1)}, u32[]{:S(2)}, u32[]{:S(2)}) %all-to-all-start) | async-done | bytes 524320 | tf_op jit(solution)/shard_map/all_to_all | solution.py:1092
  38.1 3.5 %all-to-all-start.1 = ((bf16[256,8,128]{2,0,1:T(8,128)(2,1)}), bf16[256,8,128]{2,0,1:T(8,128)(2,1)S(1)}, u32[]{:S(2)}, u32[]{:S(2)}) async-start(bf16[256,8,128]{2,0,1:T(8,128)(2,1)} %copy.70), calls=%async_computation.1 | async-start | bytes 1048576 | tf_op jit(solution)/shard_map/all_to_all | solution.py:1093
  41.7 0.2 copy.71
  41.9 1.0 copy.72
  42.9 8.3 %all-to-all-done.1 = bf16[256,8,128]{2,0,1:T(8,128)(2,1)S(1)} async-done(((bf16[256,8,128]{2,0,1:T(8,128)(2,1)}), bf16[256,8,128]{2,0,1:T(8,128)(2,1)S(1)}, u32[]{:S(2)}, u32[]{:S(2)}) %all-to-all-start.1) | async-done | bytes 524320 | tf_op jit(solution)/shard_map/all_to_all | solution.py:1093
  51.3 3.7 %all-to-all-start.2 = ((bf16[256,8,128]{2,0,1:T(8,128)(2,1)}), bf16[256,8,128]{2,0,1:T(8,128)(2,1)S(1)}, u32[]{:S(2)}, u32[]{:S(2)}) async-start(bf16[256,8,128]{2,0,1:T(8,128)(2,1)} %copy.72), calls=%async_computation.2 | async-start | bytes 1048576 | tf_op jit(solution)/shard_map/all_to_all | solution.py:1094
  55.0 0.1 reshape.234
  55.1 0.1 broadcast_in_dim_tile.6
  55.2 0.1 broadcast_in_dim_tile.7
  55.3 0.6 concatenate.32.refs_0_
  56.0 0.6 pad_maximum_fusion.2.refs_10_
  56.6 0.6 multiply_convert_fusion.refs_11_
  57.2 7.2 %all-to-all-done.2 = bf16[256,8,128]{2,0,1:T(8,128)(2,1)S(1)} async-done(((bf16[256,8,128]{2,0,1:T(8,128)(2,1)}), bf16[256,8,128]{2,0,1:T(8,128)(2,1)S(1)}, u32[]{:S(2)}, u32[]{:S(2)}) %all-to-all-start.2) | async-done | bytes 524320 | tf_op jit(solution)/shard_map/all_to_all | solution.py:1094
  64.4 1.3 broadcast_in_dim.94.bias_ref
  65.7 12.6 %attend_forward.1 = (bf16[2048,128]{1,0:T(8,128)(2,1)}, f32[8,2,256]{2,1,0:T(2,128)}) custom-call(s32[8]{0:T(128)} %copy-done.17, bf16[2048,128]{1,0:T(8,128)(2,1)} %bitcast.67, bf16[2048,128]{1,0:T(8,128)(2,1)} %bitcast.69, bf16[2048,128]{1,0:T(8,128)(2,1)} %bitcast.71, f32[2048,128]{1,0:T(8,128)} %broadcast_in_dim.94.bias_ref), custom_call_target="tpu_custom_call" | custom-call | tf_op jit(solution)/shard_map/attend_forward/pallas_call | solution.py:160
  78.3 0.8 broadcast_in_dim.97.refs_12_
  79.0 1.3 broadcast_in_dim.96.refs_6_
  80.4 195.8 %back_part.1 = (bf16[256,1024]{1,0:T(8,128)(2,1)}, f32[256,1024]{1,0:T(8,128)}, f32[8,128]{1,0:T(8,128)}, f32[32,1024]{1,0:T(8,128)}, f32[32,1024]{1,0:T(8,128)}...) custom-call(s32[115]{0:T(128)} %concatenate.32.refs_0_, ...), custom_call_target="tpu_custom_call" | custom-call | tf_op jit(solution)/shard_map/back_part/pallas_call | solution.py:958
  276.2 1.2 slice.57
  277.4 1.1 slice.58
  278.5 0.2 copy.76
  278.7 0.1 constant_dynamic-slice_fusion
  278.8 1.2 fusion.14
  280.0 8.6 %fusion.19 = f32[1,1024]{1,0:T(1,128)} fusion(bf16[1024,6144]{1,0:T(8,128)(2,1)} %param.20, bf16[32,6144]{1,0:T(8,128)(2,1)S(1)} %bitcast.78, s32[]{:T(128)S(6)} %select_n.106, bf16[1,1024]{1,0:T(2,128)(2,1)S(1)} %copy-done.15), kind=kOutput, calls=%fused_computation.54 | convolution fusion | flops 12593152 | bytes 12615684 | tf_op jit(solution)/shard_map/dot_general | solution.py:60
  288.7 1.3 slice.51
  289.9 0.8 copy.87
  290.7 1.0 copy.88
  291.7 0.7 copy.89
  292.3 0.7 copy.90
  293.0 0.7 copy.91
  293.7 0.7 copy.92
  294.3 0.8 copy.93
  295.1 0.8 copy.94
  (58 shorter events, 0.6 us)
Async XLA Ops:
  2.2 6.5 %copy-start.2 = (bf16[256,1024]{1,0:T(8,128)(2,1)S(1)}, bf16[256,1024]{1,0:T(8,128)(2,1)}, u32[]{:S(2)}) copy-start(bf16[256,1024]{1,0:T(8,128)(2,1)} %refs_7_.1) | copy-start | bytes 1572868
  2.2 6.7 %copy-start.1 = (bf16[1024,1024]{1,0:T(8,128)(2,1)S(1)}, bf16[1024,1024]{1,0:T(8,128)(2,1)}, u32[]{:S(2)}) copy-start(bf16[1024,1024]{1,0:T(8,128)(2,1)} %refs_17_.1) | copy-start | bytes 6291460
  14.5 16.6 %copy-start = (bf16[256,1024]{1,0:T(8,128)(2,1)}, bf16[256,1024]{1,0:T(8,128)(2,1)S(1)}, u32[]{:S(2)}) copy-start(bf16[256,1024]{1,0:T(8,128)(2,1)S(1)} %fusion.3.refs_9_) | copy-start | bytes 1572868
  23.2 14.9 %all-to-all-start = ((bf16[256,8,128]{2,0,1:T(8,128)(2,1)}), bf16[256,8,128]{2,0,1:T(8,128)(2,1)S(1)}, u32[]{:S(2)}, u32[]{:S(2)}) async-start(bf16[256,8,128]{2,0,1:T(8,128)(2,1)} %copy.68), calls=%async_computation | async-start | bytes 1048576 | tf_op jit(solution)/shard_map/all_to_all | solution.py:1092
  28.5 5.0 %copy-start.17 = (s32[8]{0:T(128)}, s32[8]{0:T(128)S(1)}, u32[]{:S(2)}) copy-start(s32[8]{0:T(128)S(1)} %slice.39.first_ref) | copy-start | bytes 100
  33.5 9.4 %copy-start.16 = (s32[2048]{0:T(1024)S(1)}, s32[2048]{0:T(1024)}, u32[]{:S(2)}) copy-start(s32[2048]{0:T(1024)} %param.22) | copy-start | bytes 24580
  33.5 23.1 %copy-start.14 = (bf16[1,1024]{1,0:T(2,128)(2,1)S(1)}, bf16[1,1024]{1,0:T(2,128)(2,1)}, u32[]{:S(2)}) copy-start(bf16[1,1024]{1,0:T(2,128)(2,1)} %param.13) | copy-start | bytes 6148
  38.1 13.2 %copy-start.3 = (bf16[256,8,128]{2,0,1:T(8,128)(2,1)}, bf16[256,8,128]{2,0,1:T(8,128)(2,1)S(1)}, u32[]{:S(2)}) copy-start(bf16[256,8,128]{2,0,1:T(8,128)(2,1)S(1)} %all-to-all-done) | copy-start | bytes 1572868
  38.1 13.2 %all-to-all-start.1 = ((bf16[256,8,128]{2,0,1:T(8,128)(2,1)}), bf16[256,8,128]{2,0,1:T(8,128)(2,1)S(1)}, u32[]{:S(2)}, u32[]{:S(2)}) async-start(bf16[256,8,128]{2,0,1:T(8,128)(2,1)} %copy.70), calls=%async_computation.1 | async-start | bytes 1048576 | tf_op jit(solution)/shard_map/all_to_all | solution.py:1093
  51.3 14.5 %copy-start.4 = (bf16[256,8,128]{2,0,1:T(8,128)(2,1)}, bf16[256,8,128]{2,0,1:T(8,128)(2,1)S(1)}, u32[]{:S(2)}) copy-start(bf16[256,8,128]{2,0,1:T(8,128)(2,1)S(1)} %all-to-all-done.1) | copy-start | bytes 1572868
  51.3 13.2 %all-to-all-start.2 = ((bf16[256,8,128]{2,0,1:T(8,128)(2,1)}), bf16[256,8,128]{2,0,1:T(8,128)(2,1)S(1)}, u32[]{:S(2)}, u32[]{:S(2)}) async-start(bf16[256,8,128]{2,0,1:T(8,128)(2,1)} %copy.72), calls=%async_computation.2 | async-start | bytes 1048576 | tf_op jit(solution)/shard_map/all_to_all | solution.py:1094
  64.4 1.3 copy-start.5
  276.2 3.8 %copy-start.15 = (bf16[1,1024]{1,0:T(2,128)(2,1)S(1)}, bf16[1,1024]{1,0:T(2,128)(2,1)}, u32[]{:S(2)}) copy-start(bf16[1,1024]{1,0:T(2,128)(2,1)} %param.13) | copy-start | bytes 6148
  280.0 9.9 %copy-start.9 = (bf16[256,1024]{1,0:T(8,128)(2,1)S(1)}, bf16[256,1024]{1,0:T(8,128)(2,1)}, u32[]{:S(2)}) copy-start(bf16[256,1024]{1,0:T(8,128)(2,1)} %get-tuple-element.67) | copy-start | bytes 1572868
  280.0 10.7 %copy-start.6 = (f32[256,1024]{1,0:T(8,128)S(1)}, f32[256,1024]{1,0:T(8,128)}, u32[]{:S(2)}) copy-start(f32[256,1024]{1,0:T(8,128)} %get-tuple-element.68) | copy-start | bytes 3145732
  288.6 3.0 %copy-start.13 = (f32[32,1024]{1,0:T(8,128)S(1)}, f32[32,1024]{1,0:T(8,128)}, u32[]{:S(2)}) copy-start(f32[32,1024]{1,0:T(8,128)} %get-tuple-element.70) | copy-start | bytes 393220
  288.6 3.7 %copy-start.12 = (f32[32,1024]{1,0:T(8,128)S(1)}, f32[32,1024]{1,0:T(8,128)}, u32[]{:S(2)}) copy-start(f32[32,1024]{1,0:T(8,128)} %get-tuple-element.71) | copy-start | bytes 393220
  288.7 4.4 %copy-start.11 = (f32[32,1024]{1,0:T(8,128)S(1)}, f32[32,1024]{1,0:T(8,128)}, u32[]{:S(2)}) copy-start(f32[32,1024]{1,0:T(8,128)} %get-tuple-element.72) | copy-start | bytes 393220
  288.7 5.0 %copy-start.10 = (f32[32,1024]{1,0:T(8,128)S(1)}, f32[32,1024]{1,0:T(8,128)}, u32[]{:S(2)}) copy-start(f32[32,1024]{1,0:T(8,128)} %get-tuple-element.73) | copy-start | bytes 393220
  289.9 4.4 %copy-start.8 = (f32[32,4096]{1,0:T(8,128)S(1)}, f32[32,4096]{1,0:T(8,128)}, u32[]{:S(2)}) copy-start(f32[32,4096]{1,0:T(8,128)} %get-tuple-element.74) | copy-start | bytes 1572868
  290.7 4.4 %copy-start.7 = (f32[128,1024]{1,0:T(8,128)S(1)}, f32[128,1024]{1,0:T(8,128)}, u32[]{:S(2)}) copy-start(f32[128,1024]{1,0:T(8,128)} %get-tuple-element.75) | copy-start | bytes 1572868

commit v3 on v2

--- a/solution.py
+++ b/solution.py
@@ -16,55 +16,8 @@
 MASKED = -1e30
 
 
-def rms_normed(values):
-    return values * lax.rsqrt(jnp.mean(values * values, axis=-1, keepdims=True) + EPSILON)
-
-
-def modulate(values, shift, scaling):
-    return rms_normed(values) * (1.0 + scaling) + shift
-
-
 def frequencies(half_dim):
     return jnp.exp(jnp.arange(half_dim, dtype=jnp.float32) * (-math.log(10000.0) / half_dim))
-
-
-def rotate(values, angles):
-    half_dim = values.shape[-1] // 2
-    cosine = jnp.cos(angles)[:, None, :]
-    sine_part = jnp.sin(angles)[:, None, :]
-    first_half = values[..., :half_dim]
-    second = values[..., half_dim:]
-    return jnp.concatenate(
-        [first_half * cosine - second * sine_part, first_half * sine_part + second * cosine],
-        axis=-1,
-    )
-
-
-def group_layout(lengths, token_count, patches):
-    frame_of = jnp.arange(token_count, dtype=jnp.int32) // patches
-    clip_ends = jnp.cumsum(lengths)
-    starts = clip_ends - lengths
-    clip_of = jnp.sum((frame_of[:, None] >= clip_ends[None, :]).astype(jnp.int32), axis=1)
-    picked = clip_of[:, None] == jnp.arange(lengths.shape[0], dtype=jnp.int32)[None, :]
-    position = frame_of - jnp.sum(jnp.where(picked, starts[None, :], 0), axis=1)
-    return (clip_of, frame_of, position)
-
-
-def inner_rows(left, right):
-    return lax.dot_general(
-        left, right, (((0,), (0,)), ((), ())), preferred_element_type=jnp.float32
-    )
-
-
-def times_transposed(left, right):
-    return lax.dot_general(
-        left, right, (((1,), (1,)), ((), ())), preferred_element_type=jnp.float32
-    )
-
-
-def frame_stats(values, valid_f):
-    sums = jnp.sum(values * values, axis=2) * valid_f
-    return jnp.sqrt(jnp.sum(sums, axis=1) / (values.shape[1] * values.shape[2]) + EPSILON)
 
 
 def dot_nt(left, right):
@@ -209,7 +162,7 @@
     return value * half, slope
 
 
-def turn_pairs(values, column):
+def turn_pairs(values, _):
     lane = lax.rem(lax.broadcasted_iota(jnp.int32, values.shape, 1), HEAD_DIM)
     up = pltpu.roll(values, 128 - HEAD_DIM // 2, 1)
     down = pltpu.roll(values, HEAD_DIM // 2, 1)
@@ -220,24 +173,26 @@
     (
         table,
         att_own,
-        q_ref,
-        k_ref,
-        v_ref,
         lse_ref,
-        bias_ref,
         x_ref,
         cot_ref,
-        n1_ref,
         mod_ref,
+        rope_ref,
         cond_ref,
         valid_ref,
+        q_hbm,
+        k_hbm,
+        v_hbm,
+        bias_hbm,
+        n1_hbm,
         wo_hbm,
         up_hbm,
         down_hbm,
         wq_hbm,
         wk_hbm,
         wv_hbm,
-        block_ref,
+        wmod_hbm,
+        block_hbm,
         gin_ref,
         stat_ref,
         gq_ref,
@@ -246,10 +201,11 @@
         go_ref,
         gup_ref,
         gdown_ref,
-        rows_ref,
+        gmod_hbm,
+        gcond_ref,
+        n1_all,
         att_fr,
         do_own,
-        back,
         from_core,
         from_first,
         from_second,
@@ -257,13 +213,15 @@
         core_out,
         da_send,
         lhs,
-        n2,
         dmlp,
         dhid,
         dattn,
-        ba,
         mid,
-        wo,
+        rows_ref,
+        z_send,
+        z_recv,
+        p_send,
+        p_recv,
         load_sem,
         a2a_send,
         a2a_recv,
@@ -279,9 +237,14 @@
         row_recv,
         row_dp_send,
         row_dp_recv,
+        gather_send,
+        gather_recv,
+        z_send_sem,
+        z_recv_sem,
+        mod_sem,
     ) = refs
     tokens, width = x_ref.shape
-    frames = q_ref.shape[0]
+    frames = q_hbm.shape[0]
     hidden_width = up_hbm.shape[1]
     tiles = hidden_width // width
     chunks = width // BLOCK
@@ -305,8 +268,6 @@
     for peer in dp_peers:
         pl.semaphore_signal(barrier, inc=1, device_id=(peer, head), device_id_type=MESH_ID)
 
-    wo_load = pltpu.make_async_copy(wo_hbm, wo, load_sem.at[0])
-    wo_load.start()
     pl.semaphore_wait(barrier, 7 + len(dp_peers))
 
     own_rows = pl.ds(head * tokens, tokens)
@@ -334,17 +295,15 @@
 
     first_up = large // small
     first_out = first_up + tiles
-    count = first_out + 4
+    count = first_out + 3
 
     def slot_of(unit):
-        return unit if unit < first_out + 1 else unit - first_out - 1
+        return unit
 
     def lhs_of(unit):
         if unit < first_up:
             return unit
-        if unit < first_out:
-            return first_up
-        return first_up + 1 if unit == first_out else first_up + 2
+        return first_up if unit < first_out else first_up + 1
 
     def core_copy(unit):
         return remote(
@@ -391,30 +350,46 @@
     def added(left, right):
         return (left.astype(jnp.float32) + right.astype(jnp.float32)).astype(jnp.bfloat16)
 
-    def produce(unit, right):
+    def put(target, lanes, value, unit):
+        value = value.astype(jnp.bfloat16)
+        if unit <= first_out:
+            target[:, :, :, :, lanes] = value.reshape(n_dp, 2, 2, small, BLOCK)
+        else:
+            value = value.reshape(4, n_dp, small, BLOCK)
+            for chip in range(4):
+                target[:, chip // 2, chip % 2, :, lanes] = value[chip]
+
+    def got(source, lanes, unit):
+        if unit <= first_out:
+            return source[:, :, :, :, lanes].reshape(half_rows, BLOCK)
+        return jnp.concatenate(
+            [
+                source[:, chip // 2, chip % 2, :, lanes].reshape(half_rows // 4, BLOCK)
+                for chip in range(4)
+            ],
+            axis=0,
+        )
+
+    def produce(unit, product):
         if unit >= 2:
             core_copy(unit - 2).wait_send()
-        left = lhs_of(unit)
 
         def body(chunk, _):
             lanes = pl.ds(pl.multiple_of(chunk * BLOCK, BLOCK), BLOCK)
-            value = dot_nn(lhs[left, 1 - core], right(chunk)).astype(jnp.bfloat16)
-            core_out[unit % 2, :, :, :, :, lanes] = value.reshape(n_dp, 2, 2, small, BLOCK)
+            put(core_out.at[unit % 2], lanes, product(unit, 1 - core, chunk), unit)
             return 0
 
         lax.fori_loop(0, chunks, body, 0)
         core_copy(unit).start()
 
-    def take_core(unit, right):
+    def take_core(unit, product):
         core_copy(unit).wait_recv()
-        left, slot = lhs_of(unit), slot_of(unit)
+        place = from_core.at[slot_of(unit)]
 
         def body(chunk, _):
             lanes = pl.ds(pl.multiple_of(chunk * BLOCK, BLOCK), BLOCK)
-            value = dot_nn(lhs[left, core], right(chunk))
-            came = from_core[slot, :, :, :, :, lanes].reshape(half_rows, BLOCK)
-            value = (value + came.astype(jnp.float32)).astype(jnp.bfloat16)
-            from_core[slot, :, :, :, :, lanes] = value.reshape(n_dp, 2, 2, small, BLOCK)
+            value = product(unit, core, chunk) + got(place, lanes, unit).astype(jnp.float32)
+            put(place, lanes, value, unit)
             return 0
 
         lax.fori_loop(0, chunks, body, 0)
@@ -462,7 +437,7 @@
             place = (unit - first_up) * width
             gup_ref[:, place : place + width] = total
         else:
-            (go_ref, gv_ref, gq_ref, gk_ref)[unit - first_out][...] = total
+            go_ref[...] = total
 
     def turned_rows(index, source):
         for chunk in range(chunks):
@@ -495,23 +470,57 @@
         att_copy(flips).start()
     att_fr[:, own_lanes] = att_own[own_rows, :]
 
-    def down_right(chunk):
-        return dmlp[:, lane_block(chunk)]
-
-    def up_right(unit):
-        def value(chunk):
+    def weight_product(unit, side, chunk):
+        if unit < first_up:
+            right = dmlp[:, lane_block(chunk)]
+        elif unit < first_out:
             start = (unit - first_up) * width + chunk * BLOCK
-            return dhid[:, pl.ds(pl.multiple_of(start, BLOCK), BLOCK)]
-
-        return value
-
-    def mlp_right(unit):
-        return down_right if unit < first_up else up_right(unit)
-
-    def out_right(chunk):
-        return dattn[:, lane_block(chunk)]
-
-    def mlp_part(up, down, act, dn2):
+            right = dhid[:, pl.ds(pl.multiple_of(start, BLOCK), BLOCK)]
+        else:
+            right = dattn[:, lane_block(chunk)]
+        return dot_nn(lhs[lhs_of(unit), side], right)
+
+    def run_plan(point, product=weight_product):
+        for kind, unit in PLAN.get(point, ()):
+            if kind == "P":
+                produce(unit, product)
+            elif kind == "C":
+                take_core(unit, product)
+            elif kind == "F":
+                take_first(unit)
+            elif kind == "S":
+                take_second(unit)
+            else:
+                take_dp(unit)
+
+    half = tokens // 2
+    low, high = pl.ds(0, half), pl.ds(half, half)
+
+    def gather_copy(index):
+        if index == 0:
+            source, target, peer = n1_hbm.at[low], n1_all.at[head, low], x_peer
+        elif index == 1:
+            source, target, peer = n1_hbm.at[high], n1_all.at[head, high], y_peer
+        elif index == 2:
+            source, target, peer = n1_hbm.at[low], n1_all.at[head, low], y_peer
+        elif index == 3:
+            source, target, peer = n1_all.at[x_peer, low], n1_all.at[x_peer, low], y_peer
+        elif index == 4:
+            source, target, peer = n1_hbm.at[high], n1_all.at[head, high], x_peer
+        elif index == 5:
+            source, target, peer = n1_all.at[y_peer, high], n1_all.at[y_peer, high], x_peer
+        elif index == 6:
+            source, target, peer = n1_hbm, n1_all.at[head], core_peer
+        else:
+            block = peer_head(head, 2 * (index - 6))
+            source, target, peer = n1_all.at[block], n1_all.at[block], core_peer
+        return remote(
+            source, target, gather_send.at[index], gather_recv.at[index], (group, peer)
+        )
+
+    def mlp_part(up, down, act, dn2, wo, ba, n2):
+        wo_load = pltpu.make_async_copy(wo_hbm, wo, load_sem.at[0])
+        wo_load.start()
         up_loads = [
             pltpu.make_async_copy(
                 up_hbm.at[:, pl.ds(tile * width, width)],
@@ -532,10 +541,11 @@
             up_loads[tile].start()
             down_loads[tile].start()
 
-        turned_rows(first_up + 2, n1_ref)
         wo_load.wait()
         for flips in others:
             att_copy(flips).wait()
+        for index in (0, 1, 6):
+            gather_copy(index).start()
         turned_rows(first_up + 1, att_fr)
 
         def project(chunk, _):
@@ -575,6 +585,13 @@
                     load_sem.at[1 + tiles + tile],
                 ).wait()
 
+            @pl.when(index == GATHER_AT)
+            def _():
+                for step in (0, 1):
+                    gather_copy(step).wait()
+                for step in (2, 3, 4, 5):
+                    gather_copy(step).start()
+
             lanes = lane_block(index)
             active, slope = gelu_and_slope(dot_nn(n2[...], up[:, lanes]))
             active = active.astype(jnp.bfloat16)
@@ -592,8 +609,7 @@
 
         lax.fori_loop(0, hidden_width // BLOCK, feed, 0)
 
-        produce(0, mlp_right(0))
-        produce(1, mlp_right(1))
+        run_plan("fed")
 
         def to_normed(chunk, _):
             lanes = lane_block(chunk)
@@ -601,8 +617,7 @@
             return 0
 
         lax.fori_loop(0, chunks, to_normed, 0)
-        take_core(0, mlp_right(0))
-        take_core(1, mlp_right(1))
+        run_plan("normed")
 
         def second_norm_back(index, sums):
             shift_sum, scale_sum, gate_sum = sums
@@ -635,8 +650,7 @@
             grad_copy(flips).start()
         do_own[head] = da_send[:, own_lanes]
 
-        produce(2, mlp_right(2))
-        produce(3, mlp_right(3))
+        run_plan("attended")
 
         def branch_out(chunk, _):
             lanes = lane_block(chunk)
@@ -644,8 +658,7 @@
             return 0
 
         lax.fori_loop(0, chunks, branch_out, 0)
-        take_core(2, mlp_right(2))
-        take_core(3, mlp_right(3))
+        run_plan("branch")
 
         def outputs(index, sums):
             gate_sum, stat_mlp, stat_out = sums
@@ -653,7 +666,7 @@
             raw = ba[rows, :]
             branch = gate_two * raw
             value = mid[rows, :] + branch
-            block_ref[rows, :] = value.astype(jnp.bfloat16)
+            n2[rows, :] = value.astype(jnp.bfloat16)
             gate_sum = gate_sum + jnp.sum(
                 cot_ref[rows, :].astype(jnp.float32) * raw, axis=0, keepdims=True
             )
@@ -673,8 +686,10 @@
             (6, gate_two_grad),
         ):
             gin_ref[row : row + 1, :] = vector
-        produce(4, mlp_right(4))
-        produce(5, mlp_right(5))
+        block_copy = pltpu.make_async_copy(n2, block_hbm, load_sem.at[0])
+        block_copy.start()
+        run_plan("outputs")
+        block_copy.wait()
 
     pl.run_scoped(
         mlp_part,
@@ -682,20 +697,74 @@
         pltpu.VMEM((hidden_width, width), jnp.bfloat16),
         pltpu.VMEM((tokens, hidden_width), jnp.bfloat16),
         pltpu.VMEM((tokens, width), jnp.float32),
+        pltpu.VMEM((width, width), jnp.bfloat16),
+        pltpu.VMEM((tokens, width), jnp.float32),
+        pltpu.VMEM((tokens, width), jnp.bfloat16),
     )
     saved_rows = [gin_ref[row : row + 1, :] for row in range(3, 7)]
 
-    def attention_part(wqkv, dq_slots, dk_slots, dv_slots, qkv_send, dq_raw, dk_raw, deltas):
-        qkv_loads = [
-            pltpu.make_async_copy(source, wqkv.at[place], load_sem.at[1 + 2 * tiles + place])
-            for place, source in enumerate((wq_hbm, wk_hbm, wv_hbm))
+    def attention_part(
+        q_ref,
+        k_ref,
+        v_ref,
+        bias_ref,
+        n1_group,
+        w_own,
+        dq_slots,
+        dk_slots,
+        dv_slots,
+        deltas,
+        d_all,
+        d_turned,
+        dn1,
+        cond_sum,
+    ):
+        pieces = [
+            (q_hbm, q_ref),
+            (k_hbm, k_ref),
+            (v_hbm, v_ref),
+            (bias_hbm, bias_ref),
+            (wq_hbm.at[:, own_lanes], w_own.at[:, pl.ds(0, 128)]),
+            (wk_hbm.at[:, own_lanes], w_own.at[:, pl.ds(128, 128)]),
+            (wv_hbm.at[:, own_lanes], w_own.at[:, pl.ds(256, 128)]),
         ]
-        for copy in qkv_loads:
+        loads = [
+            pltpu.make_async_copy(source, target, load_sem.at[1 + place])
+            for place, (source, target) in enumerate(pieces)
+        ]
+        for copy in loads:
             copy.start()
-        take_first(0)
-        take_first(1)
+
+        pages = frames // 2
+
+        class mod_load:
+            def __init__(self, block):
+                self.copies = [
+                    pltpu.make_async_copy(
+                        wmod_hbm.at[pl.ds(page * tokens, tokens), pl.ds(block * width, width)],
+                        n1_group.at[block % 2 * pages + page],
+                        mod_sem.at[block, page],
+                    )
+                    for page in range(pages)
+                ]
+
+            def start(self):
+                for copy in self.copies:
+                    copy.start()
+
+            def wait(self):
+                for copy in self.copies:
+                    copy.wait()
+
+        run_plan("scope")
+        for step in (2, 3, 4, 5):
+            gather_copy(step).wait()
+        for step in (7, 8, 9):
+            gather_copy(step).start()
         for flips in others:
             grad_copy(flips).wait()
+        for copy in loads:
+            copy.wait()
         for slots in (dq_slots, dk_slots, dv_slots):
             slots[SLOTS] = jnp.zeros(slots.shape[1:], jnp.float32)
 
@@ -711,25 +780,6 @@
             return 0
 
         lax.fori_loop(0, frames, frame_delta, 0)
-
-        side_work = {
-            1: lambda: take_core(4, mlp_right(4)),
-            2: lambda: take_core(5, mlp_right(5)),
-            3: lambda: produce(6, mlp_right(6)),
-            4: lambda: take_second(0),
-            5: lambda: take_second(1),
-            6: lambda: take_first(2),
-            7: lambda: take_first(3),
-            8: lambda: take_core(6, mlp_right(6)),
-            9: lambda: produce(7, mlp_right(7)),
-            10: lambda: take_dp(0),
-            11: lambda: take_dp(1),
-            12: lambda: take_second(2),
-            13: lambda: take_second(3),
-            14: lambda: take_first(4),
-            15: lambda: take_core(7, mlp_right(7)),
-            16: lambda: take_dp(2),
-        }
 
         def one_slot(index, _):
             frame = table[index]
@@ -763,8 +813,9 @@
             dv_slots[index] = dv
             dk_slots[index] = dk
             dq_slots[index] = jnp.concatenate(dq, axis=0)
-            for place, work in side_work.items():
-                pl.when(index == place)(work)
+            for place in range(SLOTS):
+                if PLAN.get(place):
+                    pl.when(index == place)(lambda place=place: run_plan(place))
             return 0
 
         lax.fori_loop(0, SLOTS, one_slot, 0)
@@ -775,83 +826,142 @@
                 total = total + slots[table[start + 4 * frame + way]]
             return total
 
-        def combine(frame):
-            dq = summed(dq_slots, 2 * SLOTS, frame).T * 0.125
-            qkv_send[frame, 0] = dq.astype(jnp.bfloat16)
-            dk = summed(dk_slots, 2 * SLOTS + 4 * frames, frame)
-            qkv_send[frame, 1] = dk.astype(jnp.bfloat16)
-            dv = summed(dv_slots, 2 * SLOTS + 4 * frames, frame)
-            qkv_send[frame, 2] = dv.astype(jnp.bfloat16)
-
-        def qkv_copy(flips):
+        def combine(frame, _):
+            side, chip = lax.rem(frame, 2), lax.div(frame, 2)
+            cosine = rope_ref[frame, 0:1, :]
+            sine = rope_ref[frame, 1:2, :]
+
+            def turned_back(value):
+                value = value.astype(jnp.bfloat16).astype(jnp.float32)
+                return (value * cosine + turn_pairs(value, None) * sine).astype(jnp.bfloat16)
+
+            start = 2 * SLOTS + 4 * frames
+            parts = (
+                turned_back(summed(dq_slots, 2 * SLOTS, frame).T * 0.125),
+                turned_back(summed(dk_slots, start, frame)),
+                summed(dv_slots, start, frame).astype(jnp.bfloat16),
+            )
+            where = pl.ds(pl.multiple_of(frame * tokens, tokens), tokens)
+            for place, part in enumerate(parts):
+                d_all[side, chip, :, place * 128 : (place + 1) * 128] = part
+                d_turned[place * 128 : (place + 1) * 128, where] = part.T
+            return 0
+
+        lax.fori_loop(0, frames, combine, 0)
+
+        def normed_product(unit, side, chunk):
+            first = (unit - first_out - 1) * half
+            left = d_all[side, :, first : first + half, :].reshape(half_rows, 384)
+            return dot_nt(left, w_own[lane_block(chunk), :])
+
+        def normed_plan(point):
+            run_plan(point, normed_product)
+
+        for step in (6, 7, 8, 9):
+            gather_copy(step).wait()
+        group_loads = [
+            pltpu.make_async_copy(n1_hbm, n1_group.at[head], load_sem.at[0])
+        ] + [
+            pltpu.make_async_copy(
+                n1_all.at[peer_head(head, flips)],
+                n1_group.at[peer_head(head, flips)],
+                load_sem.at[flips],
+            )
+            for flips in others
+        ]
+        for copy in group_loads:
+            copy.start()
+        normed_plan("combined")
+        for copy in group_loads:
+            copy.wait()
+
+        piece = width // n_dp
+
+        def own_columns(chunk, _):
+            right = n1_group[:, :, lane_block(chunk)].reshape(frames * tokens, BLOCK)
+            value = dot_nn(d_turned[...], right).astype(jnp.bfloat16)
+            for part in range(BLOCK // piece):
+                z_send[chunk * (BLOCK // piece) + part] = value[
+                    :, part * piece : (part + 1) * piece
+                ]
+            return 0
+
+        lax.fori_loop(0, chunks, own_columns, 0)
+        mod_load(2).start()
+        mod_load(3).start()
+        z_copies = [
+            remote(
+                z_send.at[dp_peers[hop]],
+                z_recv.at[hop],
+                z_send_sem.at[hop],
+                z_recv_sem.at[hop],
+                (dp_peers[hop], head),
+            )
+            for hop in range(n_dp - 1)
+        ]
+        for copy in z_copies:
+            copy.start()
+        normed_plan("columns")
+
+        def cond_block(block, vector, first):
+            vector = vector.astype(jnp.bfloat16).astype(jnp.float32)
+
+            def body(index, _):
+                rows = pl.ds(pl.multiple_of(index * 64, 64), 64)
+                page = block % 2 * pages + lax.div(index, tokens // 64)
+                inside = pl.ds(pl.multiple_of(lax.rem(index, tokens // 64) * 64, 64), 64)
+                total = jnp.zeros((64, 128), jnp.float32) if first else cond_sum[rows, :]
+                for lanes in range(0, width, 128):
+                    total = total + n1_group[page, inside, lanes : lanes + 128].astype(
+                        jnp.float32
+                    ) * vector[:, lanes : lanes + 128]
+                cond_sum[rows, :] = total
+                return 0
+
+            lax.fori_loop(0, width // 64, body, 0)
+
+        mod_load(2).wait()
+        cond_block(2, saved_rows[0], True)
+        mod_load(4).start()
+        mod_load(3).wait()
+        cond_block(3, saved_rows[1], False)
+        mod_load(5).start()
+        normed_plan("cond1")
+        mod_load(4).wait()
+        cond_block(4, saved_rows[2], False)
+        mod_load(0).start()
+        mod_load(5).wait()
+        cond_block(5, saved_rows[3], False)
+        mod_load(1).start()
+        normed_plan("cond2")
+
+        for copy in z_copies:
+            copy.wait()
+        total = z_send[group].astype(jnp.float32)
+        for hop in range(n_dp - 1):
+            total = total + z_recv[hop].astype(jnp.float32)
+        p_send[...] = total.T.reshape(8, small, 384)
+
+        def part_copy(flips):
             peer = peer_head(head, flips)
             return remote(
-                qkv_send.at[peer],
-                back.at[:, :, own_lanes],
+                p_send.at[peer],
+                p_recv.at[head],
                 a2a_send.at[2, flips],
                 a2a_recv.at[2, flips],
                 (group, peer),
             )
 
-        def combine_loop(frame, _):
-            combine(frame)
-            return 0
-
-        lax.fori_loop(0, frames, combine_loop, 0)
         for flips in others:
-            qkv_copy(flips).start()
-        back[:, :, own_lanes] = qkv_send[head]
-
-        produce(8, out_right)
-        take_second(4)
-        take_first(5)
-        take_core(8, out_right)
-        take_dp(3)
-        for copy in qkv_loads:
-            copy.wait()
-        for flips in others:
-            qkv_copy(flips).wait()
-
-        def rope_back(chunk, _):
-            lanes = pl.ds(pl.multiple_of(chunk * 128, 128), 128)
-            cosine = mod_ref[6:7, lanes]
-            sine = mod_ref[7:8, lanes]
-            for place, target in ((0, dq_raw), (1, dk_raw)):
-                value = back[place, :, lanes].astype(jnp.float32)
-                target[:, lanes] = (value * cosine + turn_pairs(value, lanes) * sine).astype(
-                    jnp.bfloat16
-                )
-            return 0
-
-        lax.fori_loop(0, width // 128, rope_back, 0)
-
-        def value_right(chunk):
-            return back[2, :, lane_block(chunk)]
-
-        def query_right(chunk):
-            return dq_raw[:, lane_block(chunk)]
-
-        def key_right(chunk):
-            return dk_raw[:, lane_block(chunk)]
-
-        rights = {9: value_right, 10: query_right, 11: key_right}
-        produce(9, value_right)
-        produce(10, query_right)
-        take_core(9, value_right)
-        take_core(10, query_right)
-        produce(11, key_right)
-        take_core(11, key_right)
-
-        def to_first(chunk, _):
-            lanes = lane_block(chunk)
-            ba[:, lanes] = (
-                dot_nt(dq_raw[...], wqkv[0, lanes, :])
-                + dot_nt(dk_raw[...], wqkv[1, lanes, :])
-                + dot_nt(back[2], wqkv[2, lanes, :])
-            )
-            return 0
-
-        lax.fori_loop(0, chunks, to_first, 0)
+            part_copy(flips).start()
+        p_recv[head] = p_send[head]
+
+        for unit in (first_out + 1, first_out + 2):
+            second_copy(unit).wait()
+            value = from_core[slot_of(unit), :, ybit, xbit].astype(jnp.float32)
+            value = value + from_second[slot_of(unit)].astype(jnp.float32)
+            first = (unit - first_out - 1) * half
+            dn1[first : first + half, :] = value.reshape(half, width)
 
         def first_norm_back(index, sums):
             shift_sum, scale_sum = sums
@@ -859,7 +969,7 @@
             value = x_ref[rows, :].astype(jnp.float32)
             scale = lax.rsqrt(jnp.mean(value * value, axis=1, keepdims=True) + EPSILON)
             normed = value * scale
-            grad = ba[rows, :]
+            grad = dn1[rows, :]
             shift_sum = shift_sum + jnp.sum(grad, axis=0, keepdims=True)
             scale_sum = scale_sum + jnp.sum(grad * normed, axis=0, keepdims=True)
             inner = grad * (1.0 + scale_one)
@@ -872,7 +982,7 @@
         )
         vectors = jnp.concatenate(
             [
-                cond_ref[...].astype(jnp.float32),
+                cond_ref[0:1, :],
                 shift_one_grad,
                 scale_one_grad,
                 *saved_rows,
@@ -882,76 +992,132 @@
         )
         rows_ref[group, ybit, xbit, core] = vectors.astype(jnp.bfloat16)
 
+        mine = rows_ref.at[group, ybit, xbit, core]
+        row_dp = [
+            remote(mine, mine, row_dp_send.at[hop], row_dp_recv.at[hop], (dp_peers[hop], head))
+            for hop in range(n_dp - 1)
+        ]
+        y_part = rows_ref.at[:, ybit, xbit, core]
+        x_part = rows_ref.at[:, :, xbit, core]
+        core_part = rows_ref.at[:, :, :, core]
+        row_y = remote(y_part, y_part, row_send.at[0], row_recv.at[0], (group, y_peer))
+        row_x = remote(x_part, x_part, row_send.at[1], row_recv.at[1], (group, x_peer))
+        row_core = remote(core_part, core_part, row_send.at[2], row_recv.at[2], (group, core_peer))
+        for copy in row_dp:
+            copy.start()
+        run_plan("rows")
+        mod_load(0).wait()
+        cond_block(0, shift_one_grad, False)
+        mod_load(1).wait()
+        cond_block(1, scale_one_grad, False)
+        cond = cond_ref[1:2, :]
+        gate = 1.0 / (1.0 + jnp.exp(-cond))
+        gcond_ref[...] = jnp.sum(cond_sum[...].T, axis=0, keepdims=True) * (
+            gate * (1.0 + cond * (1.0 - gate))
+        )
+        for copy in row_dp:
+            copy.wait()
+        row_y.start()
+        run_plan("row_y")
+        row_y.wait()
+        row_x.start()
+        run_plan("row_x")
+        row_x.wait()
+        row_core.start()
+        for flips in others:
+            part_copy(flips).wait()
+        for block in range(8):
+            for place, target in enumerate((gq_ref, gk_ref, gv_ref)):
+                target[:, block * 128 : (block + 1) * 128] = p_recv[
+                    block, :, place * 128 : (place + 1) * 128
+                ]
+        run_plan("row_core")
+        row_core.wait()
+        everyone = rows_ref[...].reshape(n_dp * 64, width)
+        device = group * 8 + head
+        wanted = lax.broadcasted_iota(jnp.int32, (small, width), 0) + device * small
+        column = lax.broadcasted_iota(jnp.int32, (small, width), 1)
+        picked = dot_nt(jnp.where(wanted == column, 1.0, 0.0).astype(jnp.bfloat16), everyone)
+        place = lax.rem(lax.broadcasted_iota(jnp.int32, picked.shape, 1), 8)
+        picked = jnp.where(place == 0, picked, 0.0)
+        mod_out = []
+        for block in range(6):
+            left = pltpu.roll(picked, 1 + block, 1).astype(jnp.bfloat16)
+            dn1[block * small : (block + 1) * small, :] = dot_nn(left, everyone)
+            mod_out.append(
+                pltpu.make_async_copy(
+                    dn1.at[pl.ds(block * small, small), :],
+                    gmod_hbm.at[:, pl.ds(block * width, width)],
+                    load_sem.at[block],
+                )
+            )
+            mod_out[-1].start()
+        run_plan("end")
+        for copy in mod_out:
+            copy.wait()
+        for unit in (count - 2, count - 1):
+            core_copy(unit).wait_send()
+
     pl.run_scoped(
         attention_part,
-        pltpu.VMEM((3, width, width), jnp.bfloat16),
+        pltpu.VMEM((frames, tokens, 128), jnp.bfloat16),
+        pltpu.VMEM((frames, tokens, 128), jnp.bfloat16),
+        pltpu.VMEM((frames, tokens, 128), jnp.bfloat16),
+        pltpu.VMEM((frames, tokens, 128), jnp.float32),
+        pltpu.VMEM((frames, tokens, width), jnp.bfloat16),
+        pltpu.VMEM((width, 384), jnp.bfloat16),
         pltpu.VMEM((SLOTS + 1, 128, tokens), jnp.float32),
         pltpu.VMEM((SLOTS + 1, tokens, 128), jnp.float32),
         pltpu.VMEM((SLOTS + 1, tokens, 128), jnp.float32),
-        pltpu.VMEM((frames, 3, tokens, 128), jnp.bfloat16),
-        pltpu.VMEM((tokens, width), jnp.bfloat16),
-        pltpu.VMEM((tokens, width), jnp.bfloat16),
         pltpu.VMEM((frames, 2, tokens), jnp.float32),
+        pltpu.VMEM((2, frames // 2, tokens, 384), jnp.bfloat16),
+        pltpu.VMEM((384, frames * tokens), jnp.bfloat16),
+        pltpu.VMEM((tokens, width), jnp.float32),
+        pltpu.VMEM((width, 128), jnp.float32),
     )
 
-    mine = rows_ref.at[group, ybit, xbit, core]
-    row_dp = [
-        remote(mine, mine, row_dp_send.at[hop], row_dp_recv.at[hop], (dp_peers[hop], head))
-        for hop in range(n_dp - 1)
-    ]
-    y_part = rows_ref.at[:, ybit, xbit, core]
-    x_part = rows_ref.at[:, :, xbit, core]
-    core_part = rows_ref.at[:, :, :, core]
-    row_y = remote(y_part, y_part, row_send.at[0], row_recv.at[0], (group, y_peer))
-    row_x = remote(x_part, x_part, row_send.at[1], row_recv.at[1], (group, x_peer))
-    row_core = remote(core_part, core_part, row_send.at[2], row_recv.at[2], (group, core_peer))
-    for copy in row_dp:
-        copy.start()
-
-    take_first(6)
-    take_second(5)
-    take_dp(4)
-    for copy in row_dp:
-        copy.wait()
-    row_y.start()
-    take_first(7)
-    take_second(6)
-    take_dp(5)
-    row_y.wait()
-    row_x.start()
-    take_first(8)
-    take_second(7)
-    take_dp(6)
-    row_x.wait()
-    row_core.start()
-    take_first(9)
-    take_second(8)
-    take_dp(7)
-    row_core.wait()
-    take_first(10)
-    take_second(9)
-    take_dp(8)
-    take_first(11)
-    take_second(10)
-    take_dp(9)
-    take_second(11)
-    take_dp(10)
-    take_dp(11)
-    core_copy(count - 2).wait_send()
-    core_copy(count - 1).wait_send()
-
-
-def back_part(n_dp, table, attended, queries, keys, values, lse, bias, hidden, cotangent, normed,
-              modulation, cond_act, valid, weights):
+
+PLAN = {
+    "fed": [("P", 0), ("P", 1)],
+    "normed": [("C", 0), ("C", 1)],
+    "attended": [("P", 2), ("P", 3)],
+    "branch": [("C", 2), ("C", 3)],
+    "outputs": [("P", 4), ("P", 5)],
+    "scope": [("F", 0), ("F", 1)],
+    2: [("C", 4), ("P", 6)],
+    4: [("C", 5), ("P", 7)],
+    8: [("F", 2)],
+    9: [("F", 3)],
+    10: [("C", 6)],
+    12: [("S", 0)],
+    13: [("S", 1)],
+    14: [("C", 7)],
+    15: [("P", 8)],
+    "combined": [("P", 9), ("P", 10), ("C", 9), ("C", 10)],
+    "columns": [("F", 4), ("F", 5)],
+    "cond1": [("F", 9), ("F", 10)],
+    "cond2": [],
+    "rows": [("C", 8), ("S", 2), ("S", 3), ("D", 0), ("D", 1)],
+    "row_y": [("F", 6), ("F", 7), ("D", 2)],
+    "row_x": [("S", 4), ("D", 3)],
+    "row_core": [("S", 5), ("F", 8), ("S", 6), ("S", 7)],
+    "end": [("D", 4), ("D", 5), ("D", 6), ("D", 7), ("S", 8), ("D", 8)],
+}
+GATHER_AT = 8
+
+
+def back_part(n_dp, vmem_operands, hbm_operands):
+    table, attended, lse, hidden = vmem_operands[:4]
+    hbm_up = hbm_operands[6]
     tokens, width = hidden.shape
-    frames = attended.shape[0] // tokens
-    hidden_width = weights[1].shape[1]
+    group_tokens = attended.shape[0]
+    frames = group_tokens // tokens
+    hidden_width = hbm_up.shape[1]
     devices = n_dp * 8
     small, large = width // devices, hidden_width // devices
     first_up = large // small
     tiles = hidden_width // width
-    units = first_up + tiles + 4
-    slots = units - 3
+    units = first_up + tiles + 3
     dma = pltpu.SemaphoreType.DMA
     f32, bf16 = jnp.float32, jnp.bfloat16
     shape = jax.ShapeDtypeStruct
@@ -964,29 +1130,34 @@
             *[shape((small, width), f32)] * 4,
             shape((small, hidden_width), f32),
             shape((large, width), f32),
-            shape((n_dp, 2, 2, 2, 8, width), bf16),
+            shape((small, 6 * width), f32),
+            shape((1, width), f32),
+            shape((frames, tokens, width), bf16),
         ),
-        in_specs=[IN_SMEM] + [IN_VMEM] * 12 + [IN_PLACE] * 6,
-        out_specs=tuple([IN_VMEM] * 10),
+        in_specs=[IN_SMEM]
+        + [IN_VMEM] * (len(vmem_operands) - 1)
+        + [IN_PLACE] * len(hbm_operands),
+        out_specs=(IN_PLACE, *[IN_VMEM] * 8, IN_PLACE, IN_VMEM, IN_PLACE),
         scratch_shapes=[
             pltpu.VMEM((tokens, width), bf16),
             pltpu.VMEM((frames, tokens, 128), bf16),
-            pltpu.VMEM((3, tokens, width), bf16),
-            pltpu.VMEM((slots, n_dp, 2, 2, small, width), bf16),
-            pltpu.VMEM((slots, n_dp, 2, small, width), bf16),
-            pltpu.VMEM((slots, n_dp, small, width), bf16),
-            pltpu.VMEM((units, n_dp - 1, small, width), bf16),
+            pltpu.VMEM((units, n_dp, 2, 2, small, width), bf16),
+            pltpu.VMEM((units, n_dp, 2, small, width), bf16),
+            pltpu.VMEM((units, n_dp, small, width), bf16),
+            pltpu.VMEM((units - 2, n_dp - 1, small, width), bf16),
             pltpu.VMEM((2, n_dp, 2, 2, small, width), bf16),
             pltpu.VMEM((tokens, width), bf16),
-            pltpu.VMEM((first_up + 3, 2, width // 2, tokens), bf16),
-            pltpu.VMEM((tokens, width), bf16),
+            pltpu.VMEM((first_up + 2, 2, width // 2, tokens), bf16),
             pltpu.VMEM((tokens, width), bf16),
             pltpu.VMEM((tokens, hidden_width), bf16),
             pltpu.VMEM((tokens, width), bf16),
             pltpu.VMEM((tokens, width), f32),
-            pltpu.VMEM((tokens, width), f32),
-            pltpu.VMEM((width, width), bf16),
-            dma((1 + 2 * tiles + 3,)),
+            pltpu.VMEM((n_dp, 2, 2, 2, 8, width), bf16),
+            pltpu.VMEM((n_dp, 384, width // n_dp), bf16),
+            pltpu.VMEM((n_dp - 1, 384, width // n_dp), bf16),
+            pltpu.VMEM((8, small, 384), f32),
+            pltpu.VMEM((8, small, 384), f32),
+            dma((16,)),
             dma((3, 8)),
             dma((3, 8)),
             *[dma((units,))] * 6,
@@ -996,25 +1167,118 @@
             dma((3,)),
             dma((n_dp - 1,)),
             dma((n_dp - 1,)),
+            dma((10,)),
+            dma((10,)),
+            dma((n_dp - 1,)),
+            dma((n_dp - 1,)),
+            dma((6, frames // 2)),
         ],
         compiler_params=pltpu.CompilerParams(
             collective_id=0, has_side_effects=True, vmem_limit_bytes=67043328
         ),
         name="back_part",
-    )(
-        table,
-        attended,
-        *[array.reshape(frames, tokens, 128) for array in (queries, keys, values)],
-        lse,
-        bias.reshape(frames, tokens, 128),
-        hidden,
-        cotangent,
-        normed,
-        modulation,
-        cond_act,
-        valid,
-        *weights,
-    )
+    )(*vmem_operands, *hbm_operands)
+
+
+def front_kernel(*refs):
+    (
+        x_ref,
+        mod_ref,
+        rope_ref,
+        wq_hbm,
+        wk_hbm,
+        wv_hbm,
+        n1_ref,
+        q_ref,
+        k_ref,
+        v_ref,
+        weights,
+        sent,
+        load_sem,
+        send_sem,
+        recv_sem,
+    ) = refs
+    tokens, width = x_ref.shape
+    group = lax.axis_index("dp")
+    head = lax.axis_index("head")
+    core = lax.rem(head, 2)
+    barrier = pltpu.get_barrier_semaphore()
+    for flips in range(1, 8):
+        pl.semaphore_signal(
+            barrier, inc=1, device_id=(group, peer_head(head, flips)), device_id_type=MESH_ID
+        )
+    loads = [
+        pltpu.make_async_copy(source, weights.at[place], load_sem.at[place])
+        for place, source in enumerate((wq_hbm, wk_hbm, wv_hbm))
+    ]
+    for copy in loads:
+        copy.start()
+    shift, scaling = mod_ref[0:1, :], mod_ref[1:2, :]
+
+    def norm(index, _):
+        rows = pl.ds(pl.multiple_of(index * 32, 32), 32)
+        value = x_ref[rows, :].astype(jnp.float32)
+        scale = lax.rsqrt(jnp.mean(value * value, axis=1, keepdims=True) + EPSILON)
+        n1_ref[rows, :] = (value * scale * (1.0 + scaling) + shift).astype(jnp.bfloat16)
+        return 0
+
+    lax.fori_loop(0, tokens // 32, norm, 0)
+    pl.semaphore_wait(barrier, 7)
+    cosine, sine = rope_ref[0:1, :], rope_ref[1:2, :]
+    outs = (q_ref, k_ref, v_ref)
+
+    def copy_to(place, flips):
+        peer = peer_head(head, flips)
+        return remote(
+            sent.at[place, :, pl.ds(peer * 128, 128)],
+            outs[place].at[head],
+            send_sem.at[place, flips],
+            recv_sem.at[place, flips],
+            (group, peer),
+        )
+
+    for place in range(3):
+        loads[place].wait()
+        for chip_flips in (6, 2, 4, 0):
+            chip = lax.div(peer_head(head, chip_flips), 2)
+            lanes = pl.ds(pl.multiple_of(chip * BLOCK, BLOCK), BLOCK)
+            value = dot_nn(n1_ref[...], weights[place, :, lanes])
+            for side in range(2):
+                part = value[:, side * 128 : (side + 1) * 128]
+                if place < 2:
+                    part = part * cosine + turn_pairs(part, None) * sine
+                where = pl.ds(pl.multiple_of(chip * BLOCK + side * 128, 128), 128)
+                sent[place, :, where] = part.astype(jnp.bfloat16)
+            for flips in (chip_flips, chip_flips + 1):
+                if flips:
+                    copy_to(place, flips).start()
+        outs[place][head] = sent[place, :, pl.ds(pl.multiple_of(head * 128, 128), 128)]
+    for place in range(3):
+        for flips in range(1, 8):
+            copy_to(place, flips).wait()
+
+
+def front_part(hidden, modulation, rope, query_weight, key_weight, value_weight):
+    tokens, width = hidden.shape
+    dma = pltpu.SemaphoreType.DMA
+    block = jax.ShapeDtypeStruct((8, tokens, 128), jnp.bfloat16)
+    return pl.pallas_call(
+        front_kernel,
+        out_shape=(jax.ShapeDtypeStruct((tokens, width), jnp.bfloat16), block, block, block),
+        in_specs=[IN_VMEM] * 3 + [IN_PLACE] * 3,
+        out_specs=(IN_VMEM,) * 4,
+        scratch_shapes=[
+            pltpu.VMEM((3, width, width), jnp.bfloat16),
+            pltpu.VMEM((3, tokens, width), jnp.bfloat16),
+            dma((3,)),
+            dma((3, 8)),
+            dma((3, 8)),
+        ],
+        compiler_params=pltpu.CompilerParams(
+            collective_id=1, has_side_effects=True, vmem_limit_bytes=32 * 1024 * 1024
+        ),
+        name="front_part",
+    )(hidden, modulation, rope, query_weight, key_weight, value_weight)
 
 
 def slot_table(first, frames):
@@ -1049,116 +1313,84 @@
     cotangent,
 ):
     tok_dev, model_width = hidden_in.shape
-    frames_dev = frame_cond.shape[0]
     group_tokens = patch_valid.shape[0]
+    frames = group_tokens // PATCHES
     head_index = lax.axis_index("head")
-    clip_of, frame_of, position = group_layout(clip_lengths[0], group_tokens, PATCHES)
-    local_start = head_index * tok_dev
-    local_position = lax.dynamic_slice_in_dim(position, local_start, tok_dev)
-    local_valid = (
-        lax.dynamic_slice_in_dim(patch_valid, local_start, tok_dev)
-        .astype(jnp.float32)
-        .reshape(frames_dev, PATCHES)
-    )
-    angles = local_position.astype(jnp.float32)[:, None] * frequencies(HEAD_DIM // 2)[None, :]
+    n_dp = lax.axis_size("dp")
+    frame = jnp.arange(frames, dtype=jnp.int32)
+    ends = jnp.cumsum(clip_lengths[0])
+    first_frames = jnp.max(
+        jnp.where(ends[None, :] <= frame[:, None], ends[None, :], 0), axis=1
+    ).astype(jnp.int32)
+    angles = (frame - first_frames).astype(jnp.float32)[:, None] * frequencies(HEAD_DIM // 2)[None]
+    cosine, sine = jnp.cos(angles), jnp.sin(angles)
+    cosines = jnp.concatenate([cosine] * 4, axis=1)
+    sines = jnp.concatenate([-sine, sine] * 2, axis=1)
+    rope = jnp.stack([cosines, sines], axis=1)
+    rope_back = jnp.stack([cosines, -sines], axis=1)
+    local_valid = lax.dynamic_slice_in_dim(patch_valid, head_index * tok_dev, tok_dev)
     cond_value = frame_cond.astype(jnp.float32)
     cond_act = jax.nn.silu(cond_value).astype(jnp.bfloat16)
     modulation = jnp.dot(cond_act, modulation_weight, preferred_element_type=jnp.float32).reshape(
-        frames_dev, 1, 6 * model_width
+        6, model_width
     )
-    shift_one, scale_one, gate_one, shift_two, scale_two, gate_two = jnp.split(
-        modulation, 6, axis=2
+    normed_one, head_query, head_key, head_value = front_part(
+        hidden_in,
+        modulation[:2],
+        lax.dynamic_index_in_dim(rope, head_index, 0, keepdims=False),
+        query_weight,
+        key_weight,
+        value_weight,
     )
-    tokens = hidden_in.astype(jnp.float32).reshape(frames_dev, PATCHES, model_width)
-    normed_one = (
-        modulate(tokens, shift_one, scale_one).astype(jnp.bfloat16).reshape(tok_dev, model_width)
-    )
-    query_raw = jnp.dot(normed_one, query_weight, preferred_element_type=jnp.float32)
-    key_raw = jnp.dot(normed_one, key_weight, preferred_element_type=jnp.float32)
-    query_send = (
-        rotate(query_raw.reshape(tok_dev, HEADS, HEAD_DIM), angles)
-        .reshape(tok_dev, model_width)
-        .astype(jnp.bfloat16)
-    )
-    key_send = (
-        rotate(key_raw.reshape(tok_dev, HEADS, HEAD_DIM), angles)
-        .reshape(tok_dev, model_width)
-        .astype(jnp.bfloat16)
-    )
-    value_send = jnp.dot(normed_one, value_weight, preferred_element_type=jnp.float32).astype(
-        jnp.bfloat16
-    )
-    head_query, head_key, head_value = (
-        lax.all_to_all(query_send, "head", split_axis=1, concat_axis=0, tiled=True),
-        lax.all_to_all(key_send, "head", split_axis=1, concat_axis=0, tiled=True),
-        lax.all_to_all(value_send, "head", split_axis=1, concat_axis=0, tiled=True),
-    )
-    first_frames = (frame_of - position)[::PATCHES]
     bias = jnp.broadcast_to(
         jnp.where(patch_valid == 1, 0.0, MASKED).astype(jnp.float32)[:, None],
         (group_tokens, 128),
     )
-    attended_send, logsum = attend_forward(first_frames, head_query, head_key, head_value, bias)
-    n_dp = lax.axis_size("dp")
-    row_angles = angles[0]
-    cosine, sine = jnp.cos(row_angles), jnp.sin(row_angles)
-    table_rows = jnp.concatenate(
-        [
-            modulation.reshape(6, model_width),
-            jnp.tile(jnp.concatenate([cosine, cosine]), HEADS)[None],
-            jnp.tile(jnp.concatenate([sine, -sine]), HEADS)[None],
-        ],
-        axis=0,
+    attended, logsum = attend_forward(
+        first_frames,
+        *[array.reshape(group_tokens, 128) for array in (head_query, head_key, head_value)],
+        bias,
     )
-    (
-        block_out,
-        grad_input,
-        statistics,
-        grad_query,
-        grad_key,
-        grad_value,
-        grad_output,
-        grad_up,
-        grad_down,
-        gathered,
-    ) = back_part(
+    results = back_part(
         n_dp,
-        slot_table(first_frames, group_tokens // PATCHES),
-        attended_send,
-        head_query,
-        head_key,
-        head_value,
-        logsum,
-        bias,
-        hidden_in,
-        cotangent,
-        normed_one,
-        table_rows,
-        cond_act,
-        jnp.broadcast_to(local_valid.reshape(tok_dev, 1), (tok_dev, 128)),
-        (output_weight, up_weight, down_weight, query_weight, key_weight, value_weight),
+        (
+            slot_table(first_frames, frames),
+            attended,
+            logsum,
+            hidden_in,
+            cotangent,
+            modulation,
+            rope_back,
+            jnp.concatenate([cond_act.astype(jnp.float32), cond_value], axis=0),
+            jnp.broadcast_to(local_valid.astype(jnp.float32)[:, None], (tok_dev, 128)),
+        ),
+        (
+            head_query,
+            head_key,
+            head_value,
+            bias.reshape(frames, PATCHES, 128),
+            normed_one,
+            output_weight,
+            up_weight,
+            down_weight,
+            query_weight,
+            key_weight,
+            value_weight,
+            modulation_weight,
+        ),
     )
-    device = lax.axis_index("dp") * lax.axis_size("head") + head_index
-    gathered = gathered.reshape(n_dp * 8, 8, model_width)
-    share = model_width // (n_dp * 8)
-    dmod_all = gathered[:, 1:7].reshape(n_dp * 8, 6 * model_width)
-    grad_modulation = inner_rows(
-        lax.dynamic_slice_in_dim(gathered[:, 0], device * share, share, 1), dmod_all
-    )
-    modulation_grad = lax.dynamic_slice_in_dim(dmod_all, device, 1, 0)
-    cond_act_grad = times_transposed(modulation_grad, modulation_weight)
-    grad_cond = jax.vjp(jax.nn.silu, cond_value)[1](cond_act_grad)[0]
+    (block_out, grad_input, statistics, gq, gk, gv, go, gup, gdown, gmod, gcond, _) = results
     return (
         block_out,
         grad_input,
-        grad_cond,
-        grad_query,
-        grad_key,
-        grad_value,
-        grad_output,
-        grad_up,
-        grad_down,
-        grad_modulation,
+        gcond,
+        gq,
+        gk,
+        gv,
+        go,
+        gup,
+        gdown,
+        gmod,
         statistics[:1, :3],
     )
 

time: 297 us -> 249 us (0.84)
  waiting for transfers between devices: 20.2 us -> 0 us
  matrix products: 23.8 us -> 6.47 us
  starting transfers between devices: 12.4 us -> 0 us
  local copies, waits for them, and re-layouts: 24.1 us -> 30.8 us
  Pallas kernels: 208 us -> 204 us
    pallas_call x1, Pallas kernels: 196 us -> 168 us  [back_part(): pl.pallas_call(lambda *refs: back_kernel(n_dp, *refs), out_shape=(shape((...]
    pallas_call x0 -> x1, Pallas kernels: none -> 23.8 us  [front_part(): pl.pallas_call(front_kernel, out_shape=(jax.ShapeDtypeStruct((tokens, wid...]
    all_to_all x3 -> x0, waiting for transfers between devices: 20.2 us -> none  [the longest x1 8.34 us: per_device(): lax.all_to_all(key_send, 'head', split_axis=1, concat_axis=0, tiled=True)]
    dot_general x5 -> x0, matrix products: 17.3 us -> none  [the longest x1 8.64 us: times_transposed(): lax.dot_general(left, right, (((1,), (1,)), ((), ())), preferred_element_...]
    all_to_all x3 -> x0, starting transfers between devices: 12.4 us -> none  [the longest x1 5.2 us: per_device(): lax.all_to_all(query_send, 'head', split_axis=1, concat_axis=0, tiled=True)]
    unnamed x47 -> x28, local copies, waits for them, and re-layouts: 11.7 us -> 23.9 us
  transfers between devices with their start and end apart: 3 -> 0, of which waited for: 3 -> 0; matrix products, arithmetic and copies ran while one was open for 3% -> 0% of each run, Pallas kernels for 0% -> 0%
where the time goes in v3:
time: 249 us; the launch traced here: 248 us
  Pallas kernels  204 us (82%)
  local copies, waits for them, and re-layouts  30.8 us (12%)
  matrix products  6.47 us (3%)
  other arithmetic  5.86 us (2%)
    pallas_call x1, Pallas kernels, back_part(): pl.pallas_call(lambda *refs: back_kernel(n_dp, *refs), out_shape=(shape((...  168 us
    unnamed x28, local copies, waits for them, and re-layouts  23.9 us
    pallas_call x1, Pallas kernels, front_part(): pl.pallas_call(front_kernel, out_shape=(jax.ShapeDtypeStruct((tokens, wid...  23.8 us
    pallas_call x1, Pallas kernels, attend_forward(): pl.pallas_call(attend_forward_kernel, out_shape=(jax.ShapeDtypeStruct((to...  12.6 us
    dot_general x1, matrix products, per_device(): jnp.dot(cond_act, modulation_weight, preferred_element_type=jnp.float32)  6.47 us

profile of v3, /device:TPU:0, one launch (start us, length us, event | category | flops | bytes accessed | tf_op | source)
XLA Modules:
  0.0 247.9 jit_solution(12774658889018913614)
XLA Ops:
  0.6 0.8 reduce-window.8
  1.5 0.1 select_reduce_fusion.2.first_ref
  1.6 0.0 copy-start.8
  1.6 0.8 dynamic-slice_convert_fusion
  2.4 0.1 broadcast_in_dim.74
  2.4 0.1 reshape.274
  2.5 0.1 convert_reduce_fusion
  2.7 0.1 select_reduce_fusion
  2.8 0.1 reduce_sum.32
  2.9 0.1 fusion.9
  2.9 0.2 slice_reduce_fusion
  3.1 0.2 slice_reduce_fusion.1
  3.3 0.2 slice_reduce_fusion.2
  3.5 0.1 add_bitcast_fusion
  3.6 0.1 copy.35
  3.7 0.1 copy.36
  3.8 0.1 copy.37
  3.8 0.1 pad_add_fusion
  3.9 0.1 reshape.275
  4.0 0.6 concatenate.37.refs_0_
  4.6 0.7 convert_convert_fusion
  5.3 0.7 convert_element_type.27
  6.0 0.6 pad_maximum_fusion.1.refs_7_
  6.6 0.7 compare_select_fusion
  7.3 0.1 fusion.13
  7.4 0.1 maximum_negate_fusion
  7.5 0.1 maximum_bitcast_fusion
  7.6 0.1 pad_maximum_fusion.2
  7.7 0.6 pad_maximum_fusion.refs_6_
  8.3 0.0 copy-start
  8.3 0.0 copy-start.3
  8.3 6.5 %fusion.3 = f32[1,6144]{1,0:T(1,128)S(1)} fusion(bf16[1024,6144]{1,0:T(8,128)(2,1)} %refs_20_.1, bf16[1,1024]{1,0:T(2,128)(2,1)} %param.13), kind=kOutput, calls=%fused_computation.25 | convolution fusion | flops 12589056 | bytes 12609536 | tf_op jit(solution)/shard_map/dot_general | solution.py:1334
  14.8 0.0 copy-done.8
  14.8 0.6 reshape.280.refs_5_
  15.4 0.8 broadcast_in_dim.83.refs_8_
  16.2 1.3 broadcast_in_dim.82.bias_ref
  17.5 1.3 broadcast_in_dim.85.refs_12_
  18.8 0.0 copy-done
  18.8 0.0 copy-done.3
  18.8 0.0 copy-start.1
  18.8 1.6 copy-done.1
  20.4 0.0 copy-start.2
  20.4 1.6 copy-done.2
  22.0 23.8 %front_part.1 = (bf16[256,1024]{1,0:T(8,128)(2,1)S(1)}, bf16[8,256,128]{2,1,0:T(8,128)(2,1)S(1)}, bf16[8,256,128]{2,1,0:T(8,128)(2,1)S(1)}, bf16[8,256,128]{2,1,0:T(8,128)(2,1)S(1)}) custom-call(bf16[256,1024]{1,0:T(8,128)(2,1)S(1)} %copy-done.3, f32[2,1024]{1,0:T(2,128)S(1)} %slice.34.refs_1_, f32[2,128]{1,0:T(2,128)S(1)} %bitcast.32, ...), custom_call_target="tpu_custom_call" | custom-call | tf_op jit(solution)/shard_map/front_part/pallas_call | solution.py:1265
  45.8 0.0 copy-start.4
  45.8 0.8 copy-done.4
  46.6 0.0 copy-start.5
  46.6 0.8 copy-done.5
  47.4 0.0 copy-start.6
  47.4 0.8 copy-done.6
  48.2 0.8 copy-done.7
  49.0 12.6 %attend_forward.1 = (bf16[2048,128]{1,0:T(8,128)(2,1)}, f32[8,2,256]{2,1,0:T(2,128)}) custom-call(s32[8]{0:T(128)} %copy-done.8, bf16[2048,128]{1,0:T(8,128)(2,1)} %bitcast.29, bf16[2048,128]{1,0:T(8,128)(2,1)} %bitcast.30, bf16[2048,128]{1,0:T(8,128)(2,1)} %bitcast.31, f32[2048,128]{1,0:T(8,128)} %broadcast_in_dim.82.bias_ref), custom_call_target="tpu_custom_call" | custom-call | tf_op jit(solution)/shard_map/attend_forward/pallas_call | solution.py:113
  61.5 167.6 %back_part.1 = (bf16[256,1024]{1,0:T(8,128)(2,1)}, f32[256,1024]{1,0:T(8,128)}, f32[8,128]{1,0:T(8,128)}, f32[32,1024]{1,0:T(8,128)}, f32[32,1024]{1,0:T(8,128)}...) custom-call(s32[115]{0:T(128)} %concatenate.37.refs_0_, ...), custom_call_target="tpu_custom_call" | custom-call | tf_op jit(solution)/shard_map/back_part/pallas_call | solution.py:1124
  229.2 1.2 slice.35
  230.4 1.9 copy.51
  232.2 2.3 copy.52
  234.5 1.3 copy.53
  235.8 1.6 copy.54
  237.4 1.6 copy.55
  239.0 1.6 copy.56
  240.5 1.6 copy.57
  242.1 1.9 copy.58
  244.0 1.9 copy.59
  245.8 2.1 copy.60
  (13 shorter events, 0.1 us)
Async XLA Ops:
  1.6 13.2 %copy-start.8 = (s32[8]{0:T(128)}, s32[8]{0:T(128)S(1)}, u32[]{:S(2)}) copy-start(s32[8]{0:T(128)S(1)} %select_reduce_fusion.2.first_ref) | copy-start | bytes 100
  8.3 10.5 %copy-start = (bf16[1024,1024]{1,0:T(8,128)(2,1)S(1)}, bf16[1024,1024]{1,0:T(8,128)(2,1)}, u32[]{:S(2)}) copy-start(bf16[1024,1024]{1,0:T(8,128)(2,1)} %refs_17_.1) | copy-start | bytes 6291460
  8.3 10.5 %copy-start.3 = (bf16[256,1024]{1,0:T(8,128)(2,1)S(1)}, bf16[256,1024]{1,0:T(8,128)(2,1)}, u32[]{:S(2)}) copy-start(bf16[256,1024]{1,0:T(8,128)(2,1)} %refs_3_.3) | copy-start | bytes 1572868
  18.8 1.6 copy-start.1
  20.4 1.6 copy-start.2
  45.8 0.8 copy-start.4
  46.6 0.8 copy-start.5
  47.4 0.8 copy-start.6
  48.2 0.8 copy-start.7

commit v4 on v3

--- a/solution.py
+++ b/solution.py
@@ -855,7 +855,12 @@
             return dot_nt(left, w_own[lane_block(chunk), :])
 
         def normed_plan(point):
-            run_plan(point, normed_product)
+            run_plan(
+                point,
+                lambda unit, *where: (normed_product if unit > first_out else weight_product)(
+                    unit, *where
+                ),
+            )
 
         for step in (6, 7, 8, 9):
             gather_copy(step).wait()
@@ -1084,24 +1089,18 @@
     "branch": [("C", 2), ("C", 3)],
     "outputs": [("P", 4), ("P", 5)],
     "scope": [("F", 0), ("F", 1)],
-    2: [("C", 4), ("P", 6)],
-    4: [("C", 5), ("P", 7)],
-    8: [("F", 2)],
-    9: [("F", 3)],
-    10: [("C", 6)],
-    12: [("S", 0)],
-    13: [("S", 1)],
-    14: [("C", 7)],
-    15: [("P", 8)],
-    "combined": [("P", 9), ("P", 10), ("C", 9), ("C", 10)],
-    "columns": [("F", 4), ("F", 5)],
-    "cond1": [("F", 9), ("F", 10)],
-    "cond2": [],
-    "rows": [("C", 8), ("S", 2), ("S", 3), ("D", 0), ("D", 1)],
-    "row_y": [("F", 6), ("F", 7), ("D", 2)],
-    "row_x": [("S", 4), ("D", 3)],
-    "row_core": [("S", 5), ("F", 8), ("S", 6), ("S", 7)],
-    "end": [("D", 4), ("D", 5), ("D", 6), ("D", 7), ("S", 8), ("D", 8)],
+    2: [("P", 6)],
+    4: [("P", 7)],
+    6: [("P", 8)],
+    12: [("C", 4)],
+    13: [("C", 5)],
+    "combined": [("P", 9), ("P", 10), ("S", 0), ("S", 1), ("F", 2), ("F", 3), ("C", 9), ("C", 10)],
+    "columns": [("C", 8)],
+    "cond2": [("F", 4), ("F", 5), ("S", 2), ("S", 3), ("F", 9), ("F", 10), ("C", 6), ("C", 7), ("S", 4), ("S", 5), ("F", 8), ("D", 0), ("D", 1)],
+    "rows": [("D", 2), ("D", 3)],
+    "row_y": [("D", 4), ("D", 5)],
+    "row_x": [("F", 6), ("F", 7), ("S", 8)],
+    "end": [("S", 6), ("S", 7), ("D", 8), ("D", 6), ("D", 7)],
 }
 GATHER_AT = 8
 
@@ -1180,6 +1179,47 @@
     )(*vmem_operands, *hbm_operands)
 
 
+def finish_kernel(*refs):
+    count = len(refs) // 3
+    sources, targets = refs[:count], refs[count : 2 * count]
+    held, (load_sem, store_sem) = refs[2 * count : 3 * count], refs[3 * count :]
+    loads = [
+        pltpu.make_async_copy(source, room, load_sem.at[place])
+        for place, (source, room) in enumerate(zip(sources, held))
+    ]
+    stores = [
+        pltpu.make_async_copy(room, target, store_sem.at[place])
+        for place, (room, target) in enumerate(zip(held, targets))
+    ]
+    for copy in loads:
+        copy.start()
+    for place in range(count - 1):
+        loads[place].wait()
+        stores[place].start()
+    loads[-1].wait()
+    targets[-1][...] = held[-1][0:1, 0:3]
+    for copy in stores[:-1]:
+        copy.wait()
+
+
+def finish(arrays):
+    shapes = [jax.ShapeDtypeStruct(array.shape, array.dtype) for array in arrays]
+    held = [pltpu.VMEM(array.shape, array.dtype) for array in arrays]
+    shapes[-1] = jax.ShapeDtypeStruct((1, 3), jnp.float32)
+    return pl.pallas_call(
+        finish_kernel,
+        out_shape=tuple(shapes),
+        in_specs=[IN_PLACE] * len(arrays),
+        out_specs=(*[IN_PLACE] * (len(arrays) - 1), IN_VMEM),
+        scratch_shapes=[
+            *held,
+            pltpu.SemaphoreType.DMA((len(arrays),)),
+            pltpu.SemaphoreType.DMA((len(arrays),)),
+        ],
+        name="finish",
+    )(*arrays)
+
+
 def front_kernel(*refs):
     (
         x_ref,
@@ -1380,6 +1420,9 @@
         ),
     )
     (block_out, grad_input, statistics, gq, gk, gv, go, gup, gdown, gmod, gcond, _) = results
+    (grad_input, gmod, block_out, gup, gdown, gq, gk, gv, go, gcond, statistics) = finish(
+        (grad_input, gmod, block_out, gup, gdown, gq, gk, gv, go, gcond, statistics)
+    )
     return (
         block_out,
         grad_input,
@@ -1391,7 +1434,7 @@
         gup,
         gdown,
         gmod,
-        statistics[:1, :3],
+        statistics,
     )
 
 

time: 249 us -> 222 us (0.89)
  local copies, waits for them, and re-layouts: 30.8 us -> 12.1 us
  Pallas kernels: 204 us -> 196 us
    unnamed x28 -> x18, local copies, waits for them, and re-layouts: 23.9 us -> 6.36 us
    pallas_call x1, Pallas kernels: 168 us -> 156 us  [back_part(): pl.pallas_call(lambda *refs: back_kernel(n_dp, *refs), out_shape=(shape((...]
    pallas_call x0 -> x1, Pallas kernels: none -> 3.85 us  [finish(): pl.pallas_call(finish_kernel, out_shape=tuple(shapes), in_specs=[IN_PLACE...]
where the time goes in v4:
time: 222 us; the launch traced here: 221 us
  Pallas kernels  196 us (88%)
  local copies, waits for them, and re-layouts  12.1 us (5%)
  matrix products  6.47 us (3%)
  other arithmetic  5.86 us (3%)
    pallas_call x1, Pallas kernels, back_part(): pl.pallas_call(lambda *refs: back_kernel(n_dp, *refs), out_shape=(shape((...  156 us
    pallas_call x1, Pallas kernels, front_part(): pl.pallas_call(front_kernel, out_shape=(jax.ShapeDtypeStruct((tokens, wid...  23.8 us
    pallas_call x1, Pallas kernels, attend_forward(): pl.pallas_call(attend_forward_kernel, out_shape=(jax.ShapeDtypeStruct((to...  12.6 us
    dot_general x1, matrix products, per_device(): jnp.dot(cond_act, modulation_weight, preferred_element_type=jnp.float32)  6.47 us
    unnamed x18, local copies, waits for them, and re-layouts  6.36 us

profile of v4, /device:TPU:0, one launch (start us, length us, event | category | flops | bytes accessed | tf_op | source)
XLA Modules:
  0.0 221.4 jit_solution(11993499457750961687)
XLA Ops:
  0.6 0.8 reduce-window.8
  1.5 0.1 select_reduce_fusion.2.first_ref
  1.6 0.0 copy-start.8
  1.6 0.8 dynamic-slice_convert_fusion
  2.4 0.1 broadcast_in_dim.74
  2.4 0.1 reshape.274
  2.5 0.1 convert_reduce_fusion
  2.7 0.1 select_reduce_fusion
  2.8 0.1 reduce_sum.32
  2.9 0.1 fusion.9
  2.9 0.2 slice_reduce_fusion
  3.1 0.2 slice_reduce_fusion.1
  3.3 0.2 slice_reduce_fusion.2
  3.5 0.1 add_bitcast_fusion
  3.6 0.1 copy.35
  3.7 0.1 copy.36
  3.8 0.1 copy.37
  3.8 0.1 pad_add_fusion
  3.9 0.1 reshape.275
  4.0 0.6 concatenate.37.refs_0_
  4.6 0.7 convert_convert_fusion
  5.3 0.7 convert_element_type.27
  6.0 0.6 pad_maximum_fusion.1.refs_7_
  6.6 0.7 compare_select_fusion
  7.3 0.1 fusion.13
  7.4 0.1 maximum_negate_fusion
  7.5 0.1 maximum_bitcast_fusion
  7.6 0.1 pad_maximum_fusion.2
  7.7 0.6 pad_maximum_fusion.refs_6_
  8.3 0.0 copy-start
  8.3 0.0 copy-start.3
  8.3 6.5 %fusion.3 = f32[1,6144]{1,0:T(1,128)S(1)} fusion(bf16[1024,6144]{1,0:T(8,128)(2,1)} %refs_20_.1, bf16[1,1024]{1,0:T(2,128)(2,1)} %param.13), kind=kOutput, calls=%fused_computation.25 | convolution fusion | flops 12589056 | bytes 12609536 | tf_op jit(solution)/shard_map/dot_general | solution.py:1374
  14.8 0.0 copy-done.8
  14.8 0.6 reshape.280.refs_5_
  15.4 0.8 broadcast_in_dim.83.refs_8_
  16.2 1.3 broadcast_in_dim.82.bias_ref
  17.5 1.3 broadcast_in_dim.85.refs_12_
  18.8 0.0 copy-done
  18.8 0.0 copy-done.3
  18.8 0.0 copy-start.1
  18.8 1.6 copy-done.1
  20.4 0.0 copy-start.2
  20.4 1.6 copy-done.2
  22.0 23.8 %front_part.1 = (bf16[256,1024]{1,0:T(8,128)(2,1)S(1)}, bf16[8,256,128]{2,1,0:T(8,128)(2,1)S(1)}, bf16[8,256,128]{2,1,0:T(8,128)(2,1)S(1)}, bf16[8,256,128]{2,1,0:T(8,128)(2,1)S(1)}) custom-call(bf16[256,1024]{1,0:T(8,128)(2,1)S(1)} %copy-done.3, f32[2,1024]{1,0:T(2,128)S(1)} %slice.31.refs_1_, f32[2,128]{1,0:T(2,128)S(1)} %bitcast.32, ...), custom_call_target="tpu_custom_call" | custom-call | tf_op jit(solution)/shard_map/front_part/pallas_call | solution.py:1305
  45.8 0.0 copy-start.4
  45.8 0.8 copy-done.4
  46.6 0.0 copy-start.5
  46.6 0.8 copy-done.5
  47.4 0.0 copy-start.6
  47.4 0.8 copy-done.6
  48.2 0.0 copy-start.7
  48.2 0.8 copy-done.7
  49.0 12.6 %attend_forward.1 = (bf16[2048,128]{1,0:T(8,128)(2,1)}, f32[8,2,256]{2,1,0:T(2,128)}) custom-call(s32[8]{0:T(128)} %copy-done.8, bf16[2048,128]{1,0:T(8,128)(2,1)} %bitcast.29, bf16[2048,128]{1,0:T(8,128)(2,1)} %bitcast.30, bf16[2048,128]{1,0:T(8,128)(2,1)} %bitcast.31, f32[2048,128]{1,0:T(8,128)} %broadcast_in_dim.82.bias_ref), custom_call_target="tpu_custom_call" | custom-call | tf_op jit(solution)/shard_map/attend_forward/pallas_call | solution.py:113
  61.5 155.9 %back_part.1 = (bf16[256,1024]{1,0:T(8,128)(2,1)}, f32[256,1024]{1,0:T(8,128)}, f32[8,128]{1,0:T(8,128)}, f32[32,1024]{1,0:T(8,128)}, f32[32,1024]{1,0:T(8,128)}...) custom-call(s32[115]{0:T(128)} %concatenate.37.refs_0_, ...), custom_call_target="tpu_custom_call" | custom-call | tf_op jit(solution)/shard_map/back_part/pallas_call | solution.py:1123
  217.4 3.8 %finish.1 = (f32[256,1024]{1,0:T(8,128)}, f32[32,6144]{1,0:T(8,128)}, bf16[256,1024]{1,0:T(8,128)(2,1)}, f32[32,4096]{1,0:T(8,128)}, f32[128,1024]{1,0:T(8,128)}...) custom-call(f32[256,1024]{1,0:T(8,128)} %get-tuple-element.45.refs_0, ...), custom_call_target="tpu_custom_call" | custom-call | tf_op jit(solution)/shard_map/finish/pallas_call | solution.py:1209
  (12 shorter events, 0.1 us)
Async XLA Ops:
  1.6 13.2 %copy-start.8 = (s32[8]{0:T(128)}, s32[8]{0:T(128)S(1)}, u32[]{:S(2)}) copy-start(s32[8]{0:T(128)S(1)} %select_reduce_fusion.2.first_ref) | copy-start | bytes 100
  8.3 10.5 %copy-start = (bf16[1024,1024]{1,0:T(8,128)(2,1)S(1)}, bf16[1024,1024]{1,0:T(8,128)(2,1)}, u32[]{:S(2)}) copy-start(bf16[1024,1024]{1,0:T(8,128)(2,1)} %refs_17_.1) | copy-start | bytes 6291460
  8.3 10.5 %copy-start.3 = (bf16[256,1024]{1,0:T(8,128)(2,1)S(1)}, bf16[256,1024]{1,0:T(8,128)(2,1)}, u32[]{:S(2)}) copy-start(bf16[256,1024]{1,0:T(8,128)(2,1)} %refs_3_.3) | copy-start | bytes 1572868
  18.8 1.6 copy-start.1
  20.4 1.6 copy-start.2
  45.8 0.8 copy-start.4
  46.6 0.8 copy-start.5
  47.4 0.8 copy-start.6
  48.2 0.8 copy-start.7

commit v5 on v4

--- a/solution.py
+++ b/solution.py
@@ -2,6 +2,7 @@
 
 import jax
 import jax.numpy as jnp
+import numpy as np
 from jax import lax
 from jax.experimental import pallas as pl
 from jax.experimental.pallas import tpu as pltpu
@@ -14,10 +15,6 @@
 
 EPSILON = 1e-06
 MASKED = -1e30
-
-
-def frequencies(half_dim):
-    return jnp.exp(jnp.arange(half_dim, dtype=jnp.float32) * (-math.log(10000.0) / half_dim))
 
 
 def dot_nt(left, right):
@@ -162,7 +159,7 @@
     return value * half, slope
 
 
-def turn_pairs(values, _):
+def turn_pairs(values):
     lane = lax.rem(lax.broadcasted_iota(jnp.int32, values.shape, 1), HEAD_DIM)
     up = pltpu.roll(values, 128 - HEAD_DIM // 2, 1)
     down = pltpu.roll(values, HEAD_DIM // 2, 1)
@@ -179,7 +176,6 @@
         mod_ref,
         rope_ref,
         cond_ref,
-        valid_ref,
         q_hbm,
         k_hbm,
         v_hbm,
@@ -203,7 +199,7 @@
         gdown_ref,
         gmod_hbm,
         gcond_ref,
-        n1_all,
+        valid_ref,
         att_fr,
         do_own,
         from_core,
@@ -237,8 +233,6 @@
         row_recv,
         row_dp_send,
         row_dp_recv,
-        gather_send,
-        gather_recv,
         z_send_sem,
         z_recv_sem,
         mod_sem,
@@ -460,12 +454,15 @@
         return pl.ds(pl.multiple_of(chunk * BLOCK, BLOCK), BLOCK)
 
     def masked_square(values, rows):
-        sums = jnp.sum(values * values, axis=1, keepdims=True) * valid_ref[rows, :1]
+        counted = jnp.where(valid_ref[rows, :1] < -1.0, 0.0, 1.0)
+        sums = jnp.sum(values * values, axis=1, keepdims=True) * counted
         return jnp.sum(sums, axis=0, keepdims=True)
 
     one = jnp.zeros((1, 1), jnp.float32)
     row_zero = jnp.zeros((1, width), jnp.float32)
 
+    valid_load = pltpu.make_async_copy(bias_hbm.at[head], valid_ref, load_sem.at[15])
+    valid_load.start()
     for flips in others:
         att_copy(flips).start()
     att_fr[:, own_lanes] = att_own[own_rows, :]
@@ -494,29 +491,6 @@
                 take_dp(unit)
 
     half = tokens // 2
-    low, high = pl.ds(0, half), pl.ds(half, half)
-
-    def gather_copy(index):
-        if index == 0:
-            source, target, peer = n1_hbm.at[low], n1_all.at[head, low], x_peer
-        elif index == 1:
-            source, target, peer = n1_hbm.at[high], n1_all.at[head, high], y_peer
-        elif index == 2:
-            source, target, peer = n1_hbm.at[low], n1_all.at[head, low], y_peer
-        elif index == 3:
-            source, target, peer = n1_all.at[x_peer, low], n1_all.at[x_peer, low], y_peer
-        elif index == 4:
-            source, target, peer = n1_hbm.at[high], n1_all.at[head, high], x_peer
-        elif index == 5:
-            source, target, peer = n1_all.at[y_peer, high], n1_all.at[y_peer, high], x_peer
-        elif index == 6:
-            source, target, peer = n1_hbm, n1_all.at[head], core_peer
-        else:
-            block = peer_head(head, 2 * (index - 6))
-            source, target, peer = n1_all.at[block], n1_all.at[block], core_peer
-        return remote(
-            source, target, gather_send.at[index], gather_recv.at[index], (group, peer)
-        )
 
     def mlp_part(up, down, act, dn2, wo, ba, n2):
         wo_load = pltpu.make_async_copy(wo_hbm, wo, load_sem.at[0])
@@ -541,11 +515,10 @@
             up_loads[tile].start()
             down_loads[tile].start()
 
+        valid_load.wait()
         wo_load.wait()
         for flips in others:
             att_copy(flips).wait()
-        for index in (0, 1, 6):
-            gather_copy(index).start()
         turned_rows(first_up + 1, att_fr)
 
         def project(chunk, _):
@@ -584,13 +557,6 @@
                     down.at[pl.ds(0, width), :],
                     load_sem.at[1 + tiles + tile],
                 ).wait()
-
-            @pl.when(index == GATHER_AT)
-            def _():
-                for step in (0, 1):
-                    gather_copy(step).wait()
-                for step in (2, 3, 4, 5):
-                    gather_copy(step).start()
 
             lanes = lane_block(index)
             active, slope = gelu_and_slope(dot_nn(n2[...], up[:, lanes]))
@@ -756,11 +722,9 @@
                 for copy in self.copies:
                     copy.wait()
 
+        group_load = pltpu.make_async_copy(n1_hbm, n1_group, load_sem.at[0])
+        group_load.start()
         run_plan("scope")
-        for step in (2, 3, 4, 5):
-            gather_copy(step).wait()
-        for step in (7, 8, 9):
-            gather_copy(step).start()
         for flips in others:
             grad_copy(flips).wait()
         for copy in loads:
@@ -833,7 +797,7 @@
 
             def turned_back(value):
                 value = value.astype(jnp.bfloat16).astype(jnp.float32)
-                return (value * cosine + turn_pairs(value, None) * sine).astype(jnp.bfloat16)
+                return (value * cosine - turn_pairs(value) * sine).astype(jnp.bfloat16)
 
             start = 2 * SLOTS + 4 * frames
             parts = (
@@ -862,23 +826,8 @@
                 ),
             )
 
-        for step in (6, 7, 8, 9):
-            gather_copy(step).wait()
-        group_loads = [
-            pltpu.make_async_copy(n1_hbm, n1_group.at[head], load_sem.at[0])
-        ] + [
-            pltpu.make_async_copy(
-                n1_all.at[peer_head(head, flips)],
-                n1_group.at[peer_head(head, flips)],
-                load_sem.at[flips],
-            )
-            for flips in others
-        ]
-        for copy in group_loads:
-            copy.start()
         normed_plan("combined")
-        for copy in group_loads:
-            copy.wait()
+        group_load.wait()
 
         piece = width // n_dp
 
@@ -985,9 +934,11 @@
         shift_one_grad, scale_one_grad = lax.fori_loop(
             0, steps, first_norm_back, (row_zero, row_zero)
         )
+        cond = cond_ref[...].astype(jnp.float32)
+        gate = 1.0 / (1.0 + jnp.exp(-cond))
         vectors = jnp.concatenate(
             [
-                cond_ref[0:1, :],
+                cond * gate,
                 shift_one_grad,
                 scale_one_grad,
                 *saved_rows,
@@ -1015,8 +966,6 @@
         cond_block(0, shift_one_grad, False)
         mod_load(1).wait()
         cond_block(1, scale_one_grad, False)
-        cond = cond_ref[1:2, :]
-        gate = 1.0 / (1.0 + jnp.exp(-cond))
         gcond_ref[...] = jnp.sum(cond_sum[...].T, axis=0, keepdims=True) * (
             gate * (1.0 + cond * (1.0 - gate))
         )
@@ -1102,7 +1051,6 @@
     "row_x": [("F", 6), ("F", 7), ("S", 8)],
     "end": [("S", 6), ("S", 7), ("D", 8), ("D", 6), ("D", 7)],
 }
-GATHER_AT = 8
 
 
 def back_part(n_dp, vmem_operands, hbm_operands):
@@ -1131,13 +1079,13 @@
             shape((large, width), f32),
             shape((small, 6 * width), f32),
             shape((1, width), f32),
-            shape((frames, tokens, width), bf16),
         ),
         in_specs=[IN_SMEM]
         + [IN_VMEM] * (len(vmem_operands) - 1)
         + [IN_PLACE] * len(hbm_operands),
-        out_specs=(IN_PLACE, *[IN_VMEM] * 8, IN_PLACE, IN_VMEM, IN_PLACE),
+        out_specs=(IN_PLACE, *[IN_VMEM] * 8, IN_PLACE, IN_VMEM),
         scratch_shapes=[
+            pltpu.VMEM((tokens, 128), f32),
             pltpu.VMEM((tokens, width), bf16),
             pltpu.VMEM((frames, tokens, 128), bf16),
             pltpu.VMEM((units, n_dp, 2, 2, small, width), bf16),
@@ -1166,8 +1114,6 @@
             dma((3,)),
             dma((n_dp - 1,)),
             dma((n_dp - 1,)),
-            dma((10,)),
-            dma((10,)),
             dma((n_dp - 1,)),
             dma((n_dp - 1,)),
             dma((6, frames // 2)),
@@ -1220,122 +1166,317 @@
     )(*arrays)
 
 
+def tables_kernel(lengths, valid_ref, wave_ref, table, first_ref, rope_ref, bias_ref):
+    frames = rope_ref.shape[0]
+    ends = [lengths[0, 0]]
+    for clip in range(1, lengths.shape[1] - 1):
+        ends.append(ends[-1] + lengths[0, clip])
+    columns = 2 * SLOTS + 4 * frames
+    for slot in range(SLOTS):
+        table[slot] = 0
+        table[SLOTS + slot] = 0
+    for frame in range(frames):
+        for way in range(1, 4):
+            table[columns + 4 * frame + way] = SLOTS
+    used = jnp.int32(0)
+    for frame in range(frames):
+        first = jnp.int32(0)
+        for end in ends:
+            first = jnp.where(end <= frame, end, first)
+        first_ref[frame] = first
+        cosine, sine = wave_ref[0, 0:1, :], wave_ref[0, 1:2, :]
+        for place in range(1, wave_ref.shape[0]):
+            here = frame - first == place
+            cosine = jnp.where(here, wave_ref[place, 0:1, :], cosine)
+            sine = jnp.where(here, wave_ref[place, 1:2, :], sine)
+        rope_ref[frame, 0:1, :] = cosine
+        rope_ref[frame, 1:2, :] = sine
+        for back in range(4):
+            if back > frame:
+                table[2 * SLOTS + 4 * frame + back] = SLOTS
+                continue
+            held = frame - back >= first
+            slot = jnp.where(held, used, SLOTS)
+            table[2 * SLOTS + 4 * frame + back] = slot
+            table[columns + 4 * (frame - back) + back] = slot
+
+            @pl.when(held)
+            def _(slot=slot, frame=frame, back=back):
+                table[slot] = frame
+                table[SLOTS + slot] = frame - back
+
+            used = used + jnp.where(held, 1, 0)
+    for slot in range(SLOTS):
+        table[columns + 4 * frames + slot] = jnp.where(table[slot] == table[SLOTS + slot], 1, 0)
+    for row in range(valid_ref.shape[0]):
+        keep = jnp.broadcast_to(valid_ref[row : row + 1, :], (128, 128)).astype(jnp.float32)
+        bias_ref[row * 128 : (row + 1) * 128, :] = jnp.where(keep.T > 0.5, 0.0, MASKED)
+
+
+def tables_part(lengths, valid):
+    group_tokens = valid.shape[0]
+    frames = group_tokens // PATCHES
+    powers = 10000.0 ** (-np.arange(HEAD_DIM // 2, dtype=np.float64) / (HEAD_DIM // 2))
+    angles = np.arange(4, dtype=np.float32)[:, None] * powers.astype(np.float32)[None]
+    cosine, sine = np.cos(angles), np.sin(angles)
+    wave = np.stack(
+        [np.concatenate([cosine] * 4, axis=1), np.concatenate([-sine, sine] * 2, axis=1)], axis=1
+    ).astype(np.float32)
+    return pl.pallas_call(
+        tables_kernel,
+        out_shape=(
+            jax.ShapeDtypeStruct((3 * SLOTS + 8 * frames,), jnp.int32),
+            jax.ShapeDtypeStruct((frames,), jnp.int32),
+            jax.ShapeDtypeStruct((frames, 2, 128), jnp.float32),
+            jax.ShapeDtypeStruct((group_tokens, 128), jnp.float32),
+        ),
+        in_specs=[IN_SMEM, IN_VMEM, IN_VMEM],
+        out_specs=(IN_SMEM, IN_SMEM, IN_VMEM, IN_VMEM),
+        name="tables",
+    )(lengths, valid.reshape(group_tokens // 128, 128), jnp.asarray(wave))
+
+
 def front_kernel(*refs):
     (
-        x_ref,
-        mod_ref,
+        x_hbm,
+        cond_ref,
         rope_ref,
         wq_hbm,
         wk_hbm,
         wv_hbm,
-        n1_ref,
-        q_ref,
-        k_ref,
-        v_ref,
-        weights,
-        sent,
+        wmod_hbm,
+        n1_hbm,
+        q_hbm,
+        k_hbm,
+        v_hbm,
+        mod_ref,
+        x_all,
+        n1_all,
+        q_all,
+        k_all,
+        v_all,
+        w_own,
+        wmod,
+        cond_own,
+        cond_all,
+        steer,
         load_sem,
-        send_sem,
-        recv_sem,
+        mod_sem,
+        out_sem,
+        cond_send,
+        cond_recv,
+        gather_send,
+        gather_recv,
     ) = refs
-    tokens, width = x_ref.shape
+    tokens, width = x_hbm.shape
+    frames = x_all.shape[0]
+    half = tokens // 2
     group = lax.axis_index("dp")
     head = lax.axis_index("head")
     core = lax.rem(head, 2)
+    xbit = lax.rem(lax.div(head, 2), 2)
+    ybit = lax.div(head, 4)
+    core_peer, x_peer, y_peer = peer_head(head, 1), peer_head(head, 2), peer_head(head, 4)
+    diagonal = peer_head(head, 6)
+    others = range(1, 8)
     barrier = pltpu.get_barrier_semaphore()
-    for flips in range(1, 8):
+    for flips in others:
         pl.semaphore_signal(
             barrier, inc=1, device_id=(group, peer_head(head, flips)), device_id_type=MESH_ID
         )
-    loads = [
-        pltpu.make_async_copy(source, weights.at[place], load_sem.at[place])
+    own_lanes = pl.ds(head * 128, 128)
+    mod_loads = [
+        pltpu.make_async_copy(
+            wmod_hbm.at[:, pl.ds(block * width, width)], wmod.at[block], mod_sem.at[block]
+        )
+        for block in range(6)
+    ]
+    loads = [pltpu.make_async_copy(x_hbm, x_all.at[head], load_sem.at[0])] + [
+        pltpu.make_async_copy(
+            source.at[:, own_lanes], w_own.at[:, pl.ds(place * 128, 128)], load_sem.at[1 + place]
+        )
         for place, source in enumerate((wq_hbm, wk_hbm, wv_hbm))
     ]
-    for copy in loads:
+    for copy in mod_loads[:2] + loads + mod_loads[2:]:
         copy.start()
-    shift, scaling = mod_ref[0:1, :], mod_ref[1:2, :]
-
-    def norm(index, _):
-        rows = pl.ds(pl.multiple_of(index * 32, 32), 32)
-        value = x_ref[rows, :].astype(jnp.float32)
-        scale = lax.rsqrt(jnp.mean(value * value, axis=1, keepdims=True) + EPSILON)
-        n1_ref[rows, :] = (value * scale * (1.0 + scaling) + shift).astype(jnp.bfloat16)
-        return 0
-
-    lax.fori_loop(0, tokens // 32, norm, 0)
-    pl.semaphore_wait(barrier, 7)
-    cosine, sine = rope_ref[0:1, :], rope_ref[1:2, :]
-    outs = (q_ref, k_ref, v_ref)
-
-    def copy_to(place, flips):
+    value = cond_ref[...].astype(jnp.float32)
+    act = jnp.broadcast_to(value / (1.0 + jnp.exp(-value)), (8, width)).astype(jnp.bfloat16)
+    cond_own[...] = act
+    cond_all[head] = act
+
+    low, high = pl.ds(0, half), pl.ds(half, half)
+
+    def gather_copy(index):
+        if index == 0:
+            source, target, peer = x_hbm.at[low], x_all.at[head, low], x_peer
+        elif index == 1:
+            source, target, peer = x_hbm.at[high], x_all.at[head, high], y_peer
+        elif index == 2:
+            source, target, peer = x_hbm.at[low], x_all.at[head, low], y_peer
+        elif index == 3:
+            source, target, peer = x_hbm.at[high], x_all.at[head, high], x_peer
+        elif index == 4:
+            source, target, peer = x_all.at[x_peer, low], x_all.at[x_peer, low], y_peer
+        elif index == 5:
+            source, target, peer = x_all.at[y_peer, high], x_all.at[y_peer, high], x_peer
+        elif index == 6:
+            source, target, peer = x_hbm, x_all.at[head], core_peer
+        else:
+            block = (x_peer, y_peer, y_peer, x_peer, diagonal, diagonal)[index - 7]
+            rows = (low, high, low, high, low, high)[index - 7]
+            source, target, peer = x_all.at[block, rows], x_all.at[block, rows], core_peer
+        return remote(
+            source, target, gather_send.at[index], gather_recv.at[index], (group, peer)
+        )
+
+    def cond_copy(flips):
         peer = peer_head(head, flips)
         return remote(
-            sent.at[place, :, pl.ds(peer * 128, 128)],
-            outs[place].at[head],
-            send_sem.at[place, flips],
-            recv_sem.at[place, flips],
-            (group, peer),
-        )
-
-    for place in range(3):
-        loads[place].wait()
-        for chip_flips in (6, 2, 4, 0):
-            chip = lax.div(peer_head(head, chip_flips), 2)
-            lanes = pl.ds(pl.multiple_of(chip * BLOCK, BLOCK), BLOCK)
-            value = dot_nn(n1_ref[...], weights[place, :, lanes])
-            for side in range(2):
-                part = value[:, side * 128 : (side + 1) * 128]
-                if place < 2:
-                    part = part * cosine + turn_pairs(part, None) * sine
-                where = pl.ds(pl.multiple_of(chip * BLOCK + side * 128, 128), 128)
-                sent[place, :, where] = part.astype(jnp.bfloat16)
-            for flips in (chip_flips, chip_flips + 1):
-                if flips:
-                    copy_to(place, flips).start()
-        outs[place][head] = sent[place, :, pl.ds(pl.multiple_of(head * 128, 128), 128)]
-    for place in range(3):
-        for flips in range(1, 8):
-            copy_to(place, flips).wait()
-
-
-def front_part(hidden, modulation, rope, query_weight, key_weight, value_weight):
+            cond_own, cond_all.at[head], cond_send.at[flips], cond_recv.at[flips], (group, peer)
+        )
+
+    pl.semaphore_wait(barrier, 7)
+    for flips in others:
+        cond_copy(flips).start()
+    for index in (0, 1, 6, 2, 3):
+        gather_copy(index).start()
+
+    for flips in others:
+        cond_copy(flips).wait()
+    everyone = cond_all[...].reshape(frames * 8, width)
+
+    def modulate(block):
+        mod_loads[block].wait()
+
+        def body(chunk, _):
+            lanes = pl.ds(pl.multiple_of(chunk * BLOCK, BLOCK), BLOCK)
+            steer[block, :, lanes] = dot_nn(everyone, wmod[block, :, lanes])
+            return 0
+
+        lax.fori_loop(0, width // BLOCK, body, 0)
+        mod_ref[block : block + 1, :] = steer[block, pl.ds(pl.multiple_of(head * 8, 8), 8), :][0:1]
+
+    modulate(0)
+    modulate(1)
+    for copy in loads:
+        copy.wait()
+
+    def out_copy(frame, rows, item):
+        return pltpu.make_async_copy(
+            n1_all.at[frame, rows], n1_hbm.at[frame, rows], out_sem.at[item]
+        )
+
+    def project(frame, side, item):
+        steer_rows = pl.ds(pl.multiple_of(frame * 8, 8), 8)
+        shift, scaling = steer[0, steer_rows, :][0:1], steer[1, steer_rows, :][0:1]
+
+        def norm(index, _):
+            rows = pl.ds(pl.multiple_of(side * half + index * 32, 32), 32)
+            value = x_all[frame, rows, :].astype(jnp.float32)
+            scale = lax.rsqrt(jnp.mean(value * value, axis=1, keepdims=True) + EPSILON)
+            n1_all[frame, rows, :] = (value * scale * (1.0 + scaling) + shift).astype(
+                jnp.bfloat16
+            )
+            return 0
+
+        lax.fori_loop(0, half // 32, norm, 0)
+        rows = pl.ds(pl.multiple_of(side * half, half), half)
+        out_copy(frame, rows, item).start()
+        value = dot_nn(n1_all[frame, rows, :], w_own[...])
+        cosine, sine = rope_ref[frame, 0:1, :], rope_ref[frame, 1:2, :]
+        for place, target in enumerate((q_all, k_all, v_all)):
+            part = value[:, place * 128 : (place + 1) * 128]
+            if place < 2:
+                part = part * cosine + turn_pairs(part) * sine
+            target[frame, rows, :] = part.astype(jnp.bfloat16)
+
+    def stage(number, other_core):
+        at_core = 1 - core if other_core else core
+
+        def body(index, _):
+            if number == 0:
+                at_x, at_y, side = xbit, ybit, index
+            elif number == 3:
+                at_x, at_y, side = 1 - xbit, 1 - ybit, index
+            else:
+                at_x = xbit + (1 - index) * (1 - 2 * xbit)
+                at_y = ybit + index * (1 - 2 * ybit)
+                side = index if number == 1 else 1 - index
+            frame = 4 * at_y + 2 * at_x + at_core
+            project(frame, side, number * 4 + other_core * 2 + index)
+            return 0
+
+        lax.fori_loop(0, 2, body, 0)
+
+    stage(0, 0)
+    gather_copy(6).wait()
+    stage(0, 1)
+    for block in range(2, 6):
+        modulate(block)
+    for number, arrivals in ((1, (0, 1)), (2, (2, 3)), (3, (4, 5))):
+        for index in arrivals:
+            gather_copy(index).wait()
+            if number == 1:
+                gather_copy(index + 4).start()
+            gather_copy(index + 7).start()
+        stage(number, 0)
+        for index in arrivals:
+            gather_copy(index + 7).wait()
+        stage(number, 1)
+    outs = [
+        pltpu.make_async_copy(source, target, load_sem.at[place])
+        for place, (source, target) in enumerate(((q_all, q_hbm), (k_all, k_hbm), (v_all, v_hbm)))
+    ]
+    for copy in outs:
+        copy.start()
+    for item in range(16):
+        out_copy(0, low, item).wait()
+    for copy in outs:
+        copy.wait()
+
+
+def front_part(hidden, cond, rope, query_weight, key_weight, value_weight, modulation_weight):
     tokens, width = hidden.shape
+    frames = rope.shape[0]
     dma = pltpu.SemaphoreType.DMA
-    block = jax.ShapeDtypeStruct((8, tokens, 128), jnp.bfloat16)
+    bf16, f32 = jnp.bfloat16, jnp.float32
+    in_hbm = pl.BlockSpec(memory_space=pltpu.HBM)
+    block = jax.ShapeDtypeStruct((frames, tokens, 128), bf16)
     return pl.pallas_call(
         front_kernel,
-        out_shape=(jax.ShapeDtypeStruct((tokens, width), jnp.bfloat16), block, block, block),
-        in_specs=[IN_VMEM] * 3 + [IN_PLACE] * 3,
-        out_specs=(IN_VMEM,) * 4,
+        out_shape=(
+            jax.ShapeDtypeStruct((frames, tokens, width), bf16),
+            block,
+            block,
+            block,
+            jax.ShapeDtypeStruct((8, width), f32),
+        ),
+        in_specs=[in_hbm, IN_VMEM, IN_VMEM] + [in_hbm] * 4,
+        out_specs=(in_hbm,) * 4 + (IN_VMEM,),
         scratch_shapes=[
-            pltpu.VMEM((3, width, width), jnp.bfloat16),
-            pltpu.VMEM((3, tokens, width), jnp.bfloat16),
-            dma((3,)),
-            dma((3, 8)),
-            dma((3, 8)),
+            pltpu.VMEM((frames, tokens, width), bf16),
+            pltpu.VMEM((frames, tokens, width), bf16),
+            pltpu.VMEM((frames, tokens, 128), bf16),
+            pltpu.VMEM((frames, tokens, 128), bf16),
+            pltpu.VMEM((frames, tokens, 128), bf16),
+            pltpu.VMEM((width, 384), bf16),
+            pltpu.VMEM((6, width, width), bf16),
+            pltpu.VMEM((8, width), bf16),
+            pltpu.VMEM((frames, 8, width), bf16),
+            pltpu.VMEM((6, frames * 8, width), f32),
+            dma((4,)),
+            dma((6,)),
+            dma((16,)),
+            dma((8,)),
+            dma((8,)),
+            dma((13,)),
+            dma((13,)),
         ],
         compiler_params=pltpu.CompilerParams(
-            collective_id=1, has_side_effects=True, vmem_limit_bytes=32 * 1024 * 1024
+            collective_id=1, has_side_effects=True, vmem_limit_bytes=67043328
         ),
         name="front_part",
-    )(hidden, modulation, rope, query_weight, key_weight, value_weight)
-
-
-def slot_table(first, frames):
-    pair = jnp.arange(4 * frames, dtype=jnp.int32)
-    frame, back = pair // 4, pair % 4
-    held = (frame - back) >= jnp.repeat(first, 4)
-    rank = jnp.sum((held[None, :] & (pair[None, :] < pair[:, None])).astype(jnp.int32), axis=1)
-    slot = jnp.where(held, rank, SLOTS)
-    hit = slot[None, :] == jnp.arange(SLOTS, dtype=jnp.int32)[:, None]
-    query = jnp.sum(jnp.where(hit, frame[None, :], 0), axis=1)
-    key = jnp.sum(jnp.where(hit, (frame - back)[None, :], 0), axis=1)
-    grid = slot.reshape(frames, 4)
-    columns = [
-        jnp.concatenate([grid[way:, way], jnp.full((way,), SLOTS, jnp.int32)]) for way in range(4)
-    ]
-    same = (query == key).astype(jnp.int32)
-    return jnp.concatenate([query, key, slot, jnp.stack(columns, axis=1).reshape(-1), same])
+    )(hidden, cond, rope, query_weight, key_weight, value_weight, modulation_weight)
 
 
 def per_device(
@@ -1357,34 +1498,9 @@
     frames = group_tokens // PATCHES
     head_index = lax.axis_index("head")
     n_dp = lax.axis_size("dp")
-    frame = jnp.arange(frames, dtype=jnp.int32)
-    ends = jnp.cumsum(clip_lengths[0])
-    first_frames = jnp.max(
-        jnp.where(ends[None, :] <= frame[:, None], ends[None, :], 0), axis=1
-    ).astype(jnp.int32)
-    angles = (frame - first_frames).astype(jnp.float32)[:, None] * frequencies(HEAD_DIM // 2)[None]
-    cosine, sine = jnp.cos(angles), jnp.sin(angles)
-    cosines = jnp.concatenate([cosine] * 4, axis=1)
-    sines = jnp.concatenate([-sine, sine] * 2, axis=1)
-    rope = jnp.stack([cosines, sines], axis=1)
-    rope_back = jnp.stack([cosines, -sines], axis=1)
-    local_valid = lax.dynamic_slice_in_dim(patch_valid, head_index * tok_dev, tok_dev)
-    cond_value = frame_cond.astype(jnp.float32)
-    cond_act = jax.nn.silu(cond_value).astype(jnp.bfloat16)
-    modulation = jnp.dot(cond_act, modulation_weight, preferred_element_type=jnp.float32).reshape(
-        6, model_width
-    )
-    normed_one, head_query, head_key, head_value = front_part(
-        hidden_in,
-        modulation[:2],
-        lax.dynamic_index_in_dim(rope, head_index, 0, keepdims=False),
-        query_weight,
-        key_weight,
-        value_weight,
-    )
-    bias = jnp.broadcast_to(
-        jnp.where(patch_valid == 1, 0.0, MASKED).astype(jnp.float32)[:, None],
-        (group_tokens, 128),
+    table, first_frames, rope, bias = tables_part(clip_lengths, patch_valid)
+    normed_group, head_query, head_key, head_value, modulation = front_part(
+        hidden_in, frame_cond, rope, query_weight, key_weight, value_weight, modulation_weight
     )
     attended, logsum = attend_forward(
         first_frames,
@@ -1393,23 +1509,13 @@
     )
     results = back_part(
         n_dp,
-        (
-            slot_table(first_frames, frames),
-            attended,
-            logsum,
-            hidden_in,
-            cotangent,
-            modulation,
-            rope_back,
-            jnp.concatenate([cond_act.astype(jnp.float32), cond_value], axis=0),
-            jnp.broadcast_to(local_valid.astype(jnp.float32)[:, None], (tok_dev, 128)),
-        ),
+        (table, attended, logsum, hidden_in, cotangent, modulation, rope, frame_cond),
         (
             head_query,
             head_key,
             head_value,
             bias.reshape(frames, PATCHES, 128),
-            normed_one,
+            normed_group,
             output_weight,
             up_weight,
             down_weight,
@@ -1419,7 +1525,7 @@
             modulation_weight,
         ),
     )
-    (block_out, grad_input, statistics, gq, gk, gv, go, gup, gdown, gmod, gcond, _) = results
+    (block_out, grad_input, statistics, gq, gk, gv, go, gup, gdown, gmod, gcond) = results
     (grad_input, gmod, block_out, gup, gdown, gq, gk, gv, go, gcond, statistics) = finish(
         (grad_input, gmod, block_out, gup, gdown, gq, gk, gv, go, gcond, statistics)
     )

time: 222 us -> 204 us (0.919)
  local copies, waits for them, and re-layouts: 12.1 us -> 0 us
  Pallas kernels: 196 us -> 203 us
  matrix products: 6.47 us -> 0 us
  other arithmetic: 5.86 us -> 0 us
    pallas_call x1 -> x2, Pallas kernels: 23.8 us -> 32.6 us  [the longest x1 30.5 us: front_part(): pl.pallas_call(front_kernel, out_shape=(jax.ShapeDtypeStruct((frames, tok...]
    dot_general x1 -> x0, matrix products: 6.47 us -> none  [per_device(): jnp.dot(cond_act, modulation_weight, preferred_element_type=jnp.float32)]
    unnamed x18 -> x0, local copies, waits for them, and re-layouts: 6.36 us -> none
    broadcast_in_dim x5 -> x0, local copies, waits for them, and re-layouts: 3.44 us -> none  [the longest x3 2.62 us: per_device(): jnp.broadcast_to(jnp.where(patch_valid == 1, 0.0, MASKED).astype(jnp.floa...]
where the time goes in v5:
time: 204 us
  Pallas kernels  203 us (100%)
    pallas_call x1, Pallas kernels, back_part(): pl.pallas_call(lambda *refs: back_kernel(n_dp, *refs), out_shape=(shape((...  154 us
    pallas_call x1, Pallas kernels, front_part(): pl.pallas_call(front_kernel, out_shape=(jax.ShapeDtypeStruct((frames, tok...  30.5 us
    pallas_call x1, Pallas kernels, attend_forward(): pl.pallas_call(attend_forward_kernel, out_shape=(jax.ShapeDtypeStruct((to...  12.6 us

profile of v5, /device:TPU:0, one launch (start us, length us, event | category | flops | bytes accessed | tf_op | source)
XLA Modules:
  0.0 203.9 jit_solution(17733749967732717399)
XLA Ops:
  0.6 2.0 tables.1
  2.7 30.5 %front_part.1 = (bf16[8,256,1024]{2,1,0:T(8,128)(2,1)}, bf16[8,256,128]{2,1,0:T(8,128)(2,1)}, bf16[8,256,128]{2,1,0:T(8,128)(2,1)}, bf16[8,256,128]{2,1,0:T(8,128)(2,1)}, f32[8,1024]{1,0:T(8,128)}) custom-call(bf16[256,1024]{1,0:T(8,128)(2,1)} %refs_3_.3, bf16[1,1024]{1,0:T(2,128)(2,1)} %refs_7_.1, f32[8,2,128]{2,1,0:T(2,128)} %get-tuple-element.46.refs_2_.refs_6_, ...), custom_call_target="tpu_custom_call" | custom-call | tf_op jit(solution)/shard_map/front_part/pallas_call | solution.py:1445
  33.2 12.6 %attend_forward.1 = (bf16[2048,128]{1,0:T(8,128)(2,1)}, f32[8,2,256]{2,1,0:T(2,128)}) custom-call(s32[8]{0:T(128)} %get-tuple-element.45.first_ref, bf16[2048,128]{1,0:T(8,128)(2,1)} %bitcast.6, bf16[2048,128]{1,0:T(8,128)(2,1)} %bitcast.7, bf16[2048,128]{1,0:T(8,128)(2,1)} %bitcast.8, f32[2048,128]{1,0:T(8,128)} %get-tuple-element.50.bias_ref), custom_call_target="tpu_custom_call" | custom-call | tf_op jit(solution)/shard_map/attend_forward/pallas_call | solution.py:110
  45.8 154.1 %back_part.1 = (bf16[256,1024]{1,0:T(8,128)(2,1)}, f32[256,1024]{1,0:T(8,128)}, f32[8,128]{1,0:T(8,128)}, f32[32,1024]{1,0:T(8,128)}, f32[32,1024]{1,0:T(8,128)}...) custom-call(s32[115]{0:T(128)} %get-tuple-element.44.refs_0_, ...), custom_call_target="tpu_custom_call" | custom-call | tf_op jit(solution)/shard_map/back_part/pallas_call | solution.py:1071
  199.9 3.8 %finish.1 = (f32[256,1024]{1,0:T(8,128)}, f32[32,6144]{1,0:T(8,128)}, bf16[256,1024]{1,0:T(8,128)(2,1)}, f32[32,4096]{1,0:T(8,128)}, f32[128,1024]{1,0:T(8,128)}...) custom-call(f32[256,1024]{1,0:T(8,128)} %get-tuple-element.55.refs_0, ...), custom_call_target="tpu_custom_call" | custom-call | tf_op jit(solution)/shard_map/finish/pallas_call | solution.py:1155

commit v6 on v5

--- a/solution.py
+++ b/solution.py
@@ -65,31 +65,26 @@
         low = jnp.full((1, PATCHES), MASKED, jnp.float32)
         tops = lax.fori_loop(first, frame + 1, score, (low, low))
 
-        def exponent(key_frame, totals):
-            new = []
+        def weigh(key_frame, carry):
+            turned = v_ref[pl.ds(key_frame * PATCHES, PATCHES), :].T
+            totals, sums = [], []
             for head in range(2):
                 value = jnp.exp(scores[head, key_frame - first] - tops[head])
-                scores[head, key_frame - first] = value
-                new.append(totals[head] + jnp.sum(value, axis=0, keepdims=True))
-            return tuple(new)
+                totals.append(carry[head] + jnp.sum(value, axis=0, keepdims=True))
+                sums.append(
+                    carry[2 + head]
+                    + dot_nn(
+                        turned[head * HEAD_DIM : (head + 1) * HEAD_DIM, :],
+                        value.astype(jnp.bfloat16),
+                    )
+                )
+            return (*totals, *sums)
 
         zero = jnp.zeros((1, PATCHES), jnp.float32)
-        totals = lax.fori_loop(first, frame + 1, exponent, (zero, zero))
-        inverse = [1.0 / total for total in totals]
-
-        def weigh(key_frame, sums):
-            turned = v_ref[pl.ds(key_frame * PATCHES, PATCHES), :].T
-            new = []
-            for head in range(2):
-                probs = (scores[head, key_frame - first] * inverse[head]).astype(jnp.bfloat16)
-                new.append(
-                    sums[head]
-                    + dot_nn(turned[head * HEAD_DIM : (head + 1) * HEAD_DIM, :], probs)
-                )
-            return tuple(new)
-
         empty = jnp.zeros((HEAD_DIM, PATCHES), jnp.float32)
-        sums = lax.fori_loop(first, frame + 1, weigh, (empty, empty))
+        carry = lax.fori_loop(first, frame + 1, weigh, (zero, zero, empty, empty))
+        totals = carry[:2]
+        sums = [carry[2 + head] * (1.0 / totals[head]) for head in range(2)]
         o_ref[rows, :] = jnp.concatenate(sums, axis=0).T.astype(jnp.bfloat16)
         for head in range(2):
             lse_ref[frame, head : head + 1, :] = tops[head] + jnp.log(totals[head])

time: 204 us -> 204 us (level)
  no operation moved by 1% of the time
where the time goes in v6:
time: 204 us; the launch traced here: 203 us
  Pallas kernels  203 us (100%)
    pallas_call x1, Pallas kernels, back_part(): pl.pallas_call(lambda *refs: back_kernel(n_dp, *refs), out_shape=(shape((...  155 us
    pallas_call x1, Pallas kernels, front_part(): pl.pallas_call(front_kernel, out_shape=(jax.ShapeDtypeStruct((frames, tok...  30.5 us
    pallas_call x1, Pallas kernels, attend_forward(): pl.pallas_call(attend_forward_kernel, out_shape=(jax.ShapeDtypeStruct((to...  11.6 us

profile of v6, /device:TPU:0, one launch (start us, length us, event | category | flops | bytes accessed | tf_op | source)
XLA Modules:
  0.0 203.4 jit_solution(1307957596467502941)
XLA Ops:
  0.6 2.0 %tables.1 = (s32[115]{0:T(128)}, s32[8]{0:T(128)}, f32[8,2,128]{2,1,0:T(2,128)}, f32[2048,128]{1,0:T(8,128)}) custom-call(s32[1,3]{1,0:T(1,128)} %lengths.1, s32[16,128]{1,0:T(8,128)} %bitcast.9, f32[4,2,128]{2,1,0:T(2,128)} %constant.2.clone.wave_ref), custom_call_target="tpu_custom_call" | custom-call | tf_op jit(solution)/shard_map/tables/pallas_call | solution.py:1220
  2.7 30.5 %front_part.1 = (bf16[8,256,1024]{2,1,0:T(8,128)(2,1)}, bf16[8,256,128]{2,1,0:T(8,128)(2,1)}, bf16[8,256,128]{2,1,0:T(8,128)(2,1)}, bf16[8,256,128]{2,1,0:T(8,128)(2,1)}, f32[8,1024]{1,0:T(8,128)}) custom-call(bf16[256,1024]{1,0:T(8,128)(2,1)} %refs_3_.3, bf16[1,1024]{1,0:T(2,128)(2,1)} %refs_7_.1, f32[8,2,128]{2,1,0:T(2,128)} %get-tuple-element.46.refs_2_.refs_6_, ...), custom_call_target="tpu_custom_call" | custom-call | tf_op jit(solution)/shard_map/front_part/pallas_call | solution.py:1440
  33.2 11.6 %attend_forward.1 = (bf16[2048,128]{1,0:T(8,128)(2,1)}, f32[8,2,256]{2,1,0:T(2,128)}) custom-call(s32[8]{0:T(128)} %get-tuple-element.45.first_ref, bf16[2048,128]{1,0:T(8,128)(2,1)} %bitcast.6, bf16[2048,128]{1,0:T(8,128)(2,1)} %bitcast.7, bf16[2048,128]{1,0:T(8,128)(2,1)} %bitcast.8, f32[2048,128]{1,0:T(8,128)} %get-tuple-element.50.bias_ref), custom_call_target="tpu_custom_call" | custom-call | tf_op jit(solution)/shard_map/attend_forward/pallas_call | solution.py:105
  44.8 154.6 %back_part.1 = (bf16[256,1024]{1,0:T(8,128)(2,1)}, f32[256,1024]{1,0:T(8,128)}, f32[8,128]{1,0:T(8,128)}, f32[32,1024]{1,0:T(8,128)}, f32[32,1024]{1,0:T(8,128)}...) custom-call(s32[115]{0:T(128)} %get-tuple-element.44.refs_0_, ...), custom_call_target="tpu_custom_call" | custom-call | tf_op jit(solution)/shard_map/back_part/pallas_call | solution.py:1066
  199.4 3.8 %finish.1 = (f32[256,1024]{1,0:T(8,128)}, f32[32,6144]{1,0:T(8,128)}, bf16[256,1024]{1,0:T(8,128)(2,1)}, f32[32,4096]{1,0:T(8,128)}, f32[128,1024]{1,0:T(8,128)}...) custom-call(f32[256,1024]{1,0:T(8,128)} %get-tuple-element.55.refs_0, ...), custom_call_target="tpu_custom_call" | custom-call | tf_op jit(solution)/shard_map/finish/pallas_call | solution.py:1150
